TPU v7x, 128 devices: a whole 4x4x4 slice. The times are simulated.
128 devices in a mesh: tm: 4 (over x), space: 32 (over y, z, core).
Axes of the slice: x: 4, y: 4, z: 4, core: 2. Of those that a mesh axis runs over, the one named last changes fastest.
Arguments:
- pixel_cot: bfloat16 [16, 256, 64, 128], P('tm', 'space'), may hold values from -6 to 6
- frame_group: int32 [16], P('tm'), may hold values from 0 to 3
- advantage: float32 [4], replicated, may hold values from -4 to 4
- block_in: bfloat16 [2, 16, 256, 64, 128], P(None, 'tm', 'space'), may hold values from -6 to 6
- conv1_weight: bfloat16 [2, 3, 3, 3, 128, 128], replicated, may hold values from -0.109375 to 0.109375
- conv2_weight: bfloat16 [2, 3, 3, 3, 128, 128], replicated, may hold values from -0.109375 to 0.109375
- owner_map: int32 [4, 32, 64, 1], P('tm', 'space'), may hold values from 0 to 31; in each aligned block of 64 rows (0 to 63, 64 to 127, ..., all dimensions but the last counted through in order) at most 4 rows name the same one
Outputs:
- latent_grad: bfloat16 [4, 32, 32, 4, 1024], P('tm', 'space')
Inputs may be any that keep to these rules, and one draw needn't show every extreme that they name: `owner_map`: among the units of one device, at most 4 have the same owner, and in some devices exactly 4 do.
All inputs are finite; a program needn't handle non-finite values.
Results may differ from a plain program's by a relative error of at most 0.013.
Values may be sent and summed in bfloat16 or wider, within the bound.
No kernel may reach another device: no remote copies, remote signals or barrier semaphores. Data moves between devices by JAX's collectives and lax.ppermute only.
A program may use at most 128 MiB of HBM per device.

v0:
```python
import jax
import jax.numpy as jnp
from jax import lax
from jax.experimental import pallas as pl
from jax.experimental.pallas import tpu as pltpu
from jax.sharding import PartitionSpec as P

COLS = 64
C = 128
BF = jnp.bfloat16
F32 = jnp.float32


def side():
    return lax.rem(lax.axis_index("space"), 2)


def shift_add(partial):
    m = partial.shape[0]
    col = lax.broadcasted_iota(jnp.int32, (m, C), 0) % COLS
    low = jnp.where(col == 0, 0.0, pltpu.roll(partial[:, :C], 1, 0))
    high = jnp.where(col == COLS - 1, 0.0, pltpu.roll(partial[:, 2 * C :], m - 1, 0))
    return low + partial[:, C : 2 * C] + high


def patches(ext, t, r0, nr):
    return jnp.concatenate(
        [
            ext[t + dt, r0 + dr : r0 + dr + nr].reshape(nr * COLS, C)
            for dt in range(3)
            for dr in range(3)
        ],
        axis=1,
    )


def conv_back(ext, w, t, r0, nr):
    rhs = jnp.concatenate(
        [
            jnp.concatenate([w[2 - dt, 2 - dr, 2 - j] for j in range(3)], axis=0)
            for dt in range(3)
            for dr in range(3)
        ],
        axis=1,
    )
    out = lax.dot_general(
        patches(ext, t, r0, nr), rhs, (((1,), (1,)), ((), ())), preferred_element_type=F32
    )
    return shift_add(out).reshape(nr, COLS, C)


def conv_fore(ext, w, t, r0, nr):
    rhs = jnp.concatenate(
        [
            jnp.concatenate([w[dt, dr, j] for j in range(3)], axis=1)
            for dt in range(3)
            for dr in range(3)
        ],
        axis=0,
    )
    out = jnp.dot(patches(ext, t, r0, nr), rhs, preferred_element_type=F32)
    return shift_add(out).reshape(nr, COLS, C)


def factor(pre):
    s = jax.nn.sigmoid(pre)
    return s * (1.0 + pre * (1.0 - s))


def put_edges(ext, frames, inner, outer):
    p = side()
    ext[frames, pl.ds(10 * (1 - p), 2)] = inner
    ext[frames, pl.ds(10 * p, 2)] = outer


def store_ten(out, t, value):
    value = value.astype(BF)
    s = lax.axis_index("space")
    zero = jnp.zeros((1, COLS, C), BF)
    out[t, 1:9] = value[1:9]
    out[t, 0:1] = jnp.where(s == 0, zero, value[0:1])
    out[t, 9:10] = jnp.where(s == lax.axis_size("space") - 1, zero, value[9:10])


def send_edges(first, late, rin, rout):
    p = side()
    rin[0:2] = first[:, pl.ds(1 + 6 * (1 - p), 2)]
    rout[0:2] = first[:, pl.ds(1 + 6 * p, 2)]
    rin[2:4] = late[:, pl.ds(6 * (1 - p), 2)]
    rout[2:4] = late[:, pl.ds(6 * p, 2)]


def start_kernel(cot, bi, group, adv, v0, rin, rout, v0s, b1s, b0s, dmi, dmo, dpi, dpo):
    p = side()
    for t in range(4):
        scale = adv[group[t]]
        v0[t] = (cot[t].astype(F32) * scale).astype(BF)
    inner, outer = pl.ds(6 * (1 - p), 2), pl.ds(6 * p, 2)
    rin[0], rout[0] = v0[:, inner], v0[:, outer]
    for k in range(2):
        rin[1 + k], rout[1 + k] = bi[1 - k, :, inner], bi[1 - k, :, outer]
        dpi[k], dpo[k] = bi[1 - k, 2:4, inner], bi[1 - k, 2:4, outer]
    v0s[...] = v0[0:2]
    b1s[...] = bi[1, 2:4]
    b0s[...] = bi[0, 2:4]
    for t in range(2):
        dmi[t] = v0[t, 7 * (1 - p)]
        dmo[t] = v0[t, 7 * p]


def early_kernel(v0, bi, rin, rout, w2, w1, w1n, ga, d1, d0, ext, ext1, ext0):
    ext[:, 2:10] = v0[...]
    put_edges(ext, slice(0, 4), rin[0], rout[0])
    for k, old in enumerate((ext1, ext0)):
        old[:, 2:10] = bi[1 - k]
        put_edges(old, slice(0, 4), rin[1 + k], rout[1 + k])
    for t in range(2):
        ga[t] = conv_back(ext, w2, t, 0, 10)
    for old, w, d in ((ext1, w1, d1), (ext0, w1n, d0)):
        for t in range(2):
            d[t] = factor(conv_fore(old, w, t, 1, 8))


def fore_halo(ext, k, bi, rin, rout, bx, dpi, dpo):
    ext[0:2, 2:10] = bx[...]
    put_edges(ext, slice(0, 2), dpi[k], dpo[k])
    ext[2:4, 2:10] = bi[1 - k, 0:2]
    put_edges(ext, slice(2, 4), rin[1 + k, 0:2], rout[1 + k, 0:2])


def pre01_kernel(bi, rin, rout, bx, dpi, dpo, ga, w1, v1x, ext):
    fore_halo(ext, 0, bi, rin, rout, bx, dpi, dpo)
    for t in range(2):
        store_ten(v1x, t, ga[t] * factor(conv_fore(ext, w1, t, 0, 10)))


def factor01_kernel(bi, rin, rout, bx, dpi, dpo, w1, d, ext):
    fore_halo(ext, 1, bi, rin, rout, bx, dpi, dpo)
    for t in range(2):
        d[t] = factor(conv_fore(ext, w1, t, 0, 10))


def pre23_kernel(v0, rin, rout, vx, dmi, dmo, d, v1x, w2, v1, ein, eout, ext):
    p = side()
    ext[0:2, 2:10] = v0[2:4]
    put_edges(ext, slice(0, 2), rin[0, 2:4], rout[0, 2:4])
    ext[2:4, 2:10] = vx[...]
    for t in range(2):
        ext[2 + t, 10 - 9 * p] = dmi[t]
        ext[2 + t, 1 + 9 * p] = dmo[t]
    for t in range(2):
        v1[t] = (conv_back(ext, w2, t, 1, 8) * d[t]).astype(BF)
    send_edges(v1x, v1, ein, eout)


def local01(ext, vx, v, rin, rout):
    ext[0:2, 1:11] = vx[...]
    ext[2:4, 2:10] = v[...]
    put_edges(ext, slice(0, 4), rin[...], rout[...])


def local23(ext, v, rin, rout, vxr):
    ext[0:2, 2:10] = v[...]
    put_edges(ext, slice(0, 2), rin[2:4], rout[2:4])
    ext[2:4, 1:11] = vxr[...]


def up01_kernel(v1x, v1, rin, rout, v0, r0in, r0out, w1, v2x, ext, old):
    p = side()
    local01(ext, v1x, v1, rin, rout)
    old[:, 2:10] = v0[0:2]
    put_edges(old, slice(0, 2), r0in[0, 0:2], r0out[0, 0:2])
    for t in range(2):
        store_ten(v2x, t, old[t, 1:11].astype(F32) + conv_back(ext, w1, t, 0, 10))


def up23_kernel(v1, rin, rout, vxr, v0, v2x, w1, v2, ein, eout, ext):
    local23(ext, v1, rin, rout, vxr)
    for t in range(2):
        v2[t] = (v0[2 + t].astype(F32) + conv_back(ext, w1, t, 1, 8)).astype(BF)
    send_edges(v2x, v2, ein, eout)


def grad01_kernel(v2x, v2, rin, rout, d, w2, v3x, ext):
    local01(ext, v2x, v2, rin, rout)
    for t in range(2):
        store_ten(v3x, t, conv_back(ext, w2, t, 0, 10) * d[t])


def grad23_kernel(v2, rin, rout, vxr, d, v3x, w2, v3, ein, eout, ext):
    local23(ext, v2, rin, rout, vxr)
    for t in range(2):
        v3[t] = (conv_back(ext, w2, t, 1, 8) * d[t]).astype(BF)
    send_edges(v3x, v3, ein, eout)


def row_pairs(up):
    up = up.astype(BF).astype(F32).reshape(4, 2, COLS, C)
    return up[:, 0] + up[:, 1]


def last01_kernel(v3x, v3, rin, rout, v2x, w1, pool, ext):
    local01(ext, v3x, v3, rin, rout)
    for t in range(2):
        pool[t] = row_pairs(v2x[t, 1:9].astype(F32) + conv_back(ext, w1, t, 1, 8))


def last23_kernel(v3, rin, rout, vxr, v2, pool, owner, w1, out, ext, rows):
    local23(ext, v3, rin, rout, vxr)
    half = 2 * 4 * COLS
    rows[0:half] = pool[...].reshape(half, C)
    for t in range(2):
        pair = row_pairs(v2[t].astype(F32) + conv_back(ext, w1, t, 1, 8))
        rows[half + t * 4 * COLS : half + (t + 1) * 4 * COLS] = pair.reshape(4 * COLS, C)
    units = owner.shape[0]
    slots = out.shape[0]
    capacity = slots // lax.axis_size("space")
    u = lax.broadcasted_iota(jnp.int32, (units, units), 0)
    v = lax.broadcasted_iota(jnp.int32, (units, units), 1)
    mine = jnp.broadcast_to(owner[...], (units, units))
    named = jnp.sum(jnp.where(u == v, mine, 0), axis=0, keepdims=True)
    same = jnp.where((mine == named) & (u < v), 1, 0)
    slot = named * capacity + jnp.sum(same, axis=0, keepdims=True)
    place = jnp.where(
        lax.broadcasted_iota(jnp.int32, (slots, units), 0) == slot, 1.0, 0.0
    ).astype(BF)
    for j in range(8):
        even = rows[pl.ds(2 * j, units, stride=16), :]
        odd = rows[pl.ds(2 * j + 1, units, stride=16), :]
        unit = (even + odd).astype(BF)
        out[:, j * C : (j + 1) * C] = jnp.dot(
            place, unit, preferred_element_type=F32
        ).astype(BF)


VM = pl.BlockSpec(memory_space=pltpu.VMEM)
SM = pl.BlockSpec(memory_space=pltpu.SMEM)


def field(*lead, dtype=BF):
    return jax.ShapeDtypeStruct((*lead, COLS, C), dtype)


def run(kernel, outs, args, units, scratch=None, in_specs=None):
    if scratch is None:
        scratch = [pltpu.VMEM((4, 12, COLS, C), BF)]
    single = not isinstance(outs, list)
    moved = sum(a.size * a.dtype.itemsize for a in args)
    return pl.pallas_call(
        kernel,
        out_shape=outs,
        in_specs=in_specs or [VM] * len(args),
        out_specs=VM if single else [VM] * len(outs),
        scratch_shapes=scratch,
        compiler_params=pltpu.CompilerParams(vmem_limit_bytes=24 << 20),
        cost_estimate=pl.CostEstimate(
            flops=units * COLS * 27 * C * C * 3, bytes_accessed=moved, transcendentals=0
        ),
        name=kernel.__name__,
    )(*args)


def on_device(pixel_cot, frame_group, advantage, block_in, conv1_weight, conv2_weight, owner_map):
    times, strips = lax.axis_size("tm"), lax.axis_size("space")

    def outer_of(s):
        return s + 1 if s % 2 else s - 1

    inner_pairs = [(s, s ^ 1) for s in range(strips)]
    outer_pairs = [(s, outer_of(s)) for s in range(strips) if 0 <= outer_of(s) < strips]
    later = [(t + 1, t) for t in range(times - 1)]
    sooner = [(t, t + 1) for t in range(times - 1)]

    def corner(steps, pairs):
        return [(a * strips + s, b * strips + r) for a, b in steps for s, r in pairs]

    def swap_in(x):
        return lax.ppermute(x, "space", inner_pairs)

    def swap_out(x):
        return lax.ppermute(x, "space", outer_pairs)

    def from_later(x):
        return lax.ppermute(x, "tm", later)

    def both(x, pairs):
        return lax.ppermute(x, ("tm", "space"), pairs)

    w1, w1n = conv1_weight[1], conv1_weight[0]
    w2, w2n = conv2_weight[1], conv2_weight[0]
    bi = block_in
    ext = pltpu.VMEM((4, 12, COLS, C), BF)

    v0, rin, rout, v0s, b1s, b0s, dmi, dmo, dpi, dpo = run(
        start_kernel,
        [
            field(4, 8), field(3, 4, 2), field(3, 4, 2), field(2, 8), field(2, 8), field(2, 8),
            field(2), field(2), field(2, 2, 2), field(2, 2, 2),
        ],
        (pixel_cot, bi, frame_group, advantage),
        1,
        scratch=[],
        in_specs=[VM, VM, SM, SM],
    )
    rin, rout = swap_in(rin), swap_out(rout)
    b1x = lax.ppermute(b1s, "tm", sooner)
    dpi, dpo = both(dpi, corner(sooner, inner_pairs)), both(dpo, corner(sooner, outer_pairs))
    v0x = from_later(v0s)
    dmi, dmo = both(dmi, corner(later, inner_pairs)), both(dmo, corner(later, outer_pairs))
    b0x = lax.ppermute(b0s, "tm", sooner)

    ga, d1, d0 = run(
        early_kernel,
        [field(2, 10, dtype=F32), field(2, 8, dtype=F32), field(2, 8, dtype=F32)],
        (v0, bi, rin, rout, w2, w1, w1n),
        52,
        scratch=[ext, ext, ext],
    )
    v1x = run(pre01_kernel, field(2, 10), (bi, rin, rout, b1x, dpi, dpo, ga, w1), 20)
    v1xr = from_later(v1x)
    edges = [field(2, 8), field(4, 2), field(4, 2)]
    v1, ein, eout = run(pre23_kernel, edges, (v0, rin, rout, v0x, dmi, dmo, d1, v1x, w2), 16)
    r1in, r1out = swap_in(ein), swap_out(eout)
    d0a = run(factor01_kernel, field(2, 10, dtype=F32), (bi, rin, rout, b0x, dpi, dpo, w1n), 20)
    v2x = run(
        up01_kernel,
        field(2, 10),
        (v1x, v1, r1in, r1out, v0, rin, rout, w1),
        20,
        scratch=[ext, pltpu.VMEM((2, 12, COLS, C), BF)],
    )
    v2xr = from_later(v2x)
    v2, ein, eout = run(up23_kernel, edges, (v1, r1in, r1out, v1xr, v0, v2x, w1), 16)
    r2in, r2out = swap_in(ein), swap_out(eout)
    v3x = run(grad01_kernel, field(2, 10), (v2x, v2, r2in, r2out, d0a, w2n), 20)
    v3xr = from_later(v3x)
    v3, ein, eout = run(grad23_kernel, edges, (v2, r2in, r2out, v2xr, d0, v3x, w2n), 16)
    r3in, r3out = swap_in(ein), swap_out(eout)
    pool = run(
        last01_kernel, field(2, 4, dtype=F32), (v3x, v3, r3in, r3out, v2x, w1n), 16
    )
    owner = owner_map.reshape(-1, 1)
    units = owner.shape[0]
    capacity = max(2, 2 * units // strips)
    outgoing = run(
        last23_kernel,
        jax.ShapeDtypeStruct((strips * capacity, 8 * C), BF),
        (v3, r3in, r3out, v3xr, v2, pool, owner, w1n),
        16,
        scratch=[ext, pltpu.VMEM((4 * 4 * COLS, C), F32)],
    )
    outgoing = outgoing.reshape(strips, capacity, 8 * C)
    arrived = lax.all_to_all(outgoing, "space", split_axis=0, concat_axis=0, tiled=True)
    return arrived.reshape(1, 1, strips, capacity, 8 * C)


def solution(mesh):
    in_specs = (
        P("tm", "space", None, None),
        P("tm"),
        P(),
        P(None, "tm", "space", None, None),
        P(),
        P(),
        P("tm", "space", None, None),
    )
    out_specs = P("tm", "space", None, None, None)
    return jax.shard_map(
        on_device, mesh=mesh, in_specs=in_specs, out_specs=out_specs, check_vma=False
    )
```

profile of v0, /device:TPU:7, one launch (start us, length us, event | category | flops | bytes accessed | tf_op | source)
XLA Modules:
  0.0 97.6 jit_solution(11825136529464197385)
XLA Ops:
  0.0 1.2 %copy-done = bf16[2,4,8,64,128]{4,3,2,1,0:T(8,128)(2,1)S(1)} copy-done((bf16[2,4,8,64,128]{4,3,2,1,0:T(8,128)(2,1)S(1)}, bf16[2,4,8,64,128]{4,3,2,1,0:T(8,128)(2,1)}, u32[]{:S(2)}) %copy-start) | copy-done | bytes 1048600
  1.2 1.0 %copy-done.2 = bf16[4,8,64,128]{3,2,1,0:T(8,128)(2,1)S(1)} copy-done((bf16[4,8,64,128]{3,2,1,0:T(8,128)(2,1)S(1)}, bf16[4,8,64,128]{3,2,1,0:T(8,128)(2,1)}, u32[]{:S(2)}) %copy-start.2) | copy-done | bytes 524312
  2.3 0.7 copy-done.3
  2.9 0.7 copy-done.4
  3.6 0.8 start_kernel.1
  4.4 0.8 collective-permute-start
  5.1 3.4 %collective-permute-start.1 = (bf16[3,4,2,64,128]{4,3,2,1,0:T(8,128)(2,1)S(1)}, bf16[3,4,2,64,128]{4,3,2,1,0:T(8,128)(2,1)S(1)}, u32[]{:S(2)}, u32[]{:S(2)}) collective-permute-start(bf16[3,4,2,64,128]{4,3,2,1,0:T(8,128)(2,1)S(1)} %get-tuple-element.29), channel_id=1, source_target_pairs={{1,2},{2,1},{3,4},{4,3},{5,6},{6,5},{7,8},{8,7},{9,10},{10,9},{11,... | collective-permute-start | bytes 1179656 | tf_op jit(solution)/shard_map/ppermute | solution.py:281
  8.6 1.3 %collective-permute-start.6 = (bf16[2,2,2,64,128]{4,3,2,1,0:T(8,128)(2,1)S(1)}, bf16[2,2,2,64,128]{4,3,2,1,0:T(8,128)(2,1)S(1)}, u32[]{:S(2)}, u32[]{:S(2)}) collective-permute-start(bf16[2,2,2,64,128]{4,3,2,1,0:T(8,128)(2,1)S(1)} %get-tuple-element.35), channel_id=1, source_target_pairs={{0,33},{1,32},{2,35},{3,34},{4,37},{5,36},{6,39},{7,38},{8,41},{9,... | collective-permute-start | bytes 393224 | tf_op jit(solution)/shard_map/ppermute | solution.py:287
  9.9 1.3 %collective-permute-start.7 = (bf16[2,2,2,64,128]{4,3,2,1,0:T(8,128)(2,1)S(1)}, bf16[2,2,2,64,128]{4,3,2,1,0:T(8,128)(2,1)S(1)}, u32[]{:S(2)}, u32[]{:S(2)}) collective-permute-start(bf16[2,2,2,64,128]{4,3,2,1,0:T(8,128)(2,1)S(1)} %get-tuple-element.36), channel_id=1, source_target_pairs={{1,34},{2,33},{3,36},{4,35},{5,38},{6,37},{7,40},{8,39},{9,42},{10... | collective-permute-start | bytes 393224 | tf_op jit(solution)/shard_map/ppermute | solution.py:287
  11.2 0.0 copy-start.1
  11.2 1.4 %collective-permute-start.5 = (bf16[2,8,64,128]{3,2,1,0:T(8,128)(2,1)S(1)}, bf16[2,8,64,128]{3,2,1,0:T(8,128)(2,1)S(1)}, u32[]{:S(2)}, u32[]{:S(2)}) collective-permute-start(bf16[2,8,64,128]{3,2,1,0:T(8,128)(2,1)S(1)} %get-tuple-element.34), channel_id=1, source_target_pairs={{0,32},{32,64},{64,96},{1,33},{33,65},{65,97},{2,34},{34,66},{66,9... | collective-permute-start | bytes 786440 | tf_op jit(solution)/shard_map/ppermute | solution.py:306
  12.6 2.4 %slice_bitcast_fusion = (bf16[3,3,3,128,128]{4,3,2,1,0:T(8,128)(2,1)S(1)}, bf16[3,3,3,128,128]{4,3,2,1,0:T(8,128)(2,1)S(1)}, bf16[3,3,3,128,128]{4,3,2,1,0:T(8,128)(2,1)S(1)}, bf16[3,3,3,128,128]{4,3,2,1,0:T(8,128)(2,1)S(1)}) fusion(bf16[2,3,3,3,128,128]{5,4,3,2,1,0:T(8,128)(2,1)} %param.12, bf16[2,3,3,3,128,128]{5,4,3,2,1,0:T(8,128)(2,1)} %param.11), kind=kLoop, calls=%fused_computation | loop fusion | bytes 7077888 | tf_op jit(solution)/shard_map/squeeze | solution.py:290
  15.0 0.0 collective-permute-done.rin.r0in
  15.0 4.5 %collective-permute-start.2 = (bf16[2,8,64,128]{3,2,1,0:T(8,128)(2,1)S(1)}, bf16[2,8,64,128]{3,2,1,0:T(8,128)(2,1)S(1)}, u32[]{:S(2)}, u32[]{:S(2)}) collective-permute-start(bf16[2,8,64,128]{3,2,1,0:T(8,128)(2,1)S(1)} %get-tuple-element.30), channel_id=1, source_target_pairs={{32,0},{64,32},{96,64},{33,1},{65,33},{97,65},{34,2},{66,34},{98,6... | collective-permute-start | bytes 786440 | tf_op jit(solution)/shard_map/ppermute | solution.py:284
  19.6 0.0 collective-permute-done.1.rout.r0out
  19.6 3.7 %collective-permute-start.3 = (bf16[2,64,128]{2,1,0:T(8,128)(2,1)S(1)}, bf16[2,64,128]{2,1,0:T(8,128)(2,1)S(1)}, u32[]{:S(2)}, u32[]{:S(2)}) collective-permute-start(bf16[2,64,128]{2,1,0:T(8,128)(2,1)S(1)} %get-tuple-element.31), channel_id=1, source_target_pairs={{32,1},{33,0},{34,3},{35,2},{36,5},{37,4},{38,7},{39,6},{40,9},{41... | collective-permute-start | bytes 98312 | tf_op jit(solution)/shard_map/ppermute | solution.py:287
  23.2 4.5 %early_kernel.1 = (f32[2,10,64,128]{3,2,1,0:T(8,128)S(1)}, f32[2,8,64,128]{3,2,1,0:T(8,128)S(1)}, f32[2,8,64,128]{3,2,1,0:T(8,128)S(1)}) custom-call(bf16[4,8,64,128]{3,2,1,0:T(8,128)(2,1)S(1)} %get-tuple-element.27.v0, bf16[2,4,8,64,128]{4,3,2,1,0:T(8,128)(2,1)S(1)} %copy-done.1, bf16[3,4,2,64,128]{4,3,2,1,0:T(8,128)(2,1)S(1)} %collective-permute-done.rin.r0in, ...), custom_call_target="tpu_custom_call" | custom-call | flops 4416602112 | bytes 5013504 | tf_op jit(solution)/shard_map/early_kernel/pallas_call | solution.py:249
  27.8 6.8 %collective-permute-start.4 = (bf16[2,64,128]{2,1,0:T(8,128)(2,1)S(1)}, bf16[2,64,128]{2,1,0:T(8,128)(2,1)S(1)}, u32[]{:S(2)}, u32[]{:S(2)}) collective-permute-start(bf16[2,64,128]{2,1,0:T(8,128)(2,1)S(1)} %get-tuple-element.32), channel_id=1, source_target_pairs={{33,2},{34,1},{35,4},{36,3},{37,6},{38,5},{39,8},{40,7},{41,10},{4... | collective-permute-start | bytes 98312 | tf_op jit(solution)/shard_map/ppermute | solution.py:287
  34.5 0.0 collective-permute-done.7.dpo
  34.5 1.9 %pre01_kernel.1.v1x = bf16[2,10,64,128]{3,2,1,0:T(8,128)(2,1)S(1)} custom-call(bf16[2,4,8,64,128]{4,3,2,1,0:T(8,128)(2,1)S(1)} %copy-done.1, bf16[3,4,2,64,128]{4,3,2,1,0:T(8,128)(2,1)S(1)} %collective-permute-done.rin.r0in, bf16[3,4,2,64,128]{4,3,2,1,0:T(8,128)(2,1)S(1)} %collective-permute-done.1.rout.r0out, ...), custom_call_target="tpu_custom_call" | custom-call | flops 1698693120 | bytes 3899392 | tf_op jit(solution)/shard_map/pre01_kernel/pallas_call | solution.py:249
  36.4 1.3 %collective-permute-start.10 = (bf16[2,10,64,128]{3,2,1,0:T(8,128)(2,1)S(1)}, bf16[2,10,64,128]{3,2,1,0:T(8,128)(2,1)S(1)}, u32[]{:S(2)}, u32[]{:S(2)}) collective-permute-start(bf16[2,10,64,128]{3,2,1,0:T(8,128)(2,1)S(1)} %pre01_kernel.1.v1x), channel_id=1, source_target_pairs={{32,0},{64,32},{96,64},{33,1},{65,33},{97,65},{34,2},{66,34},{98,6... | collective-permute-start | bytes 983048 | tf_op jit(solution)/shard_map/ppermute | solution.py:284
  37.7 0.0 collective-permute-done.3.dmi
  37.7 0.0 collective-permute-done.4.dmo
  37.8 1.5 %pre23_kernel.1 = (bf16[2,8,64,128]{3,2,1,0:T(8,128)(2,1)S(1)}, bf16[4,2,64,128]{3,2,1,0:T(8,128)(2,1)S(1)}, bf16[4,2,64,128]{3,2,1,0:T(8,128)(2,1)S(1)}) custom-call(bf16[4,8,64,128]{3,2,1,0:T(8,128)(2,1)S(1)} %get-tuple-element.27.v0, bf16[3,4,2,64,128]{4,3,2,1,0:T(8,128)(2,1)S(1)} %collective-permute-done.rin.r0in, ...), custom_call_target="tpu_custom_call" | custom-call | flops 1358954496 | bytes 3375104 | tf_op jit(solution)/shard_map/pre23_kernel/pallas_call | solution.py:249
  39.3 0.1 collective-permute-start.8
  39.4 3.1 %collective-permute-start.9 = (bf16[4,2,64,128]{3,2,1,0:T(8,128)(2,1)S(1)}, bf16[4,2,64,128]{3,2,1,0:T(8,128)(2,1)S(1)}, u32[]{:S(2)}, u32[]{:S(2)}) collective-permute-start(bf16[4,2,64,128]{3,2,1,0:T(8,128)(2,1)S(1)} %get-tuple-element.40), channel_id=1, source_target_pairs={{1,2},{2,1},{3,4},{4,3},{5,6},{6,5},{7,8},{8,7},{9,10},{10,9},{11,... | collective-permute-start | bytes 393224 | tf_op jit(solution)/shard_map/ppermute | solution.py:281
  42.5 1.3 %collective-permute-start.14 = (bf16[2,8,64,128]{3,2,1,0:T(8,128)(2,1)S(1)}, bf16[2,8,64,128]{3,2,1,0:T(8,128)(2,1)S(1)}, u32[]{:S(2)}, u32[]{:S(2)}) collective-permute-start(bf16[2,8,64,128]{3,2,1,0:T(8,128)(2,1)S(1)} %get-tuple-element.45), channel_id=1, source_target_pairs={{0,32},{32,64},{64,96},{1,33},{33,65},{65,97},{2,34},{34,66},{66,9... | collective-permute-start | bytes 786440 | tf_op jit(solution)/shard_map/ppermute | solution.py:310
  43.8 2.2 %collective-permute-done.9.rout = bf16[4,2,64,128]{3,2,1,0:T(8,128)(2,1)S(1)} collective-permute-done((bf16[4,2,64,128]{3,2,1,0:T(8,128)(2,1)S(1)}, bf16[4,2,64,128]{3,2,1,0:T(8,128)(2,1)S(1)}, u32[]{:S(2)}, u32[]{:S(2)}) %collective-permute-start.9) | collective-permute-done | bytes 131104 | tf_op jit(solution)/shard_map/ppermute | solution.py:281
  45.9 1.8 %up01_kernel.1.v2x = bf16[2,10,64,128]{3,2,1,0:T(8,128)(2,1)S(1)} custom-call(bf16[2,10,64,128]{3,2,1,0:T(8,128)(2,1)S(1)} %pre01_kernel.1.v1x, bf16[2,8,64,128]{3,2,1,0:T(8,128)(2,1)S(1)} %get-tuple-element.38.v1, bf16[4,2,64,128]{3,2,1,0:T(8,128)(2,1)S(1)} %collective-permute-done.8.rin, bf16[4,2,64,128]{3,2,1,0:T(8,128)(2,1)S(1)} %collective-permute-done.9.rout, ...), custom_call_target="tpu_custom_call" | custom-call | flops 1698693120 | bytes 3047424 | tf_op jit(solution)/shard_map/up01_kernel/pallas_call | solution.py:249
  47.8 1.9 %collective-permute-start.13 = (bf16[2,10,64,128]{3,2,1,0:T(8,128)(2,1)S(1)}, bf16[2,10,64,128]{3,2,1,0:T(8,128)(2,1)S(1)}, u32[]{:S(2)}, u32[]{:S(2)}) collective-permute-start(bf16[2,10,64,128]{3,2,1,0:T(8,128)(2,1)S(1)} %up01_kernel.1.v2x), channel_id=1, source_target_pairs={{32,0},{64,32},{96,64},{33,1},{65,33},{97,65},{34,2},{66,34},{98,6... | collective-permute-start | bytes 983048 | tf_op jit(solution)/shard_map/ppermute | solution.py:284
  49.7 1.5 %up23_kernel.1 = (bf16[2,8,64,128]{3,2,1,0:T(8,128)(2,1)S(1)}, bf16[4,2,64,128]{3,2,1,0:T(8,128)(2,1)S(1)}, bf16[4,2,64,128]{3,2,1,0:T(8,128)(2,1)S(1)}) custom-call(bf16[2,8,64,128]{3,2,1,0:T(8,128)(2,1)S(1)} %get-tuple-element.38.v1, bf16[4,2,64,128]{3,2,1,0:T(8,128)(2,1)S(1)} %collective-permute-done.8.rin, ...), custom_call_target="tpu_custom_call" | custom-call | flops 1358954496 | bytes 2588672 | tf_op jit(solution)/shard_map/up23_kernel/pallas_call | solution.py:249
  51.2 0.1 collective-permute-start.11
  51.3 4.3 %collective-permute-start.12 = (bf16[4,2,64,128]{3,2,1,0:T(8,128)(2,1)S(1)}, bf16[4,2,64,128]{3,2,1,0:T(8,128)(2,1)S(1)}, u32[]{:S(2)}, u32[]{:S(2)}) collective-permute-start(bf16[4,2,64,128]{3,2,1,0:T(8,128)(2,1)S(1)} %get-tuple-element.43), channel_id=1, source_target_pairs={{1,2},{2,1},{3,4},{4,3},{5,6},{6,5},{7,8},{8,7},{9,10},{10,9},{11,... | collective-permute-start | bytes 393224 | tf_op jit(solution)/shard_map/ppermute | solution.py:281
  55.6 1.8 %factor01_kernel.1.d = f32[2,10,64,128]{3,2,1,0:T(8,128)S(1)} custom-call(bf16[2,4,8,64,128]{4,3,2,1,0:T(8,128)(2,1)S(1)} %copy-done.1, bf16[3,4,2,64,128]{4,3,2,1,0:T(8,128)(2,1)S(1)} %collective-permute-done.rin.r0in, bf16[3,4,2,64,128]{4,3,2,1,0:T(8,128)(2,1)S(1)} %collective-permute-done.1.rout.r0out, ...), custom_call_target="tpu_custom_call" | custom-call | flops 1698693120 | bytes 3244032 | tf_op jit(solution)/shard_map/factor01_kernel/pallas_call | solution.py:249
  57.5 0.6 collective-permute-done.12.rout
  58.1 1.8 %grad01_kernel.1.v3x = bf16[2,10,64,128]{3,2,1,0:T(8,128)(2,1)S(1)} custom-call(bf16[2,10,64,128]{3,2,1,0:T(8,128)(2,1)S(1)} %up01_kernel.1.v2x, bf16[2,8,64,128]{3,2,1,0:T(8,128)(2,1)S(1)} %get-tuple-element.41.v2, bf16[4,2,64,128]{3,2,1,0:T(8,128)(2,1)S(1)} %collective-permute-done.11.rin, bf16[4,2,64,128]{3,2,1,0:T(8,128)(2,1)S(1)} %collective-permute-done.12.rout, ...), custom_call_target="tpu_custom_call" | custom-call | flops 1698693120 | bytes 2392064 | tf_op jit(solution)/shard_map/grad01_kernel/pallas_call | solution.py:249
  59.9 1.9 %collective-permute-start.17 = (bf16[2,10,64,128]{3,2,1,0:T(8,128)(2,1)S(1)}, bf16[2,10,64,128]{3,2,1,0:T(8,128)(2,1)S(1)}, u32[]{:S(2)}, u32[]{:S(2)}) collective-permute-start(bf16[2,10,64,128]{3,2,1,0:T(8,128)(2,1)S(1)} %grad01_kernel.1.v3x), channel_id=1, source_target_pairs={{32,0},{64,32},{96,64},{33,1},{65,33},{97,65},{34,2},{66,34},{98,6... | collective-permute-start | bytes 983048 | tf_op jit(solution)/shard_map/ppermute | solution.py:284
  61.8 0.0 copy-start.5
  61.8 1.5 %grad23_kernel.1 = (bf16[2,8,64,128]{3,2,1,0:T(8,128)(2,1)S(1)}, bf16[4,2,64,128]{3,2,1,0:T(8,128)(2,1)S(1)}, bf16[4,2,64,128]{3,2,1,0:T(8,128)(2,1)S(1)}) custom-call(bf16[2,8,64,128]{3,2,1,0:T(8,128)(2,1)S(1)} %get-tuple-element.41.v2, bf16[4,2,64,128]{3,2,1,0:T(8,128)(2,1)S(1)} %collective-permute-done.11.rin, ...), custom_call_target="tpu_custom_call" | custom-call | flops 1358954496 | bytes 2588672 | tf_op jit(solution)/shard_map/grad23_kernel/pallas_call | solution.py:249
  63.4 0.1 collective-permute-start.15
  63.5 4.9 %collective-permute-start.16 = (bf16[4,2,64,128]{3,2,1,0:T(8,128)(2,1)S(1)}, bf16[4,2,64,128]{3,2,1,0:T(8,128)(2,1)S(1)}, u32[]{:S(2)}, u32[]{:S(2)}) collective-permute-start(bf16[4,2,64,128]{3,2,1,0:T(8,128)(2,1)S(1)} %get-tuple-element.48), channel_id=1, source_target_pairs={{1,2},{2,1},{3,4},{4,3},{5,6},{6,5},{7,8},{8,7},{9,10},{10,9},{11,... | collective-permute-start | bytes 393224 | tf_op jit(solution)/shard_map/ppermute | solution.py:281
  68.4 0.1 copy.8.owner
  68.5 2.5 %collective-permute-done.16.rout = bf16[4,2,64,128]{3,2,1,0:T(8,128)(2,1)S(1)} collective-permute-done((bf16[4,2,64,128]{3,2,1,0:T(8,128)(2,1)S(1)}, bf16[4,2,64,128]{3,2,1,0:T(8,128)(2,1)S(1)}, u32[]{:S(2)}, u32[]{:S(2)}) %collective-permute-start.16) | collective-permute-done | bytes 131104 | tf_op jit(solution)/shard_map/ppermute | solution.py:281
  71.0 1.5 %last01_kernel.1.pool = f32[2,4,64,128]{3,2,1,0:T(8,128)S(1)} custom-call(bf16[2,10,64,128]{3,2,1,0:T(8,128)(2,1)S(1)} %grad01_kernel.1.v3x, bf16[2,8,64,128]{3,2,1,0:T(8,128)(2,1)S(1)} %get-tuple-element.46.v3, bf16[4,2,64,128]{3,2,1,0:T(8,128)(2,1)S(1)} %collective-permute-done.15.rin, bf16[4,2,64,128]{3,2,1,0:T(8,128)(2,1)S(1)} %collective-permute-done.16.rout, ...), custom_call_target="tpu_custom_call" | custom-call | flops 1358954496 | bytes 2064384 | tf_op jit(solution)/shard_map/last01_kernel/pallas_call | solution.py:249
  72.5 1.8 %last23_kernel.1 = bf16[128,1024]{1,0:T(8,128)(2,1)S(1)} custom-call(bf16[2,8,64,128]{3,2,1,0:T(8,128)(2,1)S(1)} %get-tuple-element.46.v3, bf16[4,2,64,128]{3,2,1,0:T(8,128)(2,1)S(1)} %collective-permute-done.15.rin, bf16[4,2,64,128]{3,2,1,0:T(8,128)(2,1)S(1)} %collective-permute-done.16.rout, bf16[2,10,64,128]{3,2,1,0:T(8,128)(2,1)S(1)} %collective-permute-done.17.vxr, ...), custom_call_target="tpu_custom_call" | custom-call | flops 1358954496 | bytes 2261248 | tf_op jit(solution)/shard_map/last23_kernel/pallas_call | solution.py:249
  74.3 0.1 reshape.10
  74.4 22.5 %all_to_all.5 = bf16[32,4,1024]{2,1,0:T(4,128)(2,1)S(1)} all-to-all(bf16[32,4,1024]{2,1,0:T(4,128)(2,1)S(1)} %reshape.10), channel_id=1, replica_groups=mesh['tm'=4,'space'=32] {'space'}, dimensions={0} | all-to-all | bytes 524288 | tf_op jit(solution)/shard_map/all_to_all | solution.py:353
  96.9 0.7 copy.10
  (16 shorter events, 0.0 us)
Async XLA Ops:
  0.0 1.2 %copy-start = (bf16[2,4,8,64,128]{4,3,2,1,0:T(8,128)(2,1)S(1)}, bf16[2,4,8,64,128]{4,3,2,1,0:T(8,128)(2,1)}, u32[]{:S(2)}) copy-start(bf16[2,4,8,64,128]{4,3,2,1,0:T(8,128)(2,1)} %bi.7) | copy-start | bytes 3145732
  1.2 1.0 %copy-start.2 = (bf16[4,8,64,128]{3,2,1,0:T(8,128)(2,1)S(1)}, bf16[4,8,64,128]{3,2,1,0:T(8,128)(2,1)}, u32[]{:S(2)}) copy-start(bf16[4,8,64,128]{3,2,1,0:T(8,128)(2,1)} %cot.1) | copy-start | bytes 1572868
  2.3 0.7 copy-start.3
  2.9 0.7 copy-start.4
  4.4 10.6 %collective-permute-start = (bf16[3,4,2,64,128]{4,3,2,1,0:T(8,128)(2,1)S(1)}, bf16[3,4,2,64,128]{4,3,2,1,0:T(8,128)(2,1)S(1)}, u32[]{:S(2)}, u32[]{:S(2)}) collective-permute-start(bf16[3,4,2,64,128]{4,3,2,1,0:T(8,128)(2,1)S(1)} %get-tuple-element.28), channel_id=1, source_target_pairs={{0,1},{1,0},{2,3},{3,2},{4,5},{5,4},{6,7},{7,6},{8,9},{9,8},{10,11... | collective-permute-start | bytes 1179656 | tf_op jit(solution)/shard_map/ppermute | solution.py:278
  5.1 14.5 %collective-permute-start.1 = (bf16[3,4,2,64,128]{4,3,2,1,0:T(8,128)(2,1)S(1)}, bf16[3,4,2,64,128]{4,3,2,1,0:T(8,128)(2,1)S(1)}, u32[]{:S(2)}, u32[]{:S(2)}) collective-permute-start(bf16[3,4,2,64,128]{4,3,2,1,0:T(8,128)(2,1)S(1)} %get-tuple-element.29), channel_id=1, source_target_pairs={{1,2},{2,1},{3,4},{4,3},{5,6},{6,5},{7,8},{8,7},{9,10},{10,9},{11,... | collective-permute-start | bytes 1179656 | tf_op jit(solution)/shard_map/ppermute | solution.py:281
  8.6 19.2 %collective-permute-start.6 = (bf16[2,2,2,64,128]{4,3,2,1,0:T(8,128)(2,1)S(1)}, bf16[2,2,2,64,128]{4,3,2,1,0:T(8,128)(2,1)S(1)}, u32[]{:S(2)}, u32[]{:S(2)}) collective-permute-start(bf16[2,2,2,64,128]{4,3,2,1,0:T(8,128)(2,1)S(1)} %get-tuple-element.35), channel_id=1, source_target_pairs={{0,33},{1,32},{2,35},{3,34},{4,37},{5,36},{6,39},{7,38},{8,41},{9,... | collective-permute-start | bytes 393224 | tf_op jit(solution)/shard_map/ppermute | solution.py:287
  9.9 24.7 %collective-permute-start.7 = (bf16[2,2,2,64,128]{4,3,2,1,0:T(8,128)(2,1)S(1)}, bf16[2,2,2,64,128]{4,3,2,1,0:T(8,128)(2,1)S(1)}, u32[]{:S(2)}, u32[]{:S(2)}) collective-permute-start(bf16[2,2,2,64,128]{4,3,2,1,0:T(8,128)(2,1)S(1)} %get-tuple-element.36), channel_id=1, source_target_pairs={{1,34},{2,33},{3,36},{4,35},{5,38},{6,37},{7,40},{8,39},{9,42},{10... | collective-permute-start | bytes 393224 | tf_op jit(solution)/shard_map/ppermute | solution.py:287
  11.2 12.1 %copy-start.1 = (bf16[2,4,8,64,128]{4,3,2,1,0:T(8,128)(2,1)S(1)}, bf16[2,4,8,64,128]{4,3,2,1,0:T(8,128)(2,1)}, u32[]{:S(2)}) copy-start(bf16[2,4,8,64,128]{4,3,2,1,0:T(8,128)(2,1)} %bi.7) | copy-start | bytes 3145732
  11.2 23.4 %collective-permute-start.5 = (bf16[2,8,64,128]{3,2,1,0:T(8,128)(2,1)S(1)}, bf16[2,8,64,128]{3,2,1,0:T(8,128)(2,1)S(1)}, u32[]{:S(2)}, u32[]{:S(2)}) collective-permute-start(bf16[2,8,64,128]{3,2,1,0:T(8,128)(2,1)S(1)} %get-tuple-element.34), channel_id=1, source_target_pairs={{0,32},{32,64},{64,96},{1,33},{33,65},{65,97},{2,34},{34,66},{66,9... | collective-permute-start | bytes 786440 | tf_op jit(solution)/shard_map/ppermute | solution.py:306
  15.0 22.8 %collective-permute-start.2 = (bf16[2,8,64,128]{3,2,1,0:T(8,128)(2,1)S(1)}, bf16[2,8,64,128]{3,2,1,0:T(8,128)(2,1)S(1)}, u32[]{:S(2)}, u32[]{:S(2)}) collective-permute-start(bf16[2,8,64,128]{3,2,1,0:T(8,128)(2,1)S(1)} %get-tuple-element.30), channel_id=1, source_target_pairs={{32,0},{64,32},{96,64},{33,1},{65,33},{97,65},{34,2},{66,34},{98,6... | collective-permute-start | bytes 786440 | tf_op jit(solution)/shard_map/ppermute | solution.py:284
  19.6 18.2 %collective-permute-start.3 = (bf16[2,64,128]{2,1,0:T(8,128)(2,1)S(1)}, bf16[2,64,128]{2,1,0:T(8,128)(2,1)S(1)}, u32[]{:S(2)}, u32[]{:S(2)}) collective-permute-start(bf16[2,64,128]{2,1,0:T(8,128)(2,1)S(1)} %get-tuple-element.31), channel_id=1, source_target_pairs={{32,1},{33,0},{34,3},{35,2},{36,5},{37,4},{38,7},{39,6},{40,9},{41... | collective-permute-start | bytes 98312 | tf_op jit(solution)/shard_map/ppermute | solution.py:287
  27.8 10.0 %collective-permute-start.4 = (bf16[2,64,128]{2,1,0:T(8,128)(2,1)S(1)}, bf16[2,64,128]{2,1,0:T(8,128)(2,1)S(1)}, u32[]{:S(2)}, u32[]{:S(2)}) collective-permute-start(bf16[2,64,128]{2,1,0:T(8,128)(2,1)S(1)} %get-tuple-element.32), channel_id=1, source_target_pairs={{33,2},{34,1},{35,4},{36,3},{37,6},{38,5},{39,8},{40,7},{41,10},{4... | collective-permute-start | bytes 98312 | tf_op jit(solution)/shard_map/ppermute | solution.py:287
  36.4 13.3 %collective-permute-start.10 = (bf16[2,10,64,128]{3,2,1,0:T(8,128)(2,1)S(1)}, bf16[2,10,64,128]{3,2,1,0:T(8,128)(2,1)S(1)}, u32[]{:S(2)}, u32[]{:S(2)}) collective-permute-start(bf16[2,10,64,128]{3,2,1,0:T(8,128)(2,1)S(1)} %pre01_kernel.1.v1x), channel_id=1, source_target_pairs={{32,0},{64,32},{96,64},{33,1},{65,33},{97,65},{34,2},{66,34},{98,6... | collective-permute-start | bytes 983048 | tf_op jit(solution)/shard_map/ppermute | solution.py:284
  39.3 4.5 %collective-permute-start.8 = (bf16[4,2,64,128]{3,2,1,0:T(8,128)(2,1)S(1)}, bf16[4,2,64,128]{3,2,1,0:T(8,128)(2,1)S(1)}, u32[]{:S(2)}, u32[]{:S(2)}) collective-permute-start(bf16[4,2,64,128]{3,2,1,0:T(8,128)(2,1)S(1)} %get-tuple-element.39), channel_id=1, source_target_pairs={{0,1},{1,0},{2,3},{3,2},{4,5},{5,4},{6,7},{7,6},{8,9},{9,8},{10,11... | collective-permute-start | bytes 393224 | tf_op jit(solution)/shard_map/ppermute | solution.py:278
  39.4 6.6 %collective-permute-start.9 = (bf16[4,2,64,128]{3,2,1,0:T(8,128)(2,1)S(1)}, bf16[4,2,64,128]{3,2,1,0:T(8,128)(2,1)S(1)}, u32[]{:S(2)}, u32[]{:S(2)}) collective-permute-start(bf16[4,2,64,128]{3,2,1,0:T(8,128)(2,1)S(1)} %get-tuple-element.40), channel_id=1, source_target_pairs={{1,2},{2,1},{3,4},{4,3},{5,6},{6,5},{7,8},{8,7},{9,10},{10,9},{11,... | collective-permute-start | bytes 393224 | tf_op jit(solution)/shard_map/ppermute | solution.py:281
  42.5 13.2 %collective-permute-start.14 = (bf16[2,8,64,128]{3,2,1,0:T(8,128)(2,1)S(1)}, bf16[2,8,64,128]{3,2,1,0:T(8,128)(2,1)S(1)}, u32[]{:S(2)}, u32[]{:S(2)}) collective-permute-start(bf16[2,8,64,128]{3,2,1,0:T(8,128)(2,1)S(1)} %get-tuple-element.45), channel_id=1, source_target_pairs={{0,32},{32,64},{64,96},{1,33},{33,65},{65,97},{2,34},{34,66},{66,9... | collective-permute-start | bytes 786440 | tf_op jit(solution)/shard_map/ppermute | solution.py:310
  47.8 14.1 %collective-permute-start.13 = (bf16[2,10,64,128]{3,2,1,0:T(8,128)(2,1)S(1)}, bf16[2,10,64,128]{3,2,1,0:T(8,128)(2,1)S(1)}, u32[]{:S(2)}, u32[]{:S(2)}) collective-permute-start(bf16[2,10,64,128]{3,2,1,0:T(8,128)(2,1)S(1)} %up01_kernel.1.v2x), channel_id=1, source_target_pairs={{32,0},{64,32},{96,64},{33,1},{65,33},{97,65},{34,2},{66,34},{98,6... | collective-permute-start | bytes 983048 | tf_op jit(solution)/shard_map/ppermute | solution.py:284
  51.2 6.3 %collective-permute-start.11 = (bf16[4,2,64,128]{3,2,1,0:T(8,128)(2,1)S(1)}, bf16[4,2,64,128]{3,2,1,0:T(8,128)(2,1)S(1)}, u32[]{:S(2)}, u32[]{:S(2)}) collective-permute-start(bf16[4,2,64,128]{3,2,1,0:T(8,128)(2,1)S(1)} %get-tuple-element.42), channel_id=1, source_target_pairs={{0,1},{1,0},{2,3},{3,2},{4,5},{5,4},{6,7},{7,6},{8,9},{9,8},{10,11... | collective-permute-start | bytes 393224 | tf_op jit(solution)/shard_map/ppermute | solution.py:278
  51.3 6.8 %collective-permute-start.12 = (bf16[4,2,64,128]{3,2,1,0:T(8,128)(2,1)S(1)}, bf16[4,2,64,128]{3,2,1,0:T(8,128)(2,1)S(1)}, u32[]{:S(2)}, u32[]{:S(2)}) collective-permute-start(bf16[4,2,64,128]{3,2,1,0:T(8,128)(2,1)S(1)} %get-tuple-element.43), channel_id=1, source_target_pairs={{1,2},{2,1},{3,4},{4,3},{5,6},{6,5},{7,8},{8,7},{9,10},{10,9},{11,... | collective-permute-start | bytes 393224 | tf_op jit(solution)/shard_map/ppermute | solution.py:281
  59.9 12.6 %collective-permute-start.17 = (bf16[2,10,64,128]{3,2,1,0:T(8,128)(2,1)S(1)}, bf16[2,10,64,128]{3,2,1,0:T(8,128)(2,1)S(1)}, u32[]{:S(2)}, u32[]{:S(2)}) collective-permute-start(bf16[2,10,64,128]{3,2,1,0:T(8,128)(2,1)S(1)} %grad01_kernel.1.v3x), channel_id=1, source_target_pairs={{32,0},{64,32},{96,64},{33,1},{65,33},{97,65},{34,2},{66,34},{98,6... | collective-permute-start | bytes 983048 | tf_op jit(solution)/shard_map/ppermute | solution.py:284
  61.8 6.5 %copy-start.5 = (s32[1,1,64,1]{2,3,1,0:T(1,128)S(1)}, s32[1,1,64,1]{2,3,1,0:T(1,128)}, u32[]{:S(2)}) copy-start(s32[1,1,64,1]{2,3,1,0:T(1,128)} %param.13) | copy-start | bytes 772
  63.4 5.1 %collective-permute-start.15 = (bf16[4,2,64,128]{3,2,1,0:T(8,128)(2,1)S(1)}, bf16[4,2,64,128]{3,2,1,0:T(8,128)(2,1)S(1)}, u32[]{:S(2)}, u32[]{:S(2)}) collective-permute-start(bf16[4,2,64,128]{3,2,1,0:T(8,128)(2,1)S(1)} %get-tuple-element.47), channel_id=1, source_target_pairs={{0,1},{1,0},{2,3},{3,2},{4,5},{5,4},{6,7},{7,6},{8,9},{9,8},{10,11... | collective-permute-start | bytes 393224 | tf_op jit(solution)/shard_map/ppermute | solution.py:278
  63.5 7.5 %collective-permute-start.16 = (bf16[4,2,64,128]{3,2,1,0:T(8,128)(2,1)S(1)}, bf16[4,2,64,128]{3,2,1,0:T(8,128)(2,1)S(1)}, u32[]{:S(2)}, u32[]{:S(2)}) collective-permute-start(bf16[4,2,64,128]{3,2,1,0:T(8,128)(2,1)S(1)} %get-tuple-element.48), channel_id=1, source_target_pairs={{1,2},{2,1},{3,4},{4,3},{5,6},{6,5},{7,8},{8,7},{9,10},{10,9},{11,... | collective-permute-start | bytes 393224 | tf_op jit(solution)/shard_map/ppermute | solution.py:281
where the time goes:
time: 98.2 us; the launch traced here: 97.6 us
  starting transfers between devices  42.2 us (43%)
  blocking collectives  22.5 us (23%)
  Pallas kernels  20.4 us (21%)
  local copies, waits for them, and re-layouts  6.88 us (7%)
  waiting for transfers between devices  5.33 us (5%)
    all_to_all x1, blocking collectives, on_device(): lax.all_to_all(outgoing, 'space', split_axis=0, concat_axis=0, tiled=True)  22.5 us
    pallas_call x11, Pallas kernels, run(): pl.pallas_call(kernel, out_shape=outs, in_specs=in_specs or [VM] * len(ar...  20.4 us
    ppermute x4, starting transfers between devices, swap_out(): return lax.ppermute(x, 'space', outer_pairs)  15.8 us
    ppermute x4, starting transfers between devices, both(): return lax.ppermute(x, ('tm', 'space'), pairs)  13 us
    ppermute x4, starting transfers between devices, from_later(): return lax.ppermute(x, 'tm', later)  9.69 us
    ppermute x4, waiting for transfers between devices, swap_out(): return lax.ppermute(x, 'space', outer_pairs)  5.29 us
    unnamed x13, local copies, waits for them, and re-layouts  4.29 us
    squeeze x1, local copies, waits for them, and re-layouts, on_device(): w2, w2n = (conv2_weight[1], conv2_weight[0])  2.38 us
  transfers between devices with their start and end apart: 18, of which 3 were waited for; matrix products, arithmetic and copies ran while one was open for 3% of the time, Pallas kernels for 18%

commit v1 on v0

v1 whole, which is shorter than its diff:
```python
import jax
import jax.numpy as jnp
from jax import lax
from jax.experimental import pallas as pl
from jax.experimental.pallas import tpu as pltpu
from jax.sharding import PartitionSpec as P

COLS = 64
C = 128
BF = jnp.bfloat16
F32 = jnp.float32


def side():
    return lax.rem(lax.axis_index("space"), 2)


def shift_add(partial):
    m = partial.shape[0]
    col = lax.broadcasted_iota(jnp.int32, (m, C), 0) % COLS
    low = jnp.where(col == 0, 0.0, pltpu.roll(partial[:, :C], 1, 0))
    high = jnp.where(col == COLS - 1, 0.0, pltpu.roll(partial[:, 2 * C :], m - 1, 0))
    return low + partial[:, C : 2 * C] + high


def patches(ext, t, r0, nr, steps=(0, 1, 2)):
    return jnp.concatenate(
        [
            ext[t + dt, r0 + dr : r0 + dr + nr].reshape(nr * COLS, C)
            for dt in steps
            for dr in range(3)
        ],
        axis=1,
    )


def conv_back(ext, w, layer, t, r0, nr, steps=(0, 1, 2)):
    rhs = jnp.concatenate(
        [
            jnp.concatenate([w[layer, 2 - dt, 2 - dr, 2 - j] for j in range(3)], axis=0)
            for dt in steps
            for dr in range(3)
        ],
        axis=1,
    )
    out = lax.dot_general(
        patches(ext, t, r0, nr, steps),
        rhs,
        (((1,), (1,)), ((), ())),
        preferred_element_type=F32,
    )
    return shift_add(out).reshape(nr, COLS, C)


def conv_fore(ext, w, layer, t, r0, nr):
    rhs = jnp.concatenate(
        [
            jnp.concatenate([w[layer, dt, dr, j] for j in range(3)], axis=1)
            for dt in range(3)
            for dr in range(3)
        ],
        axis=0,
    )
    out = jnp.dot(patches(ext, t, r0, nr), rhs, preferred_element_type=F32)
    return shift_add(out).reshape(nr, COLS, C)


def factor(pre):
    s = jax.nn.sigmoid(pre)
    return s * (1.0 + pre * (1.0 - s))


def inside(outer):
    s = lax.axis_index("space")
    end = (s == 0) | (s == lax.axis_size("space") - 1)
    return jnp.where(end, jnp.zeros_like(outer), outer)


def with_later(halo):
    last = lax.axis_index("tm") == lax.axis_size("tm") - 1
    return jnp.where(last, jnp.zeros_like(halo), halo)


def with_sooner(halo):
    return jnp.where(lax.axis_index("tm") == 0, jnp.zeros_like(halo), halo)


def put_edges(ext, frames, inner, outer):
    p = side()
    ext[frames, pl.ds(10 * (1 - p), 2)] = inner
    ext[frames, pl.ds(10 * p, 2)] = inside(outer)


def store_ten(out, t, value):
    value = value.astype(BF)
    s = lax.axis_index("space")
    zero = jnp.zeros((1, COLS, C), BF)
    out[t, 1:9] = value[1:9]
    out[t, 0:1] = jnp.where(s == 0, zero, value[0:1])
    out[t, 9:10] = jnp.where(s == lax.axis_size("space") - 1, zero, value[9:10])


def send_edges(first, late, rin, rout):
    p = side()
    rin[0:2] = first[:, pl.ds(1 + 6 * (1 - p), 2)]
    rout[0:2] = first[:, pl.ds(1 + 6 * p, 2)]
    rin[2:4] = late[:, pl.ds(6 * (1 - p), 2)]
    rout[2:4] = late[:, pl.ds(6 * p, 2)]


def start_kernel(cot, bi, group, adv, v0, rin, rout, raw, gs, ads, sem):
    p = side()
    inner, outer = pl.ds(6 * (1 - p), 2), pl.ds(6 * p, 2)
    copies = [
        pltpu.make_async_copy(group, gs, sem.at[0]),
        pltpu.make_async_copy(adv, ads, sem.at[1]),
    ]
    copies += [pltpu.make_async_copy(cot.at[t], raw.at[t], sem.at[2 + t]) for t in range(4)]
    for k in range(2):
        copies += [
            pltpu.make_async_copy(bi.at[1 - k, :, inner], rin.at[1 + k], sem.at[6 + 2 * k]),
            pltpu.make_async_copy(bi.at[1 - k, :, outer], rout.at[1 + k], sem.at[7 + 2 * k]),
        ]
    for copy in copies:
        copy.start()
    copies[0].wait()
    copies[1].wait()
    for t in range(4):
        copies[2 + t].wait()
        scale = ads[gs[t]]
        v0[t] = (raw[t].astype(F32) * scale).astype(BF)
        rin[0, t] = (raw[t, inner].astype(F32) * scale).astype(BF)
        rout[0, t] = (raw[t, outer].astype(F32) * scale).astype(BF)
    for copy in copies[6:]:
        copy.wait()


def extend_kernel(v0, bi, rin, rout, vx, bx):
    p = side()
    for t in range(2):
        vx[t, 1:9] = v0[t]
        vx[t, 9 * (1 - p)] = rin[0, t, p]
        vx[t, 9 * p] = inside(rout[0, t, 1 - p])
    bx[:, 2:10] = bi[1, 2:4]
    put_edges(bx, slice(0, 2), rin[1, 2:4], rout[1, 2:4])


def early_kernel(v0, bi, rin, rout, w2, w1h, ga, d1, d0, bx, ext, ext1, ext0, w1, sem):
    weights = pltpu.make_async_copy(w1h, w1, sem)
    weights.start()
    ext[:, 2:10] = v0[...]
    put_edges(ext, slice(0, 4), rin[0], rout[0])
    for k, old in enumerate((ext1, ext0)):
        old[:, 2:10] = bi[1 - k]
        put_edges(old, slice(0, 4), rin[1 + k], rout[1 + k])
    bx[...] = ext0[2:4]
    for t in range(2):
        ga[t] = conv_back(ext, w2, 1, t, 0, 10)
    weights.wait()
    for k, (old, d) in enumerate(((ext1, d1), (ext0, d0))):
        for t in range(2):
            d[t] = factor(conv_fore(old, w1, 1 - k, t, 1, 8))


def fore_halo(ext, k, bi, rin, rout, bx):
    ext[0:2] = with_sooner(bx[...])
    ext[2:4, 2:10] = bi[1 - k, 0:2]
    put_edges(ext, slice(2, 4), rin[1 + k, 0:2], rout[1 + k, 0:2])


def pre01_kernel(bi, rin, rout, bx, ga, w1, v1x, ext):
    fore_halo(ext, 0, bi, rin, rout, bx)
    for t in range(2):
        store_ten(v1x, t, ga[t] * factor(conv_fore(ext, w1, 1, t, 0, 10)))


def factor01_kernel(bi, rin, rout, bx, w1, d, ext):
    fore_halo(ext, 1, bi, rin, rout, bx)
    for t in range(2):
        d[t] = factor(conv_fore(ext, w1, 0, t, 0, 10))


def pre23_kernel(v0, rin, rout, vx, d, v1x, w2, v1, ein, eout, ext):
    ext[0:2, 2:10] = v0[2:4]
    put_edges(ext, slice(0, 2), rin[0, 2:4], rout[0, 2:4])
    ext[2:4, 1:11] = with_later(vx[...])
    for t in range(2):
        v1[t] = (conv_back(ext, w2, 1, t, 1, 8) * d[t]).astype(BF)
    send_edges(v1x, v1, ein, eout)


def local01(ext, vx, v, rin, rout):
    ext[0:2, 1:11] = vx[...]
    ext[2:4, 2:10] = v[...]
    put_edges(ext, slice(0, 4), rin[...], rout[...])


def local23(ext, v, rin, rout, vxr):
    ext[0:2, 2:10] = v[...]
    put_edges(ext, slice(0, 2), rin[2:4], rout[2:4])
    ext[2:4, 1:11] = with_later(vxr[...])


def up01_kernel(v1x, v1, rin, rout, v0, r0in, r0out, w1, v2x, ext, old):
    p = side()
    local01(ext, v1x, v1, rin, rout)
    old[:, 2:10] = v0[0:2]
    put_edges(old, slice(0, 2), r0in[0, 0:2], r0out[0, 0:2])
    for t in range(2):
        store_ten(v2x, t, old[t, 1:11].astype(F32) + conv_back(ext, w1, 1, t, 0, 10))


def up23_kernel(v1, rin, rout, vxr, v0, v2x, w1, v2, ein, eout, ext):
    local23(ext, v1, rin, rout, vxr)
    for t in range(2):
        v2[t] = (v0[2 + t].astype(F32) + conv_back(ext, w1, 1, t, 1, 8)).astype(BF)
    send_edges(v2x, v2, ein, eout)


def grad01_kernel(v2x, v2, rin, rout, d, w2, v3x, ext):
    local01(ext, v2x, v2, rin, rout)
    for t in range(2):
        store_ten(v3x, t, conv_back(ext, w2, 0, t, 0, 10) * d[t])


def grad23_kernel(v2, rin, rout, vxr, d, v3x, w2, v3, ein, eout, ext):
    local23(ext, v2, rin, rout, vxr)
    for t in range(2):
        v3[t] = (conv_back(ext, w2, 0, t, 1, 8) * d[t]).astype(BF)
    send_edges(v3x, v3, ein, eout)


def row_pairs(up):
    up = up.astype(BF).astype(F32).reshape(4, 2, COLS, C)
    return up[:, 0] + up[:, 1]


def last01_kernel(v3x, v3, rin, rout, v2x, v2, w1, pool, part, ext):
    local01(ext, v3x, v3, rin, rout)
    for t in range(2):
        pool[t] = row_pairs(v2x[t, 1:9].astype(F32) + conv_back(ext, w1, 0, t, 1, 8))
    for t, steps in ((0, (0, 1)), (1, (0,))):
        part[t] = v2[t].astype(F32) + conv_back(ext, w1, 0, 2 + t, 1, 8, steps)


def last23_kernel(vxr, pool, part, owner, w1, out, ext, rows):
    ext[2:4, 1:11] = with_later(vxr[...])
    half = 2 * 4 * COLS
    rows[0:half] = pool[...].reshape(half, C)
    for t, steps in ((0, (2,)), (1, (1, 2))):
        pair = row_pairs(part[t] + conv_back(ext, w1, 0, t, 1, 8, steps))
        rows[half + t * 4 * COLS : half + (t + 1) * 4 * COLS] = pair.reshape(4 * COLS, C)
    units = owner.shape[0]
    strips, capacity = out.shape[0], out.shape[1]
    slots = strips * capacity
    u = lax.broadcasted_iota(jnp.int32, (units, units), 0)
    v = lax.broadcasted_iota(jnp.int32, (units, units), 1)
    mine = jnp.broadcast_to(owner[...], (units, units))
    named = jnp.sum(jnp.where(u == v, mine, 0), axis=0, keepdims=True)
    same = jnp.where((mine == named) & (u < v), 1, 0)
    slot = named * capacity + jnp.sum(same, axis=0, keepdims=True)
    place = jnp.where(
        lax.broadcasted_iota(jnp.int32, (slots, units), 0) == slot, 1.0, 0.0
    ).astype(BF)
    for j in range(8):
        even = rows[pl.ds(2 * j, units, stride=16), :]
        odd = rows[pl.ds(2 * j + 1, units, stride=16), :]
        unit = (even + odd).astype(BF)
        sent = jnp.dot(place, unit, preferred_element_type=F32)
        out[:, :, j * C : (j + 1) * C] = sent.reshape(strips, capacity, C).astype(BF)


VM = pl.BlockSpec(memory_space=pltpu.VMEM)
SM = pl.BlockSpec(memory_space=pltpu.SMEM)


def field(*lead, dtype=BF):
    return jax.ShapeDtypeStruct((*lead, COLS, C), dtype)


def run(kernel, outs, args, units, scratch=None, in_specs=None):
    if scratch is None:
        scratch = [pltpu.VMEM((4, 12, COLS, C), BF)]
    single = not isinstance(outs, list)
    moved = sum(a.size * a.dtype.itemsize for a in args)
    return pl.pallas_call(
        kernel,
        out_shape=outs,
        in_specs=in_specs or [VM] * len(args),
        out_specs=VM if single else [VM] * len(outs),
        scratch_shapes=scratch,
        compiler_params=pltpu.CompilerParams(vmem_limit_bytes=40 << 20),
        cost_estimate=pl.CostEstimate(
            flops=units * COLS * 27 * C * C * 3, bytes_accessed=moved, transcendentals=0
        ),
        name=kernel.__name__,
    )(*args)


def in_hbm(x):
    return pltpu.with_memory_space_constraint(x, pltpu.HBM)


def on_device(pixel_cot, frame_group, advantage, block_in, conv1_weight, conv2_weight, owner_map):
    times, strips = lax.axis_size("tm"), lax.axis_size("space")

    inner_pairs = [(s, s ^ 1) for s in range(strips)]
    outer_pairs = [(s, (s + 1 if s % 2 else s - 1) % strips) for s in range(strips)]
    later = [((t + 1) % times, t) for t in range(times)]
    sooner = [(t, (t + 1) % times) for t in range(times)]

    def swap_in(x):
        return lax.ppermute(x, "space", inner_pairs)

    def swap_out(x):
        return lax.ppermute(x, "space", outer_pairs)

    def from_later(x):
        return lax.ppermute(x, "tm", later)

    def from_sooner(x):
        return lax.ppermute(x, "tm", sooner)

    w1, w2 = conv1_weight, conv2_weight
    bi = block_in
    ext = pltpu.VMEM((4, 12, COLS, C), BF)

    v0, rin, rout = run(
        start_kernel,
        [field(4, 8), field(3, 4, 2), field(3, 4, 2)],
        tuple(in_hbm(x) for x in (pixel_cot, bi, frame_group, advantage)),
        1,
        scratch=[
            pltpu.VMEM((4, 8, COLS, C), BF),
            pltpu.SMEM(frame_group.shape, jnp.int32),
            pltpu.SMEM(advantage.shape, F32),
            pltpu.SemaphoreType.DMA((10,)),
        ],
        in_specs=[pl.BlockSpec(memory_space=pltpu.HBM)] * 4,
    )
    rin, rout = swap_in(rin), swap_out(rout)
    v0x, b1x = run(extend_kernel, [field(2, 10), field(2, 12)], (v0, bi, rin, rout), 1, scratch=[])
    b1x = from_sooner(b1x)
    v0x = from_later(v0x)
    ga, d1, d0, b0x = run(
        early_kernel,
        [field(2, 10, dtype=F32), field(2, 8, dtype=F32), field(2, 8, dtype=F32), field(2, 12)],
        (v0, bi, rin, rout, w2, in_hbm(w1)),
        52,
        scratch=[ext, ext, ext, pltpu.VMEM(w1.shape, BF), pltpu.SemaphoreType.DMA],
        in_specs=[VM] * 5 + [pl.BlockSpec(memory_space=pltpu.HBM)],
    )
    b0x = from_sooner(b0x)
    v1x = run(pre01_kernel, field(2, 10), (bi, rin, rout, b1x, ga, w1), 20)
    v1xr = from_later(v1x)
    edges = [field(2, 8), field(4, 2), field(4, 2)]
    v1, ein, eout = run(pre23_kernel, edges, (v0, rin, rout, v0x, d1, v1x, w2), 16)
    r1in, r1out = swap_in(ein), swap_out(eout)
    d0a = run(factor01_kernel, field(2, 10, dtype=F32), (bi, rin, rout, b0x, w1), 20)
    v2x = run(
        up01_kernel,
        field(2, 10),
        (v1x, v1, r1in, r1out, v0, rin, rout, w1),
        20,
        scratch=[ext, pltpu.VMEM((2, 12, COLS, C), BF)],
    )
    v2xr = from_later(v2x)
    v2, ein, eout = run(up23_kernel, edges, (v1, r1in, r1out, v1xr, v0, v2x, w1), 16)
    r2in, r2out = swap_in(ein), swap_out(eout)
    v3x = run(grad01_kernel, field(2, 10), (v2x, v2, r2in, r2out, d0a, w2), 20)
    v3xr = from_later(v3x)
    v3, ein, eout = run(grad23_kernel, edges, (v2, r2in, r2out, v2xr, d0, v3x, w2), 16)
    r3in, r3out = swap_in(ein), swap_out(eout)
    pool, part = run(
        last01_kernel,
        [field(2, 4, dtype=F32), field(2, 8, dtype=F32)],
        (v3x, v3, r3in, r3out, v2x, v2, w1),
        24,
    )
    owner = owner_map.reshape(-1, 1)
    units = owner.shape[0]
    capacity = max(2, 2 * units // strips)
    outgoing = run(
        last23_kernel,
        jax.ShapeDtypeStruct((strips, capacity, 8 * C), BF),
        (v3xr, pool, part, owner, w1),
        8,
        scratch=[ext, pltpu.VMEM((4 * 4 * COLS, C), F32)],
    )
    arrived = lax.all_to_all(outgoing, "space", split_axis=0, concat_axis=0, tiled=True)
    return arrived.reshape(1, 1, strips, capacity, 8 * C)


def solution(mesh):
    in_specs = (
        P("tm", "space", None, None),
        P("tm"),
        P(),
        P(None, "tm", "space", None, None),
        P(),
        P(),
        P("tm", "space", None, None),
    )
    out_specs = P("tm", "space", None, None, None)
    return jax.shard_map(
        on_device, mesh=mesh, in_specs=in_specs, out_specs=out_specs, check_vma=False
    )
```

time: 98.2 us -> 82.7 us (0.84)
  the two profiles are of different devices: /device:TPU:7 before, /device:TPU:1 now
where the time goes in v1:
time: 82.7 us; the launch traced here: 82.5 us
  starting transfers between devices  23.1 us (28%)
  Pallas kernels  21.5 us (26%)
  blocking collectives  18 us (22%)
  waiting for transfers between devices  16.3 us (20%)
  local copies, waits for them, and re-layouts  3.42 us (4%)
    pallas_call x12, Pallas kernels, run(): pl.pallas_call(kernel, out_shape=outs, in_specs=in_specs or [VM] * len(ar...  21.5 us
    all_to_all x1, blocking collectives, on_device(): lax.all_to_all(outgoing, 'space', split_axis=0, concat_axis=0, tiled=True)  18 us
    ppermute x4, waiting for transfers between devices, swap_out(): return lax.ppermute(x, 'space', outer_pairs)  14.8 us
    ppermute x4, starting transfers between devices, swap_in(): return lax.ppermute(x, 'space', inner_pairs)  14.6 us
    ppermute x4, starting transfers between devices, from_later(): return lax.ppermute(x, 'tm', later)  4.42 us
    unnamed x17, local copies, waits for them, and re-layouts  3.32 us
    ppermute x4, starting transfers between devices, swap_out(): return lax.ppermute(x, 'space', outer_pairs)  2.23 us
    ppermute x2, starting transfers between devices, from_sooner(): return lax.ppermute(x, 'tm', sooner)  1.85 us
  transfers between devices with their start and end apart: 14, of which 7 were waited for; matrix products, arithmetic and copies ran while one was open for 0% of the time, Pallas kernels for 23%

profile of v1, /device:TPU:1, one launch (start us, length us, event | category | flops | bytes accessed | tf_op | source)
XLA Modules:
  0.0 82.5 jit_solution(13797621960490315929)
XLA Ops:
  0.0 1.5 %start_kernel.1 = (bf16[4,8,64,128]{3,2,1,0:T(8,128)(2,1)S(1)}, bf16[3,4,2,64,128]{4,3,2,1,0:T(8,128)(2,1)S(1)}, bf16[3,4,2,64,128]{4,3,2,1,0:T(8,128)(2,1)S(1)}) custom-call(bf16[4,8,64,128]{3,2,1,0:T(8,128)(2,1)} %cot.1, bf16[2,4,8,64,128]{4,3,2,1,0:T(8,128)(2,1)} %bi.9, s32[4]{0:T(128)} %group.1, f32[4]{0:T(128)} %adv.1), custom_call_target="tpu_custom_call" | custom-call | flops 84934656 | bytes 1572896 | tf_op jit(solution)/shard_map/start_kernel/pallas_call | solution.py:286
  1.5 1.5 %collective-permute-start = (bf16[3,4,2,64,128]{4,3,2,1,0:T(8,128)(2,1)S(1)}, bf16[3,4,2,64,128]{4,3,2,1,0:T(8,128)(2,1)S(1)}, u32[]{:S(2)}, u32[]{:S(2)}) collective-permute-start(bf16[3,4,2,64,128]{4,3,2,1,0:T(8,128)(2,1)S(1)} %get-tuple-element.25), channel_id=1, source_target_pairs={{0,1},{1,0},{2,3},{3,2},{4,5},{5,4},{6,7},{7,6},{8,9},{9,8},{10,11... | collective-permute-start | bytes 1179656 | tf_op jit(solution)/shard_map/ppermute | solution.py:313
  3.0 1.7 %collective-permute-start.1 = (bf16[3,4,2,64,128]{4,3,2,1,0:T(8,128)(2,1)S(1)}, bf16[3,4,2,64,128]{4,3,2,1,0:T(8,128)(2,1)S(1)}, u32[]{:S(2)}, u32[]{:S(2)}) collective-permute-start(bf16[3,4,2,64,128]{4,3,2,1,0:T(8,128)(2,1)S(1)} %get-tuple-element.26), channel_id=1, source_target_pairs={{0,31},{1,2},{2,1},{3,4},{4,3},{5,6},{6,5},{7,8},{8,7},{9,10},{10,... | collective-permute-start | bytes 1179656 | tf_op jit(solution)/shard_map/ppermute | solution.py:316
  4.7 0.0 collective-permute-done.rin.r0in
  4.7 5.5 %collective-permute-done.1.rout.r0out = bf16[3,4,2,64,128]{4,3,2,1,0:T(8,128)(2,1)S(1)} collective-permute-done((bf16[3,4,2,64,128]{4,3,2,1,0:T(8,128)(2,1)S(1)}, bf16[3,4,2,64,128]{4,3,2,1,0:T(8,128)(2,1)S(1)}, u32[]{:S(2)}, u32[]{:S(2)}) %collective-permute-start.1) | collective-permute-done | bytes 393248 | tf_op jit(solution)/shard_map/ppermute | solution.py:316
  10.2 0.1 extend_kernel.1
  10.3 1.7 %collective-permute-start.2 = (bf16[2,12,64,128]{3,2,1,0:T(8,128)(2,1)S(1)}, bf16[2,12,64,128]{3,2,1,0:T(8,128)(2,1)S(1)}, u32[]{:S(2)}, u32[]{:S(2)}) collective-permute-start(bf16[2,12,64,128]{3,2,1,0:T(8,128)(2,1)S(1)} %get-tuple-element.28), channel_id=1, source_target_pairs={{0,32},{32,64},{64,96},{96,0},{1,33},{33,65},{65,97},{97,1},{2,34}... | collective-permute-start | bytes 1179656 | tf_op jit(solution)/shard_map/ppermute | solution.py:322
  12.0 1.4 %collective-permute-start.3 = (bf16[2,10,64,128]{3,2,1,0:T(8,128)(2,1)S(1)}, bf16[2,10,64,128]{3,2,1,0:T(8,128)(2,1)S(1)}, u32[]{:S(2)}, u32[]{:S(2)}) collective-permute-start(bf16[2,10,64,128]{3,2,1,0:T(8,128)(2,1)S(1)} %get-tuple-element.30), channel_id=1, source_target_pairs={{32,0},{64,32},{96,64},{0,96},{33,1},{65,33},{97,65},{1,97},{34,2}... | collective-permute-start | bytes 983048 | tf_op jit(solution)/shard_map/ppermute | solution.py:319
  13.3 0.0 copy-done.2
  13.3 4.8 %early_kernel.1 = (f32[2,10,64,128]{3,2,1,0:T(8,128)S(1)}, f32[2,8,64,128]{3,2,1,0:T(8,128)S(1)}, f32[2,8,64,128]{3,2,1,0:T(8,128)S(1)}, bf16[2,12,64,128]{3,2,1,0:T(8,128)(2,1)S(1)}) custom-call(bf16[4,8,64,128]{3,2,1,0:T(8,128)(2,1)S(1)} %get-tuple-element.27.v0, bf16[2,4,8,64,128]{4,3,2,1,0:T(8,128)(2,1)S(1)} %copy-done, ...), custom_call_target="tpu_custom_call" | custom-call | flops 4416602112 | bytes 5898240 | tf_op jit(solution)/shard_map/early_kernel/pallas_call | solution.py:286
  18.1 0.3 collective-permute-done.2.bx
  18.4 1.9 %pre01_kernel.1.v1x = bf16[2,10,64,128]{3,2,1,0:T(8,128)(2,1)S(1)} custom-call(bf16[2,4,8,64,128]{4,3,2,1,0:T(8,128)(2,1)S(1)} %copy-done, bf16[3,4,2,64,128]{4,3,2,1,0:T(8,128)(2,1)S(1)} %collective-permute-done.rin.r0in, bf16[3,4,2,64,128]{4,3,2,1,0:T(8,128)(2,1)S(1)} %collective-permute-done.1.rout.r0out, ...), custom_call_target="tpu_custom_call" | custom-call | flops 1698693120 | bytes 4653056 | tf_op jit(solution)/shard_map/pre01_kernel/pallas_call | solution.py:286
  20.3 1.5 %collective-permute-start.6 = (bf16[2,10,64,128]{3,2,1,0:T(8,128)(2,1)S(1)}, bf16[2,10,64,128]{3,2,1,0:T(8,128)(2,1)S(1)}, u32[]{:S(2)}, u32[]{:S(2)}) collective-permute-start(bf16[2,10,64,128]{3,2,1,0:T(8,128)(2,1)S(1)} %pre01_kernel.1.v1x), channel_id=1, source_target_pairs={{32,0},{64,32},{96,64},{0,96},{33,1},{65,33},{97,65},{1,97},{34,2}... | collective-permute-start | bytes 983048 | tf_op jit(solution)/shard_map/ppermute | solution.py:319
  21.8 0.0 collective-permute-done.3.vx
  21.8 1.5 %pre23_kernel.1 = (bf16[2,8,64,128]{3,2,1,0:T(8,128)(2,1)S(1)}, bf16[4,2,64,128]{3,2,1,0:T(8,128)(2,1)S(1)}, bf16[4,2,64,128]{3,2,1,0:T(8,128)(2,1)S(1)}) custom-call(bf16[4,8,64,128]{3,2,1,0:T(8,128)(2,1)S(1)} %get-tuple-element.27.v0, bf16[3,4,2,64,128]{4,3,2,1,0:T(8,128)(2,1)S(1)} %collective-permute-done.rin.r0in, ...), custom_call_target="tpu_custom_call" | custom-call | flops 1358954496 | bytes 4259840 | tf_op jit(solution)/shard_map/pre23_kernel/pallas_call | solution.py:286
  23.3 6.1 %collective-permute-start.4 = (bf16[4,2,64,128]{3,2,1,0:T(8,128)(2,1)S(1)}, bf16[4,2,64,128]{3,2,1,0:T(8,128)(2,1)S(1)}, u32[]{:S(2)}, u32[]{:S(2)}) collective-permute-start(bf16[4,2,64,128]{3,2,1,0:T(8,128)(2,1)S(1)} %get-tuple-element.33), channel_id=1, source_target_pairs={{0,1},{1,0},{2,3},{3,2},{4,5},{5,4},{6,7},{7,6},{8,9},{9,8},{10,11... | collective-permute-start | bytes 393224 | tf_op jit(solution)/shard_map/ppermute | solution.py:313
  29.4 0.5 collective-permute-start.5
  29.9 0.2 collective-permute-start.9
  30.1 0.3 collective-permute-done.4.rin
  30.4 3.4 %collective-permute-done.5.rout = bf16[4,2,64,128]{3,2,1,0:T(8,128)(2,1)S(1)} collective-permute-done((bf16[4,2,64,128]{3,2,1,0:T(8,128)(2,1)S(1)}, bf16[4,2,64,128]{3,2,1,0:T(8,128)(2,1)S(1)}, u32[]{:S(2)}, u32[]{:S(2)}) %collective-permute-start.5) | collective-permute-done | bytes 131104 | tf_op jit(solution)/shard_map/ppermute | solution.py:316
  33.8 1.8 %up01_kernel.1.v2x = bf16[2,10,64,128]{3,2,1,0:T(8,128)(2,1)S(1)} custom-call(bf16[2,10,64,128]{3,2,1,0:T(8,128)(2,1)S(1)} %pre01_kernel.1.v1x, bf16[2,8,64,128]{3,2,1,0:T(8,128)(2,1)S(1)} %get-tuple-element.32.v1, bf16[4,2,64,128]{3,2,1,0:T(8,128)(2,1)S(1)} %collective-permute-done.4.rin, bf16[4,2,64,128]{3,2,1,0:T(8,128)(2,1)S(1)} %collective-permute-done.5.rout, ...), custom_call_target="tpu_custom_call" | custom-call | flops 1698693120 | bytes 3932160 | tf_op jit(solution)/shard_map/up01_kernel/pallas_call | solution.py:286
  35.6 0.9 %collective-permute-start.11 = (bf16[2,10,64,128]{3,2,1,0:T(8,128)(2,1)S(1)}, bf16[2,10,64,128]{3,2,1,0:T(8,128)(2,1)S(1)}, u32[]{:S(2)}, u32[]{:S(2)}) collective-permute-start(bf16[2,10,64,128]{3,2,1,0:T(8,128)(2,1)S(1)} %up01_kernel.1.v2x), channel_id=1, source_target_pairs={{32,0},{64,32},{96,64},{0,96},{33,1},{65,33},{97,65},{1,97},{34,2}... | collective-permute-start | bytes 983048 | tf_op jit(solution)/shard_map/ppermute | solution.py:319
  36.5 0.0 collective-permute-done.6.vxr
  36.5 1.5 %up23_kernel.1 = (bf16[2,8,64,128]{3,2,1,0:T(8,128)(2,1)S(1)}, bf16[4,2,64,128]{3,2,1,0:T(8,128)(2,1)S(1)}, bf16[4,2,64,128]{3,2,1,0:T(8,128)(2,1)S(1)}) custom-call(bf16[2,8,64,128]{3,2,1,0:T(8,128)(2,1)S(1)} %get-tuple-element.32.v1, bf16[4,2,64,128]{3,2,1,0:T(8,128)(2,1)S(1)} %collective-permute-done.4.rin, ...), custom_call_target="tpu_custom_call" | custom-call | flops 1358954496 | bytes 3473408 | tf_op jit(solution)/shard_map/up23_kernel/pallas_call | solution.py:286
  38.0 3.7 %collective-permute-start.7 = (bf16[4,2,64,128]{3,2,1,0:T(8,128)(2,1)S(1)}, bf16[4,2,64,128]{3,2,1,0:T(8,128)(2,1)S(1)}, u32[]{:S(2)}, u32[]{:S(2)}) collective-permute-start(bf16[4,2,64,128]{3,2,1,0:T(8,128)(2,1)S(1)} %get-tuple-element.36), channel_id=1, source_target_pairs={{0,1},{1,0},{2,3},{3,2},{4,5},{5,4},{6,7},{7,6},{8,9},{9,8},{10,11... | collective-permute-start | bytes 393224 | tf_op jit(solution)/shard_map/ppermute | solution.py:313
  41.7 0.0 collective-permute-start.8
  41.7 0.0 collective-permute-done.9.bx
  41.7 1.8 %factor01_kernel.1.d = f32[2,10,64,128]{3,2,1,0:T(8,128)S(1)} custom-call(bf16[2,4,8,64,128]{4,3,2,1,0:T(8,128)(2,1)S(1)} %copy-done, bf16[3,4,2,64,128]{4,3,2,1,0:T(8,128)(2,1)S(1)} %collective-permute-done.rin.r0in, bf16[3,4,2,64,128]{4,3,2,1,0:T(8,128)(2,1)S(1)} %collective-permute-done.1.rout.r0out, ...), custom_call_target="tpu_custom_call" | custom-call | flops 1698693120 | bytes 3997696 | tf_op jit(solution)/shard_map/factor01_kernel/pallas_call | solution.py:286
  43.6 0.0 collective-permute-done.7.rin
  43.6 2.5 %collective-permute-done.8.rout = bf16[4,2,64,128]{3,2,1,0:T(8,128)(2,1)S(1)} collective-permute-done((bf16[4,2,64,128]{3,2,1,0:T(8,128)(2,1)S(1)}, bf16[4,2,64,128]{3,2,1,0:T(8,128)(2,1)S(1)}, u32[]{:S(2)}, u32[]{:S(2)}) %collective-permute-start.8) | collective-permute-done | bytes 131104 | tf_op jit(solution)/shard_map/ppermute | solution.py:316
  46.1 1.8 %grad01_kernel.1.v3x = bf16[2,10,64,128]{3,2,1,0:T(8,128)(2,1)S(1)} custom-call(bf16[2,10,64,128]{3,2,1,0:T(8,128)(2,1)S(1)} %up01_kernel.1.v2x, bf16[2,8,64,128]{3,2,1,0:T(8,128)(2,1)S(1)} %get-tuple-element.35.v2, bf16[4,2,64,128]{3,2,1,0:T(8,128)(2,1)S(1)} %collective-permute-done.7.rin, bf16[4,2,64,128]{3,2,1,0:T(8,128)(2,1)S(1)} %collective-permute-done.8.rout, ...), custom_call_target="tpu_custom_call" | custom-call | flops 1698693120 | bytes 3276800 | tf_op jit(solution)/shard_map/grad01_kernel/pallas_call | solution.py:286
  47.9 0.6 collective-permute-start.10
  48.5 0.0 collective-permute-done.11.vxr
  48.5 0.0 copy-done.3
  48.5 1.5 %grad23_kernel.1 = (bf16[2,8,64,128]{3,2,1,0:T(8,128)(2,1)S(1)}, bf16[4,2,64,128]{3,2,1,0:T(8,128)(2,1)S(1)}, bf16[4,2,64,128]{3,2,1,0:T(8,128)(2,1)S(1)}) custom-call(bf16[2,8,64,128]{3,2,1,0:T(8,128)(2,1)S(1)} %get-tuple-element.35.v2, bf16[4,2,64,128]{3,2,1,0:T(8,128)(2,1)S(1)} %collective-permute-done.7.rin, ...), custom_call_target="tpu_custom_call" | custom-call | flops 1358954496 | bytes 3473408 | tf_op jit(solution)/shard_map/grad23_kernel/pallas_call | solution.py:286
  50.1 0.7 copy-done.5
  50.8 3.4 %collective-permute-start.12 = (bf16[4,2,64,128]{3,2,1,0:T(8,128)(2,1)S(1)}, bf16[4,2,64,128]{3,2,1,0:T(8,128)(2,1)S(1)}, u32[]{:S(2)}, u32[]{:S(2)}) collective-permute-start(bf16[4,2,64,128]{3,2,1,0:T(8,128)(2,1)S(1)} %get-tuple-element.41), channel_id=1, source_target_pairs={{0,1},{1,0},{2,3},{3,2},{4,5},{5,4},{6,7},{7,6},{8,9},{9,8},{10,11... | collective-permute-start | bytes 393224 | tf_op jit(solution)/shard_map/ppermute | solution.py:313
  54.2 0.0 collective-permute-start.13
  54.2 0.1 copy.8.owner
  54.3 0.9 %collective-permute-done.12.rin = bf16[4,2,64,128]{3,2,1,0:T(8,128)(2,1)S(1)} collective-permute-done((bf16[4,2,64,128]{3,2,1,0:T(8,128)(2,1)S(1)}, bf16[4,2,64,128]{3,2,1,0:T(8,128)(2,1)S(1)}, u32[]{:S(2)}, u32[]{:S(2)}) %collective-permute-start.12) | collective-permute-done | bytes 131104 | tf_op jit(solution)/shard_map/ppermute | solution.py:313
  55.1 3.4 %collective-permute-done.13.rout = bf16[4,2,64,128]{3,2,1,0:T(8,128)(2,1)S(1)} collective-permute-done((bf16[4,2,64,128]{3,2,1,0:T(8,128)(2,1)S(1)}, bf16[4,2,64,128]{3,2,1,0:T(8,128)(2,1)S(1)}, u32[]{:S(2)}, u32[]{:S(2)}) %collective-permute-start.13) | collective-permute-done | bytes 131104 | tf_op jit(solution)/shard_map/ppermute | solution.py:316
  58.6 0.9 %copy-done.4 = bf16[2,8,64,128]{3,2,1,0:T(8,128)(2,1)S(1)} copy-done((bf16[2,8,64,128]{3,2,1,0:T(8,128)(2,1)S(1)}, bf16[2,8,64,128]{3,2,1,0:T(8,128)(2,1)}, u32[]{:S(2)}) %copy-start.4) | copy-done | bytes 262168
  59.5 0.9 %copy-done.6 = bf16[2,8,64,128]{3,2,1,0:T(8,128)(2,1)S(1)} copy-done((bf16[2,8,64,128]{3,2,1,0:T(8,128)(2,1)S(1)}, bf16[2,8,64,128]{3,2,1,0:T(8,128)(2,1)}, u32[]{:S(2)}) %copy-start.6) | copy-done | bytes 262168
  60.5 2.1 %last01_kernel.1 = (f32[2,4,64,128]{3,2,1,0:T(8,128)S(1)}, f32[2,8,64,128]{3,2,1,0:T(8,128)S(1)}) custom-call(bf16[2,10,64,128]{3,2,1,0:T(8,128)(2,1)S(1)} %grad01_kernel.1.v3x, bf16[2,8,64,128]{3,2,1,0:T(8,128)(2,1)S(1)} %copy-done.6, bf16[4,2,64,128]{3,2,1,0:T(8,128)(2,1)S(1)} %collective-permute-done.12.rin, ...), custom_call_target="tpu_custom_call" | custom-call | flops 2038431744 | bytes 3211264 | tf_op jit(solution)/shard_map/last01_kernel/pallas_call | solution.py:286
  62.6 0.0 collective-permute-done.10.vxr
  62.6 1.1 %last23_kernel.1 = bf16[32,4,1024]{2,1,0:T(4,128)(2,1)S(1)} custom-call(bf16[2,10,64,128]{3,2,1,0:T(8,128)(2,1)S(1)} %collective-permute-done.10.vxr, f32[2,4,64,128]{3,2,1,0:T(8,128)S(1)} %get-tuple-element.43.pool, f32[2,8,64,128]{3,2,1,0:T(8,128)S(1)} %get-tuple-element.44.part, s32[64,1]{1,0:T(8,128)S(1)} %copy.8.owner, ...), custom_call_target="tpu_custom_call" | custom-call | flops 679477248 | bytes 2883840 | tf_op jit(solution)/shard_map/last23_kernel/pallas_call | solution.py:286
  63.8 18.0 %all_to_all.5 = bf16[32,4,1024]{2,1,0:T(4,128)(2,1)S(1)} all-to-all(bf16[32,4,1024]{2,1,0:T(4,128)(2,1)S(1)} %last23_kernel.1), channel_id=1, replica_groups=mesh['tm'=4,'space'=32] {'space'}, dimensions={0} | all-to-all | bytes 524288 | tf_op jit(solution)/shard_map/all_to_all | solution.py:390
  81.8 0.7 copy.10
  (11 shorter events, 0.0 us)
Async XLA Ops:
  0.0 10.2 %copy-start = (bf16[2,4,8,64,128]{4,3,2,1,0:T(8,128)(2,1)S(1)}, bf16[2,4,8,64,128]{4,3,2,1,0:T(8,128)(2,1)}, u32[]{:S(2)}) copy-start(bf16[2,4,8,64,128]{4,3,2,1,0:T(8,128)(2,1)} %bi.9) | copy-start | bytes 3145732
  0.0 13.3 %copy-start.2 = (bf16[2,3,3,3,128,128]{5,4,3,2,1,0:T(8,128)(2,1)S(1)}, bf16[2,3,3,3,128,128]{5,4,3,2,1,0:T(8,128)(2,1)}, u32[]{:S(2)}) copy-start(bf16[2,3,3,3,128,128]{5,4,3,2,1,0:T(8,128)(2,1)} %w2.7) | copy-start | bytes 5308420
  1.5 3.2 %collective-permute-start = (bf16[3,4,2,64,128]{4,3,2,1,0:T(8,128)(2,1)S(1)}, bf16[3,4,2,64,128]{4,3,2,1,0:T(8,128)(2,1)S(1)}, u32[]{:S(2)}, u32[]{:S(2)}) collective-permute-start(bf16[3,4,2,64,128]{4,3,2,1,0:T(8,128)(2,1)S(1)} %get-tuple-element.25), channel_id=1, source_target_pairs={{0,1},{1,0},{2,3},{3,2},{4,5},{5,4},{6,7},{7,6},{8,9},{9,8},{10,11... | collective-permute-start | bytes 1179656 | tf_op jit(solution)/shard_map/ppermute | solution.py:313
  3.0 7.2 %collective-permute-start.1 = (bf16[3,4,2,64,128]{4,3,2,1,0:T(8,128)(2,1)S(1)}, bf16[3,4,2,64,128]{4,3,2,1,0:T(8,128)(2,1)S(1)}, u32[]{:S(2)}, u32[]{:S(2)}) collective-permute-start(bf16[3,4,2,64,128]{4,3,2,1,0:T(8,128)(2,1)S(1)} %get-tuple-element.26), channel_id=1, source_target_pairs={{0,31},{1,2},{2,1},{3,4},{4,3},{5,6},{6,5},{7,8},{8,7},{9,10},{10,... | collective-permute-start | bytes 1179656 | tf_op jit(solution)/shard_map/ppermute | solution.py:316
  10.3 8.1 %collective-permute-start.2 = (bf16[2,12,64,128]{3,2,1,0:T(8,128)(2,1)S(1)}, bf16[2,12,64,128]{3,2,1,0:T(8,128)(2,1)S(1)}, u32[]{:S(2)}, u32[]{:S(2)}) collective-permute-start(bf16[2,12,64,128]{3,2,1,0:T(8,128)(2,1)S(1)} %get-tuple-element.28), channel_id=1, source_target_pairs={{0,32},{32,64},{64,96},{96,0},{1,33},{33,65},{65,97},{97,1},{2,34}... | collective-permute-start | bytes 1179656 | tf_op jit(solution)/shard_map/ppermute | solution.py:322
  12.0 6.4 %copy-start.1 = (bf16[2,3,3,3,128,128]{5,4,3,2,1,0:T(8,128)(2,1)S(1)}, bf16[2,3,3,3,128,128]{5,4,3,2,1,0:T(8,128)(2,1)}, u32[]{:S(2)}) copy-start(bf16[2,3,3,3,128,128]{5,4,3,2,1,0:T(8,128)(2,1)} %w1.11) | copy-start | bytes 5308420
  12.0 9.8 %collective-permute-start.3 = (bf16[2,10,64,128]{3,2,1,0:T(8,128)(2,1)S(1)}, bf16[2,10,64,128]{3,2,1,0:T(8,128)(2,1)S(1)}, u32[]{:S(2)}, u32[]{:S(2)}) collective-permute-start(bf16[2,10,64,128]{3,2,1,0:T(8,128)(2,1)S(1)} %get-tuple-element.30), channel_id=1, source_target_pairs={{32,0},{64,32},{96,64},{0,96},{33,1},{65,33},{97,65},{1,97},{34,2}... | collective-permute-start | bytes 983048 | tf_op jit(solution)/shard_map/ppermute | solution.py:319
  20.3 16.2 %collective-permute-start.6 = (bf16[2,10,64,128]{3,2,1,0:T(8,128)(2,1)S(1)}, bf16[2,10,64,128]{3,2,1,0:T(8,128)(2,1)S(1)}, u32[]{:S(2)}, u32[]{:S(2)}) collective-permute-start(bf16[2,10,64,128]{3,2,1,0:T(8,128)(2,1)S(1)} %pre01_kernel.1.v1x), channel_id=1, source_target_pairs={{32,0},{64,32},{96,64},{0,96},{33,1},{65,33},{97,65},{1,97},{34,2}... | collective-permute-start | bytes 983048 | tf_op jit(solution)/shard_map/ppermute | solution.py:319
  23.3 7.1 %collective-permute-start.4 = (bf16[4,2,64,128]{3,2,1,0:T(8,128)(2,1)S(1)}, bf16[4,2,64,128]{3,2,1,0:T(8,128)(2,1)S(1)}, u32[]{:S(2)}, u32[]{:S(2)}) collective-permute-start(bf16[4,2,64,128]{3,2,1,0:T(8,128)(2,1)S(1)} %get-tuple-element.33), channel_id=1, source_target_pairs={{0,1},{1,0},{2,3},{3,2},{4,5},{5,4},{6,7},{7,6},{8,9},{9,8},{10,11... | collective-permute-start | bytes 393224 | tf_op jit(solution)/shard_map/ppermute | solution.py:313
  29.4 4.4 %collective-permute-start.5 = (bf16[4,2,64,128]{3,2,1,0:T(8,128)(2,1)S(1)}, bf16[4,2,64,128]{3,2,1,0:T(8,128)(2,1)S(1)}, u32[]{:S(2)}, u32[]{:S(2)}) collective-permute-start(bf16[4,2,64,128]{3,2,1,0:T(8,128)(2,1)S(1)} %get-tuple-element.34), channel_id=1, source_target_pairs={{0,31},{1,2},{2,1},{3,4},{4,3},{5,6},{6,5},{7,8},{8,7},{9,10},{10,... | collective-permute-start | bytes 393224 | tf_op jit(solution)/shard_map/ppermute | solution.py:316
  29.9 11.8 %collective-permute-start.9 = (bf16[2,12,64,128]{3,2,1,0:T(8,128)(2,1)S(1)}, bf16[2,12,64,128]{3,2,1,0:T(8,128)(2,1)S(1)}, u32[]{:S(2)}, u32[]{:S(2)}) collective-permute-start(bf16[2,12,64,128]{3,2,1,0:T(8,128)(2,1)S(1)} %get-tuple-element.38), channel_id=1, source_target_pairs={{0,32},{32,64},{64,96},{96,0},{1,33},{33,65},{65,97},{97,1},{2,34}... | collective-permute-start | bytes 1179656 | tf_op jit(solution)/shard_map/ppermute | solution.py:322
  35.6 12.9 %collective-permute-start.11 = (bf16[2,10,64,128]{3,2,1,0:T(8,128)(2,1)S(1)}, bf16[2,10,64,128]{3,2,1,0:T(8,128)(2,1)S(1)}, u32[]{:S(2)}, u32[]{:S(2)}) collective-permute-start(bf16[2,10,64,128]{3,2,1,0:T(8,128)(2,1)S(1)} %up01_kernel.1.v2x), channel_id=1, source_target_pairs={{32,0},{64,32},{96,64},{0,96},{33,1},{65,33},{97,65},{1,97},{34,2}... | collective-permute-start | bytes 983048 | tf_op jit(solution)/shard_map/ppermute | solution.py:319
  38.0 10.5 %copy-start.3 = (bf16[2,8,64,128]{3,2,1,0:T(8,128)(2,1)}, bf16[2,8,64,128]{3,2,1,0:T(8,128)(2,1)S(1)}, u32[]{:S(2)}) copy-start(bf16[2,8,64,128]{3,2,1,0:T(8,128)(2,1)S(1)} %get-tuple-element.35.v2) | copy-start | bytes 786436
  38.0 5.5 %collective-permute-start.7 = (bf16[4,2,64,128]{3,2,1,0:T(8,128)(2,1)S(1)}, bf16[4,2,64,128]{3,2,1,0:T(8,128)(2,1)S(1)}, u32[]{:S(2)}, u32[]{:S(2)}) collective-permute-start(bf16[4,2,64,128]{3,2,1,0:T(8,128)(2,1)S(1)} %get-tuple-element.36), channel_id=1, source_target_pairs={{0,1},{1,0},{2,3},{3,2},{4,5},{5,4},{6,7},{7,6},{8,9},{9,8},{10,11... | collective-permute-start | bytes 393224 | tf_op jit(solution)/shard_map/ppermute | solution.py:313
  41.7 4.4 %collective-permute-start.8 = (bf16[4,2,64,128]{3,2,1,0:T(8,128)(2,1)S(1)}, bf16[4,2,64,128]{3,2,1,0:T(8,128)(2,1)S(1)}, u32[]{:S(2)}, u32[]{:S(2)}) collective-permute-start(bf16[4,2,64,128]{3,2,1,0:T(8,128)(2,1)S(1)} %get-tuple-element.37), channel_id=1, source_target_pairs={{0,31},{1,2},{2,1},{3,4},{4,3},{5,6},{6,5},{7,8},{8,7},{9,10},{10,... | collective-permute-start | bytes 393224 | tf_op jit(solution)/shard_map/ppermute | solution.py:316
  47.9 14.7 %collective-permute-start.10 = (bf16[2,10,64,128]{3,2,1,0:T(8,128)(2,1)S(1)}, bf16[2,10,64,128]{3,2,1,0:T(8,128)(2,1)S(1)}, u32[]{:S(2)}, u32[]{:S(2)}) collective-permute-start(bf16[2,10,64,128]{3,2,1,0:T(8,128)(2,1)S(1)} %grad01_kernel.1.v3x), channel_id=1, source_target_pairs={{32,0},{64,32},{96,64},{0,96},{33,1},{65,33},{97,65},{1,97},{34,2}... | collective-permute-start | bytes 983048 | tf_op jit(solution)/shard_map/ppermute | solution.py:319
  48.5 5.6 %copy-start.7 = (s32[1,1,64,1]{2,3,1,0:T(1,128)S(1)}, s32[1,1,64,1]{2,3,1,0:T(1,128)}, u32[]{:S(2)}) copy-start(s32[1,1,64,1]{2,3,1,0:T(1,128)} %param.13) | copy-start | bytes 772
  50.1 0.7 copy-start.5
  50.8 4.4 %collective-permute-start.12 = (bf16[4,2,64,128]{3,2,1,0:T(8,128)(2,1)S(1)}, bf16[4,2,64,128]{3,2,1,0:T(8,128)(2,1)S(1)}, u32[]{:S(2)}, u32[]{:S(2)}) collective-permute-start(bf16[4,2,64,128]{3,2,1,0:T(8,128)(2,1)S(1)} %get-tuple-element.41), channel_id=1, source_target_pairs={{0,1},{1,0},{2,3},{3,2},{4,5},{5,4},{6,7},{7,6},{8,9},{9,8},{10,11... | collective-permute-start | bytes 393224 | tf_op jit(solution)/shard_map/ppermute | solution.py:313
  54.2 4.4 %collective-permute-start.13 = (bf16[4,2,64,128]{3,2,1,0:T(8,128)(2,1)S(1)}, bf16[4,2,64,128]{3,2,1,0:T(8,128)(2,1)S(1)}, u32[]{:S(2)}, u32[]{:S(2)}) collective-permute-start(bf16[4,2,64,128]{3,2,1,0:T(8,128)(2,1)S(1)} %get-tuple-element.42), channel_id=1, source_target_pairs={{0,31},{1,2},{2,1},{3,4},{4,3},{5,6},{6,5},{7,8},{8,7},{9,10},{10,... | collective-permute-start | bytes 393224 | tf_op jit(solution)/shard_map/ppermute | solution.py:316
  58.5 1.0 %copy-start.4 = (bf16[2,8,64,128]{3,2,1,0:T(8,128)(2,1)S(1)}, bf16[2,8,64,128]{3,2,1,0:T(8,128)(2,1)}, u32[]{:S(2)}) copy-start(bf16[2,8,64,128]{3,2,1,0:T(8,128)(2,1)} %copy-done.3) | copy-start | bytes 786436
  59.5 0.9 %copy-start.6 = (bf16[2,8,64,128]{3,2,1,0:T(8,128)(2,1)S(1)}, bf16[2,8,64,128]{3,2,1,0:T(8,128)(2,1)}, u32[]{:S(2)}) copy-start(bf16[2,8,64,128]{3,2,1,0:T(8,128)(2,1)} %copy-done.5) | copy-start | bytes 786436

commit v2 on v1

--- a/solution.py
+++ b/solution.py
@@ -34,7 +34,7 @@
     )
 
 
-def conv_back(ext, w, layer, t, r0, nr, steps=(0, 1, 2)):
+def back_taps(lhs, w, layer, steps=(0, 1, 2)):
     rhs = jnp.concatenate(
         [
             jnp.concatenate([w[layer, 2 - dt, 2 - dr, 2 - j] for j in range(3)], axis=0)
@@ -43,25 +43,25 @@
         ],
         axis=1,
     )
-    out = lax.dot_general(
-        patches(ext, t, r0, nr, steps),
-        rhs,
-        (((1,), (1,)), ((), ())),
-        preferred_element_type=F32,
-    )
-    return shift_add(out).reshape(nr, COLS, C)
-
-
-def conv_fore(ext, w, layer, t, r0, nr):
+    return shift_add(
+        lax.dot_general(lhs, rhs, (((1,), (1,)), ((), ())), preferred_element_type=F32)
+    )
+
+
+def conv_back(ext, w, layer, t, r0, nr, steps=(0, 1, 2)):
+    return back_taps(patches(ext, t, r0, nr, steps), w, layer, steps).reshape(nr, COLS, C)
+
+
+def conv_fore(ext, w, layer, t, r0, nr, steps=(0, 1, 2)):
     rhs = jnp.concatenate(
         [
             jnp.concatenate([w[layer, dt, dr, j] for j in range(3)], axis=1)
-            for dt in range(3)
+            for dt in steps
             for dr in range(3)
         ],
         axis=0,
     )
-    out = jnp.dot(patches(ext, t, r0, nr), rhs, preferred_element_type=F32)
+    out = jnp.dot(patches(ext, t, r0, nr, steps), rhs, preferred_element_type=F32)
     return shift_add(out).reshape(nr, COLS, C)
 
 
@@ -108,7 +108,9 @@
     rout[2:4] = late[:, pl.ds(6 * p, 2)]
 
 
-def start_kernel(cot, bi, group, adv, v0, rin, rout, raw, gs, ads, sem):
+def start_kernel(
+    cot, bi, group, adv, v0, rin, rout, b1s, dpi, dpo, raw, gs, ads, sem
+):
     p = side()
     inner, outer = pl.ds(6 * (1 - p), 2), pl.ds(6 * p, 2)
     copies = [
@@ -116,11 +118,15 @@
         pltpu.make_async_copy(adv, ads, sem.at[1]),
     ]
     copies += [pltpu.make_async_copy(cot.at[t], raw.at[t], sem.at[2 + t]) for t in range(4)]
-    for k in range(2):
-        copies += [
-            pltpu.make_async_copy(bi.at[1 - k, :, inner], rin.at[1 + k], sem.at[6 + 2 * k]),
-            pltpu.make_async_copy(bi.at[1 - k, :, outer], rout.at[1 + k], sem.at[7 + 2 * k]),
-        ]
+    copies += [
+        pltpu.make_async_copy(bi.at[1, pl.ds(2, 2)], b1s, sem.at[6]),
+        pltpu.make_async_copy(bi.at[1, :, inner], rin.at[1], sem.at[7]),
+        pltpu.make_async_copy(bi.at[1, :, outer], rout.at[1], sem.at[8]),
+        pltpu.make_async_copy(bi.at[1, pl.ds(2, 2), inner], dpi, sem.at[9]),
+        pltpu.make_async_copy(bi.at[1, pl.ds(2, 2), outer], dpo, sem.at[10]),
+        pltpu.make_async_copy(bi.at[0, :, inner], rin.at[2], sem.at[11]),
+        pltpu.make_async_copy(bi.at[0, :, outer], rout.at[2], sem.at[12]),
+    ]
     for copy in copies:
         copy.start()
     copies[0].wait()
@@ -135,57 +141,71 @@
         copy.wait()
 
 
-def extend_kernel(v0, bi, rin, rout, vx, bx):
+def extend_kernel(v0, rin, rout, vx):
     p = side()
     for t in range(2):
         vx[t, 1:9] = v0[t]
         vx[t, 9 * (1 - p)] = rin[0, t, p]
         vx[t, 9 * p] = inside(rout[0, t, 1 - p])
-    bx[:, 2:10] = bi[1, 2:4]
-    put_edges(bx, slice(0, 2), rin[1, 2:4], rout[1, 2:4])
-
-
-def early_kernel(v0, bi, rin, rout, w2, w1h, ga, d1, d0, bx, ext, ext1, ext0, w1, sem):
-    weights = pltpu.make_async_copy(w1h, w1, sem)
-    weights.start()
+
+
+def extend0_kernel(bi, rin, rout, after, bx):
+    bx[:, 2:10] = bi[0, 2:4]
+    put_edges(bx, slice(0, 2), rin[2, 2:4], rout[2, 2:4])
+
+
+def early_kernel(v0, bih, rin, rout, w2h, w1h, ga, ga23, d1, pre, ext, ext1, w2, w1, sem):
+    copies = [
+        pltpu.make_async_copy(w2h.at[1], w2.at[1], sem.at[0]),
+        pltpu.make_async_copy(bih.at[1], ext1.at[:, pl.ds(2, 8)], sem.at[1]),
+        pltpu.make_async_copy(w1h.at[1], w1.at[1], sem.at[2]),
+    ]
+    for copy in copies:
+        copy.start()
     ext[:, 2:10] = v0[...]
     put_edges(ext, slice(0, 4), rin[0], rout[0])
-    for k, old in enumerate((ext1, ext0)):
-        old[:, 2:10] = bi[1 - k]
-        put_edges(old, slice(0, 4), rin[1 + k], rout[1 + k])
-    bx[...] = ext0[2:4]
+    copies[0].wait()
     for t in range(2):
         ga[t] = conv_back(ext, w2, 1, t, 0, 10)
-    weights.wait()
-    for k, (old, d) in enumerate(((ext1, d1), (ext0, d0))):
-        for t in range(2):
-            d[t] = factor(conv_fore(old, w1, 1 - k, t, 1, 8))
-
-
-def fore_halo(ext, k, bi, rin, rout, bx):
+    for t, steps in ((0, (0, 1)), (1, (0,))):
+        ga23[t] = conv_back(ext, w2, 1, 2 + t, 1, 8, steps)
+    copies[1].wait()
+    copies[2].wait()
+    put_edges(ext1, slice(0, 4), rin[1], rout[1])
+    for t in range(2):
+        d1[t] = factor(conv_fore(ext1, w1, 1, t, 1, 8))
+    for t, steps in ((0, (2,)), (1, (1, 2))):
+        pre[t] = conv_fore(ext1, w1, 1, t - 2, 0, 10, steps)
+
+
+def pre01_kernel(bx, dpi, dpo, ga, pre, w1, v1x, ext):
+    ext[:, 2:10] = with_sooner(bx[...])
+    put_edges(ext, slice(0, 2), with_sooner(dpi[...]), with_sooner(dpo[...]))
+    for t, steps in ((0, (0, 1)), (1, (0,))):
+        whole = pre[t] + conv_fore(ext, w1, 1, t, 0, 10, steps)
+        store_ten(v1x, t, ga[t] * factor(whole))
+
+
+def factor_kernel(bi, rin, rout, bx, after, w1, da, d, ext):
     ext[0:2] = with_sooner(bx[...])
-    ext[2:4, 2:10] = bi[1 - k, 0:2]
-    put_edges(ext, slice(2, 4), rin[1 + k, 0:2], rout[1 + k, 0:2])
-
-
-def pre01_kernel(bi, rin, rout, bx, ga, w1, v1x, ext):
-    fore_halo(ext, 0, bi, rin, rout, bx)
-    for t in range(2):
-        store_ten(v1x, t, ga[t] * factor(conv_fore(ext, w1, 1, t, 0, 10)))
-
-
-def factor01_kernel(bi, rin, rout, bx, w1, d, ext):
-    fore_halo(ext, 1, bi, rin, rout, bx)
-    for t in range(2):
-        d[t] = factor(conv_fore(ext, w1, 0, t, 0, 10))
-
-
-def pre23_kernel(v0, rin, rout, vx, d, v1x, w2, v1, ein, eout, ext):
-    ext[0:2, 2:10] = v0[2:4]
-    put_edges(ext, slice(0, 2), rin[0, 2:4], rout[0, 2:4])
+    ext[2:6, 2:10] = bi[0]
+    put_edges(ext, slice(2, 6), rin[2], rout[2])
+    for t in range(2):
+        da[t] = factor(conv_fore(ext, w1, 0, t, 0, 10))
+    for t in range(2):
+        d[t] = factor(conv_fore(ext, w1, 0, 2 + t, 1, 8))
+
+
+def later_part(ext, w, layer):
+    return [
+        conv_back(ext, w, layer, t, 1, 8, steps) for t, steps in ((0, (2,)), (1, (1, 2)))
+    ]
+
+
+def pre23_kernel(ga23, vx, d, v1x, w2, v1, ein, eout, ext):
     ext[2:4, 1:11] = with_later(vx[...])
-    for t in range(2):
-        v1[t] = (conv_back(ext, w2, 1, t, 1, 8) * d[t]).astype(BF)
+    for t, more in enumerate(later_part(ext, w2, 1)):
+        v1[t] = ((ga23[t] + more) * d[t]).astype(BF)
     send_edges(v1x, v1, ein, eout)
 
 
@@ -210,6 +230,12 @@
         store_ten(v2x, t, old[t, 1:11].astype(F32) + conv_back(ext, w1, 1, t, 0, 10))
 
 
+def grad01_kernel(v2x, v2, rin, rout, d, w2, v3x, ext):
+    local01(ext, v2x, v2, rin, rout)
+    for t in range(2):
+        store_ten(v3x, t, conv_back(ext, w2, 0, t, 0, 10) * d[t])
+
+
 def up23_kernel(v1, rin, rout, vxr, v0, v2x, w1, v2, ein, eout, ext):
     local23(ext, v1, rin, rout, vxr)
     for t in range(2):
@@ -217,17 +243,14 @@
     send_edges(v2x, v2, ein, eout)
 
 
-def grad01_kernel(v2x, v2, rin, rout, d, w2, v3x, ext):
-    local01(ext, v2x, v2, rin, rout)
-    for t in range(2):
-        store_ten(v3x, t, conv_back(ext, w2, 0, t, 0, 10) * d[t])
-
-
 def grad23_kernel(v2, rin, rout, vxr, d, v3x, w2, v3, ein, eout, ext):
     local23(ext, v2, rin, rout, vxr)
     for t in range(2):
         v3[t] = (conv_back(ext, w2, 0, t, 1, 8) * d[t]).astype(BF)
-    send_edges(v3x, v3, ein, eout)
+    p = side()
+    for t in range(2):
+        ein[t], eout[t] = v3x[t, 1 + 7 * (1 - p)], v3x[t, 1 + 7 * p]
+        ein[2 + t], eout[2 + t] = v3[t, 7 * (1 - p)], v3[t, 7 * p]
 
 
 def row_pairs(up):
@@ -236,7 +259,12 @@
 
 
 def last01_kernel(v3x, v3, rin, rout, v2x, v2, w1, pool, part, ext):
-    local01(ext, v3x, v3, rin, rout)
+    p = side()
+    ext[0:2, 1:11] = v3x[...]
+    ext[2:4, 2:10] = v3[...]
+    for t in range(4):
+        ext[t, 10 - 9 * p] = rin[t]
+        ext[t, 1 + 9 * p] = inside(rout[t])
     for t in range(2):
         pool[t] = row_pairs(v2x[t, 1:9].astype(F32) + conv_back(ext, w1, 0, t, 1, 8))
     for t, steps in ((0, (0, 1)), (1, (0,))):
@@ -247,16 +275,16 @@
     ext[2:4, 1:11] = with_later(vxr[...])
     half = 2 * 4 * COLS
     rows[0:half] = pool[...].reshape(half, C)
-    for t, steps in ((0, (2,)), (1, (1, 2))):
-        pair = row_pairs(part[t] + conv_back(ext, w1, 0, t, 1, 8, steps))
+    for t, more in enumerate(later_part(ext, w1, 0)):
+        pair = row_pairs(part[t] + more)
         rows[half + t * 4 * COLS : half + (t + 1) * 4 * COLS] = pair.reshape(4 * COLS, C)
-    units = owner.shape[0]
+    units = owner.shape[1]
     strips, capacity = out.shape[0], out.shape[1]
     slots = strips * capacity
     u = lax.broadcasted_iota(jnp.int32, (units, units), 0)
     v = lax.broadcasted_iota(jnp.int32, (units, units), 1)
-    mine = jnp.broadcast_to(owner[...], (units, units))
-    named = jnp.sum(jnp.where(u == v, mine, 0), axis=0, keepdims=True)
+    named = owner[...]
+    mine = jnp.sum(jnp.where(u == v, jnp.broadcast_to(named, (units, units)), 0), axis=1, keepdims=True)
     same = jnp.where((mine == named) & (u < v), 1, 0)
     slot = named * capacity + jnp.sum(same, axis=0, keepdims=True)
     place = jnp.where(
@@ -271,7 +299,7 @@
 
 
 VM = pl.BlockSpec(memory_space=pltpu.VMEM)
-SM = pl.BlockSpec(memory_space=pltpu.SMEM)
+HB = pl.BlockSpec(memory_space=pltpu.HBM)
 
 
 def field(*lead, dtype=BF):
@@ -291,7 +319,7 @@
         scratch_shapes=scratch,
         compiler_params=pltpu.CompilerParams(vmem_limit_bytes=40 << 20),
         cost_estimate=pl.CostEstimate(
-            flops=units * COLS * 27 * C * C * 3, bytes_accessed=moved, transcendentals=0
+            flops=units * COLS * 27 * C * C * 2, bytes_accessed=moved, transcendentals=0
         ),
         name=kernel.__name__,
     )(*args)
@@ -318,6 +346,10 @@
     def from_later(x):
         return lax.ppermute(x, "tm", later)
 
+    def corner(x, steps, pairs):
+        route = [(a * strips + s, b * strips + r) for a, b in steps for s, r in pairs]
+        return lax.ppermute(x, ("tm", "space"), route)
+
     def from_sooner(x):
         return lax.ppermute(x, "tm", sooner)
 
@@ -325,38 +357,54 @@
     bi = block_in
     ext = pltpu.VMEM((4, 12, COLS, C), BF)
 
-    v0, rin, rout = run(
+    ten, eight = field(2, 10, dtype=F32), field(2, 8, dtype=F32)
+    edges = [field(2, 8), field(4, 2), field(4, 2)]
+
+    v0, rin, rout, b1x, dpi, dpo = run(
         start_kernel,
-        [field(4, 8), field(3, 4, 2), field(3, 4, 2)],
+        [
+            field(4, 8), field(3, 4, 2), field(3, 4, 2), field(2, 8), field(2, 2), field(2, 2),
+        ],
         tuple(in_hbm(x) for x in (pixel_cot, bi, frame_group, advantage)),
         1,
         scratch=[
             pltpu.VMEM((4, 8, COLS, C), BF),
             pltpu.SMEM(frame_group.shape, jnp.int32),
             pltpu.SMEM(advantage.shape, F32),
-            pltpu.SemaphoreType.DMA((10,)),
-        ],
-        in_specs=[pl.BlockSpec(memory_space=pltpu.HBM)] * 4,
-    )
-    rin, rout = swap_in(rin), swap_out(rout)
-    v0x, b1x = run(extend_kernel, [field(2, 10), field(2, 12)], (v0, bi, rin, rout), 1, scratch=[])
+            pltpu.SemaphoreType.DMA((13,)),
+        ],
+        in_specs=[HB] * 4,
+    )
     b1x = from_sooner(b1x)
-    v0x = from_later(v0x)
-    ga, d1, d0, b0x = run(
+    rout, rin = swap_out(rout), swap_in(rin)
+    dpo, dpi = corner(dpo, sooner, outer_pairs), corner(dpi, sooner, inner_pairs)
+    v0x = from_later(run(extend_kernel, field(2, 10), (v0, rin, rout), 1, scratch=[]))
+    ga, ga23, d1, pre = run(
         early_kernel,
-        [field(2, 10, dtype=F32), field(2, 8, dtype=F32), field(2, 8, dtype=F32), field(2, 12)],
-        (v0, bi, rin, rout, w2, in_hbm(w1)),
-        52,
-        scratch=[ext, ext, ext, pltpu.VMEM(w1.shape, BF), pltpu.SemaphoreType.DMA],
-        in_specs=[VM] * 5 + [pl.BlockSpec(memory_space=pltpu.HBM)],
-    )
+        [ten, eight, eight, ten],
+        (v0, in_hbm(bi), rin, rout, in_hbm(w2), in_hbm(w1)),
+        54,
+        scratch=[
+            ext,
+            ext,
+            pltpu.VMEM(w2.shape, BF),
+            pltpu.VMEM(w1.shape, BF),
+            pltpu.SemaphoreType.DMA((3,)),
+        ],
+        in_specs=[VM, HB, VM, VM, HB, HB],
+    )
+    v1x = run(
+        pre01_kernel,
+        field(2, 10),
+        (b1x, dpi, dpo, ga, pre, w1),
+        10,
+        scratch=[pltpu.VMEM((2, 12, COLS, C), BF)],
+    )
+    v1xr = from_later(v1x)
+    v1, ein, eout = run(pre23_kernel, edges, (ga23, v0x, d1, v1x, w2), 8)
+    r1out, r1in = swap_out(eout), swap_in(ein)
+    b0x = run(extend0_kernel, field(2, 12), (bi, rin, rout, v1), 1, scratch=[])
     b0x = from_sooner(b0x)
-    v1x = run(pre01_kernel, field(2, 10), (bi, rin, rout, b1x, ga, w1), 20)
-    v1xr = from_later(v1x)
-    edges = [field(2, 8), field(4, 2), field(4, 2)]
-    v1, ein, eout = run(pre23_kernel, edges, (v0, rin, rout, v0x, d1, v1x, w2), 16)
-    r1in, r1out = swap_in(ein), swap_out(eout)
-    d0a = run(factor01_kernel, field(2, 10, dtype=F32), (bi, rin, rout, b0x, w1), 20)
     v2x = run(
         up01_kernel,
         field(2, 10),
@@ -366,19 +414,26 @@
     )
     v2xr = from_later(v2x)
     v2, ein, eout = run(up23_kernel, edges, (v1, r1in, r1out, v1xr, v0, v2x, w1), 16)
-    r2in, r2out = swap_in(ein), swap_out(eout)
+    r2out, r2in = swap_out(eout), swap_in(ein)
+    d0a, d0 = run(
+        factor_kernel,
+        [ten, eight],
+        (bi, rin, rout, b0x, v2, w1),
+        36,
+        scratch=[pltpu.VMEM((6, 12, COLS, C), BF)],
+    )
     v3x = run(grad01_kernel, field(2, 10), (v2x, v2, r2in, r2out, d0a, w2), 20)
     v3xr = from_later(v3x)
-    v3, ein, eout = run(grad23_kernel, edges, (v2, r2in, r2out, v2xr, d0, v3x, w2), 16)
-    r3in, r3out = swap_in(ein), swap_out(eout)
+    v3, ein, eout = run(grad23_kernel, [field(2, 8), field(4), field(4)], (v2, r2in, r2out, v2xr, d0, v3x, w2), 16)
+    r3out, r3in = swap_out(eout), swap_in(ein)
     pool, part = run(
         last01_kernel,
-        [field(2, 4, dtype=F32), field(2, 8, dtype=F32)],
+        [field(2, 4, dtype=F32), eight],
         (v3x, v3, r3in, r3out, v2x, v2, w1),
         24,
     )
-    owner = owner_map.reshape(-1, 1)
-    units = owner.shape[0]
+    owner = owner_map.reshape(1, -1)
+    units = owner.shape[1]
     capacity = max(2, 2 * units // strips)
     outgoing = run(
         last23_kernel,

time: 82.7 us -> 78.3 us (0.947)
  waiting for transfers between devices: 16.3 us -> 9 us
  starting transfers between devices: 23.1 us -> 28.7 us
  local copies, waits for them, and re-layouts: 3.42 us -> 0.73 us
  Pallas kernels: 21.5 us -> 22.5 us
  blocking collectives: 18 us -> 17 us
    ppermute x4, waiting for transfers between devices: 14.8 us -> 6.79 us  [swap_out(): return lax.ppermute(x, 'space', outer_pairs)]
    ppermute x0 -> x2, starting transfers between devices: none -> 6.37 us  [corner(): return lax.ppermute(x, ('tm', 'space'), route)]
    unnamed x17 -> x9, local copies, waits for them, and re-layouts: 3.32 us -> 0.73 us
    all_to_all x1, blocking collectives: 18 us -> 17 us  [on_device(): lax.all_to_all(outgoing, 'space', split_axis=0, concat_axis=0, tiled=True)]
    pallas_call x12 -> x13, Pallas kernels: 21.5 us -> 22.5 us  [run(): pl.pallas_call(kernel, out_shape=outs, in_specs=in_specs or [VM] * len(ar...]
  transfers between devices with their start and end apart: 14 -> 16, of which waited for: 7 -> 5; matrix products, arithmetic and copies ran while one was open for 0% -> 0% of each run, Pallas kernels for 23% -> 25%
where the time goes in v2:
time: 78.3 us; the launch traced here: 78.1 us
  starting transfers between devices  28.7 us (37%)
  Pallas kernels  22.5 us (29%)
  blocking collectives  17 us (22%)
  waiting for transfers between devices  9 us (11%)
    pallas_call x13, Pallas kernels, run(): pl.pallas_call(kernel, out_shape=outs, in_specs=in_specs or [VM] * len(ar...  22.5 us
    all_to_all x1, blocking collectives, on_device(): lax.all_to_all(outgoing, 'space', split_axis=0, concat_axis=0, tiled=True)  17 us
    ppermute x4, starting transfers between devices, swap_in(): return lax.ppermute(x, 'space', inner_pairs)  14.1 us
    ppermute x4, waiting for transfers between devices, swap_out(): return lax.ppermute(x, 'space', outer_pairs)  6.79 us
    ppermute x2, starting transfers between devices, corner(): return lax.ppermute(x, ('tm', 'space'), route)  6.37 us
    ppermute x4, starting transfers between devices, from_later(): return lax.ppermute(x, 'tm', later)  3.94 us
    ppermute x2, starting transfers between devices, from_sooner(): return lax.ppermute(x, 'tm', sooner)  2.34 us
    ppermute x4, starting transfers between devices, swap_out(): return lax.ppermute(x, 'space', outer_pairs)  1.97 us
  transfers between devices with their start and end apart: 16, of which 5 were waited for; matrix products, arithmetic and copies ran while one was open for 0% of the time, Pallas kernels for 25%

profile of v2, /device:TPU:1, one launch (start us, length us, event | category | flops | bytes accessed | tf_op | source)
XLA Modules:
  0.0 78.1 jit_solution(15884872724468883116)
XLA Ops:
  0.0 1.5 %start_kernel.1 = (bf16[4,8,64,128]{3,2,1,0:T(8,128)(2,1)S(1)}, bf16[3,4,2,64,128]{4,3,2,1,0:T(8,128)(2,1)S(1)}, bf16[3,4,2,64,128]{4,3,2,1,0:T(8,128)(2,1)S(1)}...) custom-call(bf16[4,8,64,128]{3,2,1,0:T(8,128)(2,1)} %cot.1, ...), custom_call_target="tpu_custom_call" | custom-call | flops 56623104 | bytes 1572896 | tf_op jit(solution)/shard_map/start_kernel/pallas_call | solution.py:314
  1.5 1.5 %collective-permute-start.3 = (bf16[3,4,2,64,128]{4,3,2,1,0:T(8,128)(2,1)S(1)}, bf16[3,4,2,64,128]{4,3,2,1,0:T(8,128)(2,1)S(1)}, u32[]{:S(2)}, u32[]{:S(2)}) collective-permute-start(bf16[3,4,2,64,128]{4,3,2,1,0:T(8,128)(2,1)S(1)} %get-tuple-element.32), channel_id=1, source_target_pairs={{0,1},{1,0},{2,3},{3,2},{4,5},{5,4},{6,7},{7,6},{8,9},{9,8},{10,11... | collective-permute-start | bytes 1179656 | tf_op jit(solution)/shard_map/ppermute | solution.py:341
  3.0 1.7 %collective-permute-start.4 = (bf16[3,4,2,64,128]{4,3,2,1,0:T(8,128)(2,1)S(1)}, bf16[3,4,2,64,128]{4,3,2,1,0:T(8,128)(2,1)S(1)}, u32[]{:S(2)}, u32[]{:S(2)}) collective-permute-start(bf16[3,4,2,64,128]{4,3,2,1,0:T(8,128)(2,1)S(1)} %get-tuple-element.33), channel_id=1, source_target_pairs={{0,31},{1,2},{2,1},{3,4},{4,3},{5,6},{6,5},{7,8},{8,7},{9,10},{10,... | collective-permute-start | bytes 1179656 | tf_op jit(solution)/shard_map/ppermute | solution.py:344
  4.7 1.2 %collective-permute-start = (bf16[2,8,64,128]{3,2,1,0:T(8,128)(2,1)S(1)}, bf16[2,8,64,128]{3,2,1,0:T(8,128)(2,1)S(1)}, u32[]{:S(2)}, u32[]{:S(2)}) collective-permute-start(bf16[2,8,64,128]{3,2,1,0:T(8,128)(2,1)S(1)} %get-tuple-element.28), channel_id=1, source_target_pairs={{0,32},{32,64},{64,96},{96,0},{1,33},{33,65},{65,97},{97,1},{2,34}... | collective-permute-start | bytes 786440 | tf_op jit(solution)/shard_map/ppermute | solution.py:354
  5.9 6.4 %collective-permute-start.1 = (bf16[2,2,64,128]{3,2,1,0:T(8,128)(2,1)S(1)}, bf16[2,2,64,128]{3,2,1,0:T(8,128)(2,1)S(1)}, u32[]{:S(2)}, u32[]{:S(2)}) collective-permute-start(bf16[2,2,64,128]{3,2,1,0:T(8,128)(2,1)S(1)} %get-tuple-element.29), channel_id=1, source_target_pairs={{0,33},{1,32},{2,35},{3,34},{4,37},{5,36},{6,39},{7,38},{8,41},{9,... | collective-permute-start | bytes 196616 | tf_op jit(solution)/shard_map/ppermute | solution.py:351
  12.3 0.0 collective-permute-start.2
  12.3 0.0 collective-permute-done.3.rin.r0in
  12.3 0.0 collective-permute-done.4.rout.r0out
  12.3 0.0 copy-start
  12.4 1.5 %collective-permute-start.5 = (bf16[2,10,64,128]{3,2,1,0:T(8,128)(2,1)S(1)}, bf16[2,10,64,128]{3,2,1,0:T(8,128)(2,1)S(1)}, u32[]{:S(2)}, u32[]{:S(2)}) collective-permute-start(bf16[2,10,64,128]{3,2,1,0:T(8,128)(2,1)S(1)} %extend_kernel.1), channel_id=1, source_target_pairs={{32,0},{64,32},{96,64},{0,96},{33,1},{65,33},{97,65},{1,97},{34,2}... | collective-permute-start | bytes 983048 | tf_op jit(solution)/shard_map/ppermute | solution.py:347
  13.9 5.9 %early_kernel.1 = (f32[2,10,64,128]{3,2,1,0:T(8,128)S(1)}, f32[2,8,64,128]{3,2,1,0:T(8,128)S(1)}, f32[2,8,64,128]{3,2,1,0:T(8,128)S(1)}, f32[2,10,64,128]{3,2,1,0:T(8,128)S(1)}) custom-call(bf16[4,8,64,128]{3,2,1,0:T(8,128)(2,1)S(1)} %get-tuple-element.31.v0, bf16[2,4,8,64,128]{4,3,2,1,0:T(8,128)(2,1)} %bi.5, ...), custom_call_target="tpu_custom_call" | custom-call | flops 3057647616 | bytes 5898240 | tf_op jit(solution)/shard_map/early_kernel/pallas_call | solution.py:314
  19.8 0.0 collective-permute-done.1.dpi
  19.9 0.0 collective-permute-done.2.dpo
  19.9 0.0 collective-permute-done.bx
  19.9 0.0 copy-start.1
  19.9 1.1 %pre01_kernel.1.v1x = bf16[2,10,64,128]{3,2,1,0:T(8,128)(2,1)S(1)} custom-call(bf16[2,8,64,128]{3,2,1,0:T(8,128)(2,1)S(1)} %collective-permute-done.bx, bf16[2,2,64,128]{3,2,1,0:T(8,128)(2,1)S(1)} %collective-permute-done.1.dpi, bf16[2,2,64,128]{3,2,1,0:T(8,128)(2,1)S(1)} %collective-permute-done.2.dpo, f32[2,10,64,128]{3,2,1,0:T(8,128)S(1)} %get-tuple-element.34.ga, ...), custom_call_target="tpu_custom_call" | custom-call | flops 566231040 | bytes 3473408 | tf_op jit(solution)/shard_map/pre01_kernel/pallas_call | solution.py:314
  21.0 0.0 copy-start.2
  21.0 0.5 collective-permute-start.8
  21.5 0.0 collective-permute-done.5.vx
  21.5 0.9 %pre23_kernel.1 = (bf16[2,8,64,128]{3,2,1,0:T(8,128)(2,1)S(1)}, bf16[4,2,64,128]{3,2,1,0:T(8,128)(2,1)S(1)}, bf16[4,2,64,128]{3,2,1,0:T(8,128)(2,1)S(1)}) custom-call(f32[2,8,64,128]{3,2,1,0:T(8,128)S(1)} %get-tuple-element.36.ga23, bf16[2,10,64,128]{3,2,1,0:T(8,128)(2,1)S(1)} %collective-permute-done.5.vx, f32[2,8,64,128]{3,2,1,0:T(8,128)S(1)} %get-tuple-element.37.d, ...), custom_call_target="tpu_custom_call" | custom-call | flops 452984832 | bytes 3473408 | tf_op jit(solution)/shard_map/pre23_kernel/pallas_call | solution.py:314
  22.4 1.1 %collective-permute-start.11 = (bf16[2,12,64,128]{3,2,1,0:T(8,128)(2,1)S(1)}, bf16[2,12,64,128]{3,2,1,0:T(8,128)(2,1)S(1)}, u32[]{:S(2)}, u32[]{:S(2)}) collective-permute-start(bf16[2,12,64,128]{3,2,1,0:T(8,128)(2,1)S(1)} %extend0_kernel.1), channel_id=1, source_target_pairs={{0,32},{32,64},{64,96},{96,0},{1,33},{33,65},{65,97},{97,1},{2,34}... | collective-permute-start | bytes 1179656 | tf_op jit(solution)/shard_map/ppermute | solution.py:354
  23.5 4.7 %collective-permute-start.6 = (bf16[4,2,64,128]{3,2,1,0:T(8,128)(2,1)S(1)}, bf16[4,2,64,128]{3,2,1,0:T(8,128)(2,1)S(1)}, u32[]{:S(2)}, u32[]{:S(2)}) collective-permute-start(bf16[4,2,64,128]{3,2,1,0:T(8,128)(2,1)S(1)} %get-tuple-element.39), channel_id=1, source_target_pairs={{0,1},{1,0},{2,3},{3,2},{4,5},{5,4},{6,7},{7,6},{8,9},{9,8},{10,11... | collective-permute-start | bytes 393224 | tf_op jit(solution)/shard_map/ppermute | solution.py:341
  28.2 0.0 collective-permute-start.7
  28.2 1.0 %collective-permute-done.6.rin = bf16[4,2,64,128]{3,2,1,0:T(8,128)(2,1)S(1)} collective-permute-done((bf16[4,2,64,128]{3,2,1,0:T(8,128)(2,1)S(1)}, bf16[4,2,64,128]{3,2,1,0:T(8,128)(2,1)S(1)}, u32[]{:S(2)}, u32[]{:S(2)}) %collective-permute-start.6) | collective-permute-done | bytes 131104 | tf_op jit(solution)/shard_map/ppermute | solution.py:341
  29.2 3.7 %collective-permute-done.7.rout = bf16[4,2,64,128]{3,2,1,0:T(8,128)(2,1)S(1)} collective-permute-done((bf16[4,2,64,128]{3,2,1,0:T(8,128)(2,1)S(1)}, bf16[4,2,64,128]{3,2,1,0:T(8,128)(2,1)S(1)}, u32[]{:S(2)}, u32[]{:S(2)}) %collective-permute-start.7) | collective-permute-done | bytes 131104 | tf_op jit(solution)/shard_map/ppermute | solution.py:344
  32.9 1.8 %up01_kernel.1.v2x = bf16[2,10,64,128]{3,2,1,0:T(8,128)(2,1)S(1)} custom-call(bf16[2,10,64,128]{3,2,1,0:T(8,128)(2,1)S(1)} %pre01_kernel.1.v1x, bf16[2,8,64,128]{3,2,1,0:T(8,128)(2,1)S(1)} %get-tuple-element.38.v1.after, bf16[4,2,64,128]{3,2,1,0:T(8,128)(2,1)S(1)} %collective-permute-done.6.rin, bf16[4,2,64,128]{3,2,1,0:T(8,128)(2,1)S(1)} %collective-permute-done.7.rout, ...), custom_call_target="tpu_custom_call" | custom-call | flops 1132462080 | bytes 3932160 | tf_op jit(solution)/shard_map/up01_kernel/pallas_call | solution.py:314
  34.7 1.8 %collective-permute-start.13 = (bf16[2,10,64,128]{3,2,1,0:T(8,128)(2,1)S(1)}, bf16[2,10,64,128]{3,2,1,0:T(8,128)(2,1)S(1)}, u32[]{:S(2)}, u32[]{:S(2)}) collective-permute-start(bf16[2,10,64,128]{3,2,1,0:T(8,128)(2,1)S(1)} %up01_kernel.1.v2x), channel_id=1, source_target_pairs={{32,0},{64,32},{96,64},{0,96},{33,1},{65,33},{97,65},{1,97},{34,2}... | collective-permute-start | bytes 983048 | tf_op jit(solution)/shard_map/ppermute | solution.py:347
  36.6 0.0 collective-permute-done.8.vxr
  36.6 1.5 %up23_kernel.1 = (bf16[2,8,64,128]{3,2,1,0:T(8,128)(2,1)S(1)}, bf16[4,2,64,128]{3,2,1,0:T(8,128)(2,1)S(1)}, bf16[4,2,64,128]{3,2,1,0:T(8,128)(2,1)S(1)}) custom-call(bf16[2,8,64,128]{3,2,1,0:T(8,128)(2,1)S(1)} %get-tuple-element.38.v1.after, bf16[4,2,64,128]{3,2,1,0:T(8,128)(2,1)S(1)} %collective-permute-done.6.rin, ...), custom_call_target="tpu_custom_call" | custom-call | flops 905969664 | bytes 3473408 | tf_op jit(solution)/shard_map/up23_kernel/pallas_call | solution.py:314
  38.1 0.3 collective-permute-start.10
  38.4 7.2 %collective-permute-start.9 = (bf16[4,2,64,128]{3,2,1,0:T(8,128)(2,1)S(1)}, bf16[4,2,64,128]{3,2,1,0:T(8,128)(2,1)S(1)}, u32[]{:S(2)}, u32[]{:S(2)}) collective-permute-start(bf16[4,2,64,128]{3,2,1,0:T(8,128)(2,1)S(1)} %get-tuple-element.42), channel_id=1, source_target_pairs={{0,1},{1,0},{2,3},{3,2},{4,5},{5,4},{6,7},{7,6},{8,9},{9,8},{10,11... | collective-permute-start | bytes 393224 | tf_op jit(solution)/shard_map/ppermute | solution.py:341
  45.6 0.0 collective-permute-done.11.bx
  45.6 3.1 %factor_kernel.1 = (f32[2,10,64,128]{3,2,1,0:T(8,128)S(1)}, f32[2,8,64,128]{3,2,1,0:T(8,128)S(1)}) custom-call(bf16[2,4,8,64,128]{4,3,2,1,0:T(8,128)(2,1)S(1)} %copy-done.2, bf16[3,4,2,64,128]{4,3,2,1,0:T(8,128)(2,1)S(1)} %collective-permute-done.3.rin.r0in, bf16[3,4,2,64,128]{4,3,2,1,0:T(8,128)(2,1)S(1)} %collective-permute-done.4.rout.r0out, ...), custom_call_target="tpu_custom_call" | custom-call | flops 2038431744 | bytes 4259840 | tf_op jit(solution)/shard_map/factor_kernel/pallas_call | solution.py:314
  48.7 0.0 collective-permute-done.10.rout
  48.8 0.0 collective-permute-done.9.rin
  48.8 1.8 %grad01_kernel.1.v3x = bf16[2,10,64,128]{3,2,1,0:T(8,128)(2,1)S(1)} custom-call(bf16[2,10,64,128]{3,2,1,0:T(8,128)(2,1)S(1)} %up01_kernel.1.v2x, bf16[2,8,64,128]{3,2,1,0:T(8,128)(2,1)S(1)} %get-tuple-element.41.after.v2, bf16[4,2,64,128]{3,2,1,0:T(8,128)(2,1)S(1)} %collective-permute-done.9.rin, bf16[4,2,64,128]{3,2,1,0:T(8,128)(2,1)S(1)} %collective-permute-done.10.rout, ...), custom_call_target="tpu_custom_call" | custom-call | flops 1132462080 | bytes 3276800 | tf_op jit(solution)/shard_map/grad01_kernel/pallas_call | solution.py:314
  50.6 0.1 collective-permute-start.12
  50.7 0.0 collective-permute-done.13.vxr
  50.7 1.5 %grad23_kernel.1 = (bf16[2,8,64,128]{3,2,1,0:T(8,128)(2,1)S(1)}, bf16[4,64,128]{2,1,0:T(8,128)(2,1)S(1)}, bf16[4,64,128]{2,1,0:T(8,128)(2,1)S(1)}) custom-call(bf16[2,8,64,128]{3,2,1,0:T(8,128)(2,1)S(1)} %get-tuple-element.41.after.v2, bf16[4,2,64,128]{3,2,1,0:T(8,128)(2,1)S(1)} %collective-permute-done.9.rin, ...), custom_call_target="tpu_custom_call" | custom-call | flops 905969664 | bytes 3473408 | tf_op jit(solution)/shard_map/grad23_kernel/pallas_call | solution.py:314
  52.2 0.7 collective-permute-start.14
  52.9 0.0 collective-permute-start.15
  52.9 0.9 %collective-permute-done.14.rin = bf16[4,64,128]{2,1,0:T(8,128)(2,1)S(1)} collective-permute-done((bf16[4,64,128]{2,1,0:T(8,128)(2,1)S(1)}, bf16[4,64,128]{2,1,0:T(8,128)(2,1)S(1)}, u32[]{:S(2)}, u32[]{:S(2)}) %collective-permute-start.14) | collective-permute-done | bytes 65568 | tf_op jit(solution)/shard_map/ppermute | solution.py:341
  53.8 3.1 %collective-permute-done.15.rout = bf16[4,64,128]{2,1,0:T(8,128)(2,1)S(1)} collective-permute-done((bf16[4,64,128]{2,1,0:T(8,128)(2,1)S(1)}, bf16[4,64,128]{2,1,0:T(8,128)(2,1)S(1)}, u32[]{:S(2)}, u32[]{:S(2)}) %collective-permute-start.15) | collective-permute-done | bytes 65568 | tf_op jit(solution)/shard_map/ppermute | solution.py:344
  56.8 2.1 %last01_kernel.1 = (f32[2,4,64,128]{3,2,1,0:T(8,128)S(1)}, f32[2,8,64,128]{3,2,1,0:T(8,128)S(1)}) custom-call(bf16[2,10,64,128]{3,2,1,0:T(8,128)(2,1)S(1)} %grad01_kernel.1.v3x, bf16[2,8,64,128]{3,2,1,0:T(8,128)(2,1)S(1)} %get-tuple-element.46.v3, bf16[4,64,128]{2,1,0:T(8,128)(2,1)S(1)} %collective-permute-done.14.rin, ...), custom_call_target="tpu_custom_call" | custom-call | flops 1358954496 | bytes 3080192 | tf_op jit(solution)/shard_map/last01_kernel/pallas_call | solution.py:314
  59.0 0.3 collective-permute-done.12.vxr
  59.3 1.1 %last23_kernel.1 = bf16[32,4,1024]{2,1,0:T(4,128)(2,1)S(1)} custom-call(bf16[2,10,64,128]{3,2,1,0:T(8,128)(2,1)S(1)} %collective-permute-done.12.vxr, f32[2,4,64,128]{3,2,1,0:T(8,128)S(1)} %get-tuple-element.49.pool, f32[2,8,64,128]{3,2,1,0:T(8,128)S(1)} %get-tuple-element.50.part, s32[1,64]{1,0:T(1,128)S(1)} %bitcast.2, ...), custom_call_target="tpu_custom_call" | custom-call | flops 452984832 | bytes 2883840 | tf_op jit(solution)/shard_map/last23_kernel/pallas_call | solution.py:314
  60.4 17.0 %all_to_all.5 = bf16[32,4,1024]{2,1,0:T(4,128)(2,1)S(1)} all-to-all(bf16[32,4,1024]{2,1,0:T(4,128)(2,1)S(1)} %last23_kernel.1), channel_id=1, replica_groups=mesh['tm'=4,'space'=32] {'space'}, dimensions={0} | all-to-all | bytes 524288 | tf_op jit(solution)/shard_map/all_to_all | solution.py:445
  77.4 0.7 copy.9
  (7 shorter events, 0.1 us)
Async XLA Ops:
  1.5 10.8 %collective-permute-start.3 = (bf16[3,4,2,64,128]{4,3,2,1,0:T(8,128)(2,1)S(1)}, bf16[3,4,2,64,128]{4,3,2,1,0:T(8,128)(2,1)S(1)}, u32[]{:S(2)}, u32[]{:S(2)}) collective-permute-start(bf16[3,4,2,64,128]{4,3,2,1,0:T(8,128)(2,1)S(1)} %get-tuple-element.32), channel_id=1, source_target_pairs={{0,1},{1,0},{2,3},{3,2},{4,5},{5,4},{6,7},{7,6},{8,9},{9,8},{10,11... | collective-permute-start | bytes 1179656 | tf_op jit(solution)/shard_map/ppermute | solution.py:341
  3.0 9.3 %collective-permute-start.4 = (bf16[3,4,2,64,128]{4,3,2,1,0:T(8,128)(2,1)S(1)}, bf16[3,4,2,64,128]{4,3,2,1,0:T(8,128)(2,1)S(1)}, u32[]{:S(2)}, u32[]{:S(2)}) collective-permute-start(bf16[3,4,2,64,128]{4,3,2,1,0:T(8,128)(2,1)S(1)} %get-tuple-element.33), channel_id=1, source_target_pairs={{0,31},{1,2},{2,1},{3,4},{4,3},{5,6},{6,5},{7,8},{8,7},{9,10},{10,... | collective-permute-start | bytes 1179656 | tf_op jit(solution)/shard_map/ppermute | solution.py:344
  4.7 15.1 %collective-permute-start = (bf16[2,8,64,128]{3,2,1,0:T(8,128)(2,1)S(1)}, bf16[2,8,64,128]{3,2,1,0:T(8,128)(2,1)S(1)}, u32[]{:S(2)}, u32[]{:S(2)}) collective-permute-start(bf16[2,8,64,128]{3,2,1,0:T(8,128)(2,1)S(1)} %get-tuple-element.28), channel_id=1, source_target_pairs={{0,32},{32,64},{64,96},{96,0},{1,33},{33,65},{65,97},{97,1},{2,34}... | collective-permute-start | bytes 786440 | tf_op jit(solution)/shard_map/ppermute | solution.py:354
  5.9 13.9 %collective-permute-start.1 = (bf16[2,2,64,128]{3,2,1,0:T(8,128)(2,1)S(1)}, bf16[2,2,64,128]{3,2,1,0:T(8,128)(2,1)S(1)}, u32[]{:S(2)}, u32[]{:S(2)}) collective-permute-start(bf16[2,2,64,128]{3,2,1,0:T(8,128)(2,1)S(1)} %get-tuple-element.29), channel_id=1, source_target_pairs={{0,33},{1,32},{2,35},{3,34},{4,37},{5,36},{6,39},{7,38},{8,41},{9,... | collective-permute-start | bytes 196616 | tf_op jit(solution)/shard_map/ppermute | solution.py:351
  12.3 7.6 %collective-permute-start.2 = (bf16[2,2,64,128]{3,2,1,0:T(8,128)(2,1)S(1)}, bf16[2,2,64,128]{3,2,1,0:T(8,128)(2,1)S(1)}, u32[]{:S(2)}, u32[]{:S(2)}) collective-permute-start(bf16[2,2,64,128]{3,2,1,0:T(8,128)(2,1)S(1)} %get-tuple-element.30), channel_id=1, source_target_pairs={{0,63},{1,34},{2,33},{3,36},{4,35},{5,38},{6,37},{7,40},{8,39},{9,... | collective-permute-start | bytes 196616 | tf_op jit(solution)/shard_map/ppermute | solution.py:351
  12.3 7.5 %copy-start = (bf16[2,3,3,3,128,128]{5,4,3,2,1,0:T(8,128)(2,1)S(1)}, bf16[2,3,3,3,128,128]{5,4,3,2,1,0:T(8,128)(2,1)}, u32[]{:S(2)}) copy-start(bf16[2,3,3,3,128,128]{5,4,3,2,1,0:T(8,128)(2,1)} %w1.11) | copy-start | bytes 5308420
  12.4 9.1 %collective-permute-start.5 = (bf16[2,10,64,128]{3,2,1,0:T(8,128)(2,1)S(1)}, bf16[2,10,64,128]{3,2,1,0:T(8,128)(2,1)S(1)}, u32[]{:S(2)}, u32[]{:S(2)}) collective-permute-start(bf16[2,10,64,128]{3,2,1,0:T(8,128)(2,1)S(1)} %extend_kernel.1), channel_id=1, source_target_pairs={{32,0},{64,32},{96,64},{0,96},{33,1},{65,33},{97,65},{1,97},{34,2}... | collective-permute-start | bytes 983048 | tf_op jit(solution)/shard_map/ppermute | solution.py:347
  19.9 1.6 %copy-start.1 = (bf16[2,3,3,3,128,128]{5,4,3,2,1,0:T(8,128)(2,1)S(1)}, bf16[2,3,3,3,128,128]{5,4,3,2,1,0:T(8,128)(2,1)}, u32[]{:S(2)}) copy-start(bf16[2,3,3,3,128,128]{5,4,3,2,1,0:T(8,128)(2,1)} %w2.5) | copy-start | bytes 5308420
  21.0 1.4 %copy-start.2 = (bf16[2,4,8,64,128]{4,3,2,1,0:T(8,128)(2,1)S(1)}, bf16[2,4,8,64,128]{4,3,2,1,0:T(8,128)(2,1)}, u32[]{:S(2)}) copy-start(bf16[2,4,8,64,128]{4,3,2,1,0:T(8,128)(2,1)} %bi.5) | copy-start | bytes 3145732
  21.0 15.6 %collective-permute-start.8 = (bf16[2,10,64,128]{3,2,1,0:T(8,128)(2,1)S(1)}, bf16[2,10,64,128]{3,2,1,0:T(8,128)(2,1)S(1)}, u32[]{:S(2)}, u32[]{:S(2)}) collective-permute-start(bf16[2,10,64,128]{3,2,1,0:T(8,128)(2,1)S(1)} %pre01_kernel.1.v1x), channel_id=1, source_target_pairs={{32,0},{64,32},{96,64},{0,96},{33,1},{65,33},{97,65},{1,97},{34,2}... | collective-permute-start | bytes 983048 | tf_op jit(solution)/shard_map/ppermute | solution.py:347
  22.4 23.2 %collective-permute-start.11 = (bf16[2,12,64,128]{3,2,1,0:T(8,128)(2,1)S(1)}, bf16[2,12,64,128]{3,2,1,0:T(8,128)(2,1)S(1)}, u32[]{:S(2)}, u32[]{:S(2)}) collective-permute-start(bf16[2,12,64,128]{3,2,1,0:T(8,128)(2,1)S(1)} %extend0_kernel.1), channel_id=1, source_target_pairs={{0,32},{32,64},{64,96},{96,0},{1,33},{33,65},{65,97},{97,1},{2,34}... | collective-permute-start | bytes 1179656 | tf_op jit(solution)/shard_map/ppermute | solution.py:354
  23.5 5.7 %collective-permute-start.6 = (bf16[4,2,64,128]{3,2,1,0:T(8,128)(2,1)S(1)}, bf16[4,2,64,128]{3,2,1,0:T(8,128)(2,1)S(1)}, u32[]{:S(2)}, u32[]{:S(2)}) collective-permute-start(bf16[4,2,64,128]{3,2,1,0:T(8,128)(2,1)S(1)} %get-tuple-element.39), channel_id=1, source_target_pairs={{0,1},{1,0},{2,3},{3,2},{4,5},{5,4},{6,7},{7,6},{8,9},{9,8},{10,11... | collective-permute-start | bytes 393224 | tf_op jit(solution)/shard_map/ppermute | solution.py:341
  28.2 4.7 %collective-permute-start.7 = (bf16[4,2,64,128]{3,2,1,0:T(8,128)(2,1)S(1)}, bf16[4,2,64,128]{3,2,1,0:T(8,128)(2,1)S(1)}, u32[]{:S(2)}, u32[]{:S(2)}) collective-permute-start(bf16[4,2,64,128]{3,2,1,0:T(8,128)(2,1)S(1)} %get-tuple-element.40), channel_id=1, source_target_pairs={{0,31},{1,2},{2,1},{3,4},{4,3},{5,6},{6,5},{7,8},{8,7},{9,10},{10,... | collective-permute-start | bytes 393224 | tf_op jit(solution)/shard_map/ppermute | solution.py:344
  34.7 15.9 %collective-permute-start.13 = (bf16[2,10,64,128]{3,2,1,0:T(8,128)(2,1)S(1)}, bf16[2,10,64,128]{3,2,1,0:T(8,128)(2,1)S(1)}, u32[]{:S(2)}, u32[]{:S(2)}) collective-permute-start(bf16[2,10,64,128]{3,2,1,0:T(8,128)(2,1)S(1)} %up01_kernel.1.v2x), channel_id=1, source_target_pairs={{32,0},{64,32},{96,64},{0,96},{33,1},{65,33},{97,65},{1,97},{34,2}... | collective-permute-start | bytes 983048 | tf_op jit(solution)/shard_map/ppermute | solution.py:347
  38.1 10.7 %collective-permute-start.10 = (bf16[4,2,64,128]{3,2,1,0:T(8,128)(2,1)S(1)}, bf16[4,2,64,128]{3,2,1,0:T(8,128)(2,1)S(1)}, u32[]{:S(2)}, u32[]{:S(2)}) collective-permute-start(bf16[4,2,64,128]{3,2,1,0:T(8,128)(2,1)S(1)} %get-tuple-element.43), channel_id=1, source_target_pairs={{0,31},{1,2},{2,1},{3,4},{4,3},{5,6},{6,5},{7,8},{8,7},{9,10},{10,... | collective-permute-start | bytes 393224 | tf_op jit(solution)/shard_map/ppermute | solution.py:344
  38.4 10.4 %collective-permute-start.9 = (bf16[4,2,64,128]{3,2,1,0:T(8,128)(2,1)S(1)}, bf16[4,2,64,128]{3,2,1,0:T(8,128)(2,1)S(1)}, u32[]{:S(2)}, u32[]{:S(2)}) collective-permute-start(bf16[4,2,64,128]{3,2,1,0:T(8,128)(2,1)S(1)} %get-tuple-element.42), channel_id=1, source_target_pairs={{0,1},{1,0},{2,3},{3,2},{4,5},{5,4},{6,7},{7,6},{8,9},{9,8},{10,11... | collective-permute-start | bytes 393224 | tf_op jit(solution)/shard_map/ppermute | solution.py:341
  50.6 8.7 %collective-permute-start.12 = (bf16[2,10,64,128]{3,2,1,0:T(8,128)(2,1)S(1)}, bf16[2,10,64,128]{3,2,1,0:T(8,128)(2,1)S(1)}, u32[]{:S(2)}, u32[]{:S(2)}) collective-permute-start(bf16[2,10,64,128]{3,2,1,0:T(8,128)(2,1)S(1)} %grad01_kernel.1.v3x), channel_id=1, source_target_pairs={{32,0},{64,32},{96,64},{0,96},{33,1},{65,33},{97,65},{1,97},{34,2}... | collective-permute-start | bytes 983048 | tf_op jit(solution)/shard_map/ppermute | solution.py:347
  52.2 1.6 %collective-permute-start.14 = (bf16[4,64,128]{2,1,0:T(8,128)(2,1)S(1)}, bf16[4,64,128]{2,1,0:T(8,128)(2,1)S(1)}, u32[]{:S(2)}, u32[]{:S(2)}) collective-permute-start(bf16[4,64,128]{2,1,0:T(8,128)(2,1)S(1)} %get-tuple-element.47), channel_id=1, source_target_pairs={{0,1},{1,0},{2,3},{3,2},{4,5},{5,4},{6,7},{7,6},{8,9},{9,8},{10,11... | collective-permute-start | bytes 196616 | tf_op jit(solution)/shard_map/ppermute | solution.py:341
  52.9 4.0 %collective-permute-start.15 = (bf16[4,64,128]{2,1,0:T(8,128)(2,1)S(1)}, bf16[4,64,128]{2,1,0:T(8,128)(2,1)S(1)}, u32[]{:S(2)}, u32[]{:S(2)}) collective-permute-start(bf16[4,64,128]{2,1,0:T(8,128)(2,1)S(1)} %get-tuple-element.48), channel_id=1, source_target_pairs={{0,31},{1,2},{2,1},{3,4},{4,3},{5,6},{6,5},{7,8},{8,7},{9,10},{10,... | collective-permute-start | bytes 196616 | tf_op jit(solution)/shard_map/ppermute | solution.py:344
  56.8 2.5 %copy-start.3 = (s32[1,1,64,1]{2,3,1,0:T(1,128)S(1)}, s32[1,1,64,1]{2,3,1,0:T(1,128)}, u32[]{:S(2)}) copy-start(s32[1,1,64,1]{2,3,1,0:T(1,128)} %param.13) | copy-start | bytes 772

commit v3 on v2

--- a/solution.py
+++ b/solution.py
@@ -154,28 +154,31 @@
     put_edges(bx, slice(0, 2), rin[2, 2:4], rout[2, 2:4])
 
 
-def early_kernel(v0, bih, rin, rout, w2h, w1h, ga, ga23, d1, pre, ext, ext1, w2, w1, sem):
+def fetch_kernel(after, bi, w2, w1, bi1, w2o, w1o, sem):
     copies = [
-        pltpu.make_async_copy(w2h.at[1], w2.at[1], sem.at[0]),
-        pltpu.make_async_copy(bih.at[1], ext1.at[:, pl.ds(2, 8)], sem.at[1]),
-        pltpu.make_async_copy(w1h.at[1], w1.at[1], sem.at[2]),
+        pltpu.make_async_copy(w2.at[pl.ds(1, 1)], w2o, sem.at[0]),
+        pltpu.make_async_copy(w1.at[pl.ds(1, 1)], w1o, sem.at[1]),
+        pltpu.make_async_copy(bi.at[1], bi1, sem.at[2]),
     ]
     for copy in copies:
         copy.start()
+    for copy in copies:
+        copy.wait()
+
+
+def early_kernel(v0, bi1, rin, rout, w2, w1, ga, ga23, d1, pre, ext, ext1):
     ext[:, 2:10] = v0[...]
     put_edges(ext, slice(0, 4), rin[0], rout[0])
-    copies[0].wait()
-    for t in range(2):
-        ga[t] = conv_back(ext, w2, 1, t, 0, 10)
+    for t in range(2):
+        ga[t] = conv_back(ext, w2, 0, t, 0, 10)
     for t, steps in ((0, (0, 1)), (1, (0,))):
-        ga23[t] = conv_back(ext, w2, 1, 2 + t, 1, 8, steps)
-    copies[1].wait()
-    copies[2].wait()
+        ga23[t] = conv_back(ext, w2, 0, 2 + t, 1, 8, steps)
+    ext1[:, 2:10] = bi1[...]
     put_edges(ext1, slice(0, 4), rin[1], rout[1])
     for t in range(2):
-        d1[t] = factor(conv_fore(ext1, w1, 1, t, 1, 8))
+        d1[t] = factor(conv_fore(ext1, w1, 0, t, 1, 8))
     for t, steps in ((0, (2,)), (1, (1, 2))):
-        pre[t] = conv_fore(ext1, w1, 1, t - 2, 0, 10, steps)
+        pre[t] = conv_fore(ext1, w1, 0, t - 2, 0, 10, steps)
 
 
 def pre01_kernel(bx, dpi, dpo, ga, pre, w1, v1x, ext):
@@ -249,8 +252,7 @@
         v3[t] = (conv_back(ext, w2, 0, t, 1, 8) * d[t]).astype(BF)
     p = side()
     for t in range(2):
-        ein[t], eout[t] = v3x[t, 1 + 7 * (1 - p)], v3x[t, 1 + 7 * p]
-        ein[2 + t], eout[2 + t] = v3[t, 7 * (1 - p)], v3[t, 7 * p]
+        ein[t], eout[t] = v3[t, 7 * (1 - p)], v3[t, 7 * p]
 
 
 def row_pairs(up):
@@ -258,26 +260,47 @@
     return up[:, 0] + up[:, 1]
 
 
-def last01_kernel(v3x, v3, rin, rout, v2x, v2, w1, pool, part, ext):
-    p = side()
+def inner_last_kernel(v3x, v3, v2x, v2, w1, base, ext):
     ext[0:2, 1:11] = v3x[...]
     ext[2:4, 2:10] = v3[...]
+    ext[2:4, 1:2] = jnp.zeros((2, 1, COLS, C), BF)
+    ext[2:4, 10:11] = jnp.zeros((2, 1, COLS, C), BF)
+    for t in range(2):
+        base[t] = v2x[t, 1:9].astype(F32) + conv_back(ext, w1, 0, t, 1, 8)
+    for t, steps in ((0, (0, 1)), (1, (0,))):
+        base[2 + t] = v2[t].astype(F32) + conv_back(ext, w1, 0, 2 + t, 1, 8, steps)
+
+
+def edge_rows(halo, w, layer, dr):
+    zero = jnp.zeros((COLS, C), BF)
+    frames = [zero, zero, halo[0], halo[1], zero, zero]
+    lhs = [jnp.concatenate(frames[t : t + 3], axis=1) for t in range(4)]
+    rhs = [
+        jnp.concatenate([w[layer, 2 - dt, 2 - dr, 2 - j] for j in range(3)], axis=0)
+        for dt in range(3)
+    ]
+    out = lax.dot_general(
+        jnp.concatenate(lhs, axis=0),
+        jnp.concatenate(rhs, axis=1),
+        (((1,), (1,)), ((), ())),
+        preferred_element_type=F32,
+    )
+    return shift_add(out).reshape(4, 1, COLS, C)
+
+
+def last_kernel(base, rin, rout, vxr, owner, w1, out, ext, rows):
+    ext[2:4, 1:11] = with_later(vxr[...])
+    low, near = side() == 1, rin[...]
+    far = inside(rout[...])
+    top = edge_rows(jnp.where(low, near, far), w1, 0, 0)
+    bottom = edge_rows(jnp.where(low, far, near), w1, 0, 2)
+    more = [0.0, 0.0, *later_part(ext, w1, 0)]
     for t in range(4):
-        ext[t, 10 - 9 * p] = rin[t]
-        ext[t, 1 + 9 * p] = inside(rout[t])
-    for t in range(2):
-        pool[t] = row_pairs(v2x[t, 1:9].astype(F32) + conv_back(ext, w1, 0, t, 1, 8))
-    for t, steps in ((0, (0, 1)), (1, (0,))):
-        part[t] = v2[t].astype(F32) + conv_back(ext, w1, 0, 2 + t, 1, 8, steps)
-
-
-def last23_kernel(vxr, pool, part, owner, w1, out, ext, rows):
-    ext[2:4, 1:11] = with_later(vxr[...])
-    half = 2 * 4 * COLS
-    rows[0:half] = pool[...].reshape(half, C)
-    for t, more in enumerate(later_part(ext, w1, 0)):
-        pair = row_pairs(part[t] + more)
-        rows[half + t * 4 * COLS : half + (t + 1) * 4 * COLS] = pair.reshape(4 * COLS, C)
+        whole = jnp.concatenate(
+            [base[t, 0:1] + top[t], base[t, 1:7], base[t, 7:8] + bottom[t]], axis=0
+        )
+        pair = row_pairs(whole + more[t])
+        rows[t * 4 * COLS : (t + 1) * 4 * COLS] = pair.reshape(4 * COLS, C)
     units = owner.shape[1]
     strips, capacity = out.shape[0], out.shape[1]
     slots = strips * capacity
@@ -379,19 +402,21 @@
     rout, rin = swap_out(rout), swap_in(rin)
     dpo, dpi = corner(dpo, sooner, outer_pairs), corner(dpi, sooner, inner_pairs)
     v0x = from_later(run(extend_kernel, field(2, 10), (v0, rin, rout), 1, scratch=[]))
+    taps = jax.ShapeDtypeStruct((1, *w1.shape[1:]), BF)
+    bi1, w2late, w1late = run(
+        fetch_kernel,
+        [field(4, 8), taps, taps],
+        (v0, in_hbm(bi), in_hbm(w2), in_hbm(w1)),
+        1,
+        scratch=[pltpu.SemaphoreType.DMA((3,))],
+        in_specs=[VM, HB, HB, HB],
+    )
     ga, ga23, d1, pre = run(
         early_kernel,
         [ten, eight, eight, ten],
-        (v0, in_hbm(bi), rin, rout, in_hbm(w2), in_hbm(w1)),
+        (v0, bi1, rin, rout, w2late, w1late),
         54,
-        scratch=[
-            ext,
-            ext,
-            pltpu.VMEM(w2.shape, BF),
-            pltpu.VMEM(w1.shape, BF),
-            pltpu.SemaphoreType.DMA((3,)),
-        ],
-        in_specs=[VM, HB, VM, VM, HB, HB],
+        scratch=[ext, ext],
     )
     v1x = run(
         pre01_kernel,
@@ -424,21 +449,16 @@
     )
     v3x = run(grad01_kernel, field(2, 10), (v2x, v2, r2in, r2out, d0a, w2), 20)
     v3xr = from_later(v3x)
-    v3, ein, eout = run(grad23_kernel, [field(2, 8), field(4), field(4)], (v2, r2in, r2out, v2xr, d0, v3x, w2), 16)
+    v3, ein, eout = run(grad23_kernel, [field(2, 8), field(2), field(2)], (v2, r2in, r2out, v2xr, d0, v3x, w2), 16)
     r3out, r3in = swap_out(eout), swap_in(ein)
-    pool, part = run(
-        last01_kernel,
-        [field(2, 4, dtype=F32), eight],
-        (v3x, v3, r3in, r3out, v2x, v2, w1),
-        24,
-    )
+    base = run(inner_last_kernel, field(4, 8, dtype=F32), (v3x, v3, v2x, v2, w1), 24)
     owner = owner_map.reshape(1, -1)
     units = owner.shape[1]
     capacity = max(2, 2 * units // strips)
     outgoing = run(
-        last23_kernel,
+        last_kernel,
         jax.ShapeDtypeStruct((strips, capacity, 8 * C), BF),
-        (v3xr, pool, part, owner, w1),
+        (base, r3in, r3out, v3xr, owner, w1),
         8,
         scratch=[ext, pltpu.VMEM((4 * 4 * COLS, C), F32)],
     )

time: 78.3 us -> 75.6 us (0.966)
  waiting for transfers between devices: 9 us -> 7.07 us
    ppermute x4, starting transfers between devices: 14.1 us -> 12 us  [swap_in(): return lax.ppermute(x, 'space', inner_pairs)]
    ppermute x4, starting transfers between devices: 3.94 us -> 5.38 us  [from_later(): return lax.ppermute(x, 'tm', later)]
    ppermute x4, waiting for transfers between devices: 1.89 us -> 0.57 us  [swap_in(): return lax.ppermute(x, 'space', inner_pairs)]
    pallas_call x13 -> x14, Pallas kernels: 22.5 us -> 23 us  [run(): pl.pallas_call(kernel, out_shape=outs, in_specs=in_specs or [VM] * len(ar...]
  transfers between devices with their start and end apart: 16 -> 16, of which waited for: 5 -> 5; matrix products, arithmetic and copies ran while one was open for 0% -> 0% of each run, Pallas kernels for 25% -> 27%
where the time goes in v3:
time: 75.6 us; the launch traced here: 75.4 us
  starting transfers between devices  28 us (37%)
  Pallas kernels  23 us (30%)
  blocking collectives  16.4 us (22%)
  waiting for transfers between devices  7.07 us (9%)
    pallas_call x14, Pallas kernels, run(): pl.pallas_call(kernel, out_shape=outs, in_specs=in_specs or [VM] * len(ar...  23 us
    all_to_all x1, blocking collectives, on_device(): lax.all_to_all(outgoing, 'space', split_axis=0, concat_axis=0, tiled=True)  16.4 us
    ppermute x4, starting transfers between devices, swap_in(): return lax.ppermute(x, 'space', inner_pairs)  12 us
    ppermute x2, starting transfers between devices, corner(): return lax.ppermute(x, ('tm', 'space'), route)  6.37 us
    ppermute x4, waiting for transfers between devices, swap_out(): return lax.ppermute(x, 'space', outer_pairs)  6.11 us
    ppermute x4, starting transfers between devices, from_later(): return lax.ppermute(x, 'tm', later)  5.38 us
    ppermute x4, starting transfers between devices, swap_out(): return lax.ppermute(x, 'space', outer_pairs)  2.13 us
    ppermute x2, starting transfers between devices, from_sooner(): return lax.ppermute(x, 'tm', sooner)  2.12 us
  transfers between devices with their start and end apart: 16, of which 5 were waited for; matrix products, arithmetic and copies ran while one was open for 0% of the time, Pallas kernels for 27%

profile of v3, /device:TPU:1, one launch (start us, length us, event | category | flops | bytes accessed | tf_op | source)
XLA Modules:
  0.0 75.4 jit_solution(1906614315220984321)
XLA Ops:
  0.0 1.5 %start_kernel.1 = (bf16[4,8,64,128]{3,2,1,0:T(8,128)(2,1)S(1)}, bf16[3,4,2,64,128]{4,3,2,1,0:T(8,128)(2,1)S(1)}, bf16[3,4,2,64,128]{4,3,2,1,0:T(8,128)(2,1)S(1)}...) custom-call(bf16[4,8,64,128]{3,2,1,0:T(8,128)(2,1)} %cot.1, ...), custom_call_target="tpu_custom_call" | custom-call | flops 56623104 | bytes 1572896 | tf_op jit(solution)/shard_map/start_kernel/pallas_call | solution.py:337
  1.5 1.5 %collective-permute-start.3 = (bf16[3,4,2,64,128]{4,3,2,1,0:T(8,128)(2,1)S(1)}, bf16[3,4,2,64,128]{4,3,2,1,0:T(8,128)(2,1)S(1)}, u32[]{:S(2)}, u32[]{:S(2)}) collective-permute-start(bf16[3,4,2,64,128]{4,3,2,1,0:T(8,128)(2,1)S(1)} %get-tuple-element.34), channel_id=1, source_target_pairs={{0,1},{1,0},{2,3},{3,2},{4,5},{5,4},{6,7},{7,6},{8,9},{9,8},{10,11... | collective-permute-start | bytes 1179656 | tf_op jit(solution)/shard_map/ppermute | solution.py:364
  3.0 1.7 %collective-permute-start.4 = (bf16[3,4,2,64,128]{4,3,2,1,0:T(8,128)(2,1)S(1)}, bf16[3,4,2,64,128]{4,3,2,1,0:T(8,128)(2,1)S(1)}, u32[]{:S(2)}, u32[]{:S(2)}) collective-permute-start(bf16[3,4,2,64,128]{4,3,2,1,0:T(8,128)(2,1)S(1)} %get-tuple-element.35), channel_id=1, source_target_pairs={{0,31},{1,2},{2,1},{3,4},{4,3},{5,6},{6,5},{7,8},{8,7},{9,10},{10,... | collective-permute-start | bytes 1179656 | tf_op jit(solution)/shard_map/ppermute | solution.py:367
  4.7 1.2 %collective-permute-start = (bf16[2,8,64,128]{3,2,1,0:T(8,128)(2,1)S(1)}, bf16[2,8,64,128]{3,2,1,0:T(8,128)(2,1)S(1)}, u32[]{:S(2)}, u32[]{:S(2)}) collective-permute-start(bf16[2,8,64,128]{3,2,1,0:T(8,128)(2,1)S(1)} %get-tuple-element.29), channel_id=1, source_target_pairs={{0,32},{32,64},{64,96},{96,0},{1,33},{33,65},{65,97},{97,1},{2,34}... | collective-permute-start | bytes 786440 | tf_op jit(solution)/shard_map/ppermute | solution.py:377
  5.9 6.4 %collective-permute-start.1 = (bf16[2,2,64,128]{3,2,1,0:T(8,128)(2,1)S(1)}, bf16[2,2,64,128]{3,2,1,0:T(8,128)(2,1)S(1)}, u32[]{:S(2)}, u32[]{:S(2)}) collective-permute-start(bf16[2,2,64,128]{3,2,1,0:T(8,128)(2,1)S(1)} %get-tuple-element.30), channel_id=1, source_target_pairs={{0,33},{1,32},{2,35},{3,34},{4,37},{5,36},{6,39},{7,38},{8,41},{9,... | collective-permute-start | bytes 196616 | tf_op jit(solution)/shard_map/ppermute | solution.py:374
  12.3 0.0 collective-permute-start.2
  12.3 1.6 %fetch_kernel.1 = (bf16[4,8,64,128]{3,2,1,0:T(8,128)(2,1)S(1)}, bf16[1,3,3,3,128,128]{5,4,3,2,1,0:T(8,128)(2,1)S(1)}, bf16[1,3,3,3,128,128]{5,4,3,2,1,0:T(8,128)(2,1)S(1)}) custom-call(bf16[4,8,64,128]{3,2,1,0:T(8,128)(2,1)S(1)} %get-tuple-element.32.after.v0, bf16[2,4,8,64,128]{4,3,2,1,0:T(8,128)(2,1)} %bi.7, bf16[2,3,3,3,128,128]{5,4,3,2,1,0:T(8,128)(2,1)} %w2.7, ...), custom_call_target="tpu_custom_call" | custom-call | flops 56623104 | bytes 5111808 | tf_op jit(solution)/shard_map/fetch_kernel/pallas_call | solution.py:337
  13.9 0.0 collective-permute-done.3.rin.r0in
  13.9 0.0 collective-permute-done.4.rout.r0out
  14.0 1.5 %collective-permute-start.5 = (bf16[2,10,64,128]{3,2,1,0:T(8,128)(2,1)S(1)}, bf16[2,10,64,128]{3,2,1,0:T(8,128)(2,1)S(1)}, u32[]{:S(2)}, u32[]{:S(2)}) collective-permute-start(bf16[2,10,64,128]{3,2,1,0:T(8,128)(2,1)S(1)} %extend_kernel.1), channel_id=1, source_target_pairs={{32,0},{64,32},{96,64},{0,96},{33,1},{65,33},{97,65},{1,97},{34,2}... | collective-permute-start | bytes 983048 | tf_op jit(solution)/shard_map/ppermute | solution.py:370
  15.5 4.6 %early_kernel.1 = (f32[2,10,64,128]{3,2,1,0:T(8,128)S(1)}, f32[2,8,64,128]{3,2,1,0:T(8,128)S(1)}, f32[2,8,64,128]{3,2,1,0:T(8,128)S(1)}, f32[2,10,64,128]{3,2,1,0:T(8,128)S(1)}) custom-call(bf16[4,8,64,128]{3,2,1,0:T(8,128)(2,1)S(1)} %get-tuple-element.32.after.v0, bf16[4,8,64,128]{3,2,1,0:T(8,128)(2,1)S(1)} %get-tuple-element.33.bi1, ...), custom_call_target="tpu_custom_call" | custom-call | flops 3057647616 | bytes 3604480 | tf_op jit(solution)/shard_map/early_kernel/pallas_call | solution.py:337
  20.1 0.0 collective-permute-done.1.dpi
  20.2 0.0 collective-permute-done.2.dpo
  20.2 0.0 collective-permute-done.bx
  20.2 0.0 copy-start.1
  20.2 1.1 %pre01_kernel.1.v1x = bf16[2,10,64,128]{3,2,1,0:T(8,128)(2,1)S(1)} custom-call(bf16[2,8,64,128]{3,2,1,0:T(8,128)(2,1)S(1)} %collective-permute-done.bx, bf16[2,2,64,128]{3,2,1,0:T(8,128)(2,1)S(1)} %collective-permute-done.1.dpi, bf16[2,2,64,128]{3,2,1,0:T(8,128)(2,1)S(1)} %collective-permute-done.2.dpo, f32[2,10,64,128]{3,2,1,0:T(8,128)S(1)} %get-tuple-element.38.ga, ...), custom_call_target="tpu_custom_call" | custom-call | flops 566231040 | bytes 3473408 | tf_op jit(solution)/shard_map/pre01_kernel/pallas_call | solution.py:337
  21.3 0.0 copy-start.2
  21.3 0.3 collective-permute-start.8
  21.6 0.4 collective-permute-done.5.vx
  22.0 0.9 %pre23_kernel.1 = (bf16[2,8,64,128]{3,2,1,0:T(8,128)(2,1)S(1)}, bf16[4,2,64,128]{3,2,1,0:T(8,128)(2,1)S(1)}, bf16[4,2,64,128]{3,2,1,0:T(8,128)(2,1)S(1)}) custom-call(f32[2,8,64,128]{3,2,1,0:T(8,128)S(1)} %get-tuple-element.40.ga23, bf16[2,10,64,128]{3,2,1,0:T(8,128)(2,1)S(1)} %collective-permute-done.5.vx, f32[2,8,64,128]{3,2,1,0:T(8,128)S(1)} %get-tuple-element.41.d, ...), custom_call_target="tpu_custom_call" | custom-call | flops 452984832 | bytes 3473408 | tf_op jit(solution)/shard_map/pre23_kernel/pallas_call | solution.py:337
  22.9 0.9 %collective-permute-start.11 = (bf16[2,12,64,128]{3,2,1,0:T(8,128)(2,1)S(1)}, bf16[2,12,64,128]{3,2,1,0:T(8,128)(2,1)S(1)}, u32[]{:S(2)}, u32[]{:S(2)}) collective-permute-start(bf16[2,12,64,128]{3,2,1,0:T(8,128)(2,1)S(1)} %extend0_kernel.1), channel_id=1, source_target_pairs={{0,32},{32,64},{64,96},{96,0},{1,33},{33,65},{65,97},{97,1},{2,34}... | collective-permute-start | bytes 1179656 | tf_op jit(solution)/shard_map/ppermute | solution.py:377
  23.8 3.1 %collective-permute-start.6 = (bf16[4,2,64,128]{3,2,1,0:T(8,128)(2,1)S(1)}, bf16[4,2,64,128]{3,2,1,0:T(8,128)(2,1)S(1)}, u32[]{:S(2)}, u32[]{:S(2)}) collective-permute-start(bf16[4,2,64,128]{3,2,1,0:T(8,128)(2,1)S(1)} %get-tuple-element.43), channel_id=1, source_target_pairs={{0,1},{1,0},{2,3},{3,2},{4,5},{5,4},{6,7},{7,6},{8,9},{9,8},{10,11... | collective-permute-start | bytes 393224 | tf_op jit(solution)/shard_map/ppermute | solution.py:364
  26.9 0.4 collective-permute-start.7
  27.3 0.6 collective-permute-done.6.rin
  27.9 3.7 %collective-permute-done.7.rout = bf16[4,2,64,128]{3,2,1,0:T(8,128)(2,1)S(1)} collective-permute-done((bf16[4,2,64,128]{3,2,1,0:T(8,128)(2,1)S(1)}, bf16[4,2,64,128]{3,2,1,0:T(8,128)(2,1)S(1)}, u32[]{:S(2)}, u32[]{:S(2)}) %collective-permute-start.7) | collective-permute-done | bytes 131104 | tf_op jit(solution)/shard_map/ppermute | solution.py:367
  31.6 1.8 %up01_kernel.1.v2x = bf16[2,10,64,128]{3,2,1,0:T(8,128)(2,1)S(1)} custom-call(bf16[2,10,64,128]{3,2,1,0:T(8,128)(2,1)S(1)} %pre01_kernel.1.v1x, bf16[2,8,64,128]{3,2,1,0:T(8,128)(2,1)S(1)} %get-tuple-element.42.v1.after, bf16[4,2,64,128]{3,2,1,0:T(8,128)(2,1)S(1)} %collective-permute-done.6.rin, bf16[4,2,64,128]{3,2,1,0:T(8,128)(2,1)S(1)} %collective-permute-done.7.rout, ...), custom_call_target="tpu_custom_call" | custom-call | flops 1132462080 | bytes 3932160 | tf_op jit(solution)/shard_map/up01_kernel/pallas_call | solution.py:337
  33.4 1.9 %collective-permute-start.12 = (bf16[2,10,64,128]{3,2,1,0:T(8,128)(2,1)S(1)}, bf16[2,10,64,128]{3,2,1,0:T(8,128)(2,1)S(1)}, u32[]{:S(2)}, u32[]{:S(2)}) collective-permute-start(bf16[2,10,64,128]{3,2,1,0:T(8,128)(2,1)S(1)} %up01_kernel.1.v2x), channel_id=1, source_target_pairs={{32,0},{64,32},{96,64},{0,96},{33,1},{65,33},{97,65},{1,97},{34,2}... | collective-permute-start | bytes 983048 | tf_op jit(solution)/shard_map/ppermute | solution.py:370
  35.3 0.0 collective-permute-done.8.vxr
  35.3 1.5 %up23_kernel.1 = (bf16[2,8,64,128]{3,2,1,0:T(8,128)(2,1)S(1)}, bf16[4,2,64,128]{3,2,1,0:T(8,128)(2,1)S(1)}, bf16[4,2,64,128]{3,2,1,0:T(8,128)(2,1)S(1)}) custom-call(bf16[2,8,64,128]{3,2,1,0:T(8,128)(2,1)S(1)} %get-tuple-element.42.v1.after, bf16[4,2,64,128]{3,2,1,0:T(8,128)(2,1)S(1)} %collective-permute-done.6.rin, ...), custom_call_target="tpu_custom_call" | custom-call | flops 905969664 | bytes 3473408 | tf_op jit(solution)/shard_map/up23_kernel/pallas_call | solution.py:337
  36.8 3.7 %collective-permute-start.9 = (bf16[4,2,64,128]{3,2,1,0:T(8,128)(2,1)S(1)}, bf16[4,2,64,128]{3,2,1,0:T(8,128)(2,1)S(1)}, u32[]{:S(2)}, u32[]{:S(2)}) collective-permute-start(bf16[4,2,64,128]{3,2,1,0:T(8,128)(2,1)S(1)} %get-tuple-element.46), channel_id=1, source_target_pairs={{0,1},{1,0},{2,3},{3,2},{4,5},{5,4},{6,7},{7,6},{8,9},{9,8},{10,11... | collective-permute-start | bytes 393224 | tf_op jit(solution)/shard_map/ppermute | solution.py:364
  40.5 0.0 collective-permute-start.10
  40.5 0.0 collective-permute-done.11.bx
  40.5 3.1 %factor_kernel.1 = (f32[2,10,64,128]{3,2,1,0:T(8,128)S(1)}, f32[2,8,64,128]{3,2,1,0:T(8,128)S(1)}) custom-call(bf16[2,4,8,64,128]{4,3,2,1,0:T(8,128)(2,1)S(1)} %copy-done.2, bf16[3,4,2,64,128]{4,3,2,1,0:T(8,128)(2,1)S(1)} %collective-permute-done.3.rin.r0in, bf16[3,4,2,64,128]{4,3,2,1,0:T(8,128)(2,1)S(1)} %collective-permute-done.4.rout.r0out, ...), custom_call_target="tpu_custom_call" | custom-call | flops 2038431744 | bytes 4259840 | tf_op jit(solution)/shard_map/factor_kernel/pallas_call | solution.py:337
  43.6 0.0 collective-permute-done.9.rin
  43.6 1.2 %collective-permute-done.10.rout = bf16[4,2,64,128]{3,2,1,0:T(8,128)(2,1)S(1)} collective-permute-done((bf16[4,2,64,128]{3,2,1,0:T(8,128)(2,1)S(1)}, bf16[4,2,64,128]{3,2,1,0:T(8,128)(2,1)S(1)}, u32[]{:S(2)}, u32[]{:S(2)}) %collective-permute-start.10) | collective-permute-done | bytes 131104 | tf_op jit(solution)/shard_map/ppermute | solution.py:367
  44.9 1.8 %grad01_kernel.1.v3x = bf16[2,10,64,128]{3,2,1,0:T(8,128)(2,1)S(1)} custom-call(bf16[2,10,64,128]{3,2,1,0:T(8,128)(2,1)S(1)} %up01_kernel.1.v2x, bf16[2,8,64,128]{3,2,1,0:T(8,128)(2,1)S(1)} %get-tuple-element.45.after.v2, bf16[4,2,64,128]{3,2,1,0:T(8,128)(2,1)S(1)} %collective-permute-done.9.rin, bf16[4,2,64,128]{3,2,1,0:T(8,128)(2,1)S(1)} %collective-permute-done.10.rout, ...), custom_call_target="tpu_custom_call" | custom-call | flops 1132462080 | bytes 3276800 | tf_op jit(solution)/shard_map/grad01_kernel/pallas_call | solution.py:337
  46.7 1.6 %collective-permute-start.15 = (bf16[2,10,64,128]{3,2,1,0:T(8,128)(2,1)S(1)}, bf16[2,10,64,128]{3,2,1,0:T(8,128)(2,1)S(1)}, u32[]{:S(2)}, u32[]{:S(2)}) collective-permute-start(bf16[2,10,64,128]{3,2,1,0:T(8,128)(2,1)S(1)} %grad01_kernel.1.v3x), channel_id=1, source_target_pairs={{32,0},{64,32},{96,64},{0,96},{33,1},{65,33},{97,65},{1,97},{34,2}... | collective-permute-start | bytes 983048 | tf_op jit(solution)/shard_map/ppermute | solution.py:370
  48.3 0.0 collective-permute-done.12.vxr
  48.3 1.5 %grad23_kernel.1 = (bf16[2,8,64,128]{3,2,1,0:T(8,128)(2,1)S(1)}, bf16[2,64,128]{2,1,0:T(8,128)(2,1)S(1)}, bf16[2,64,128]{2,1,0:T(8,128)(2,1)S(1)}) custom-call(bf16[2,8,64,128]{3,2,1,0:T(8,128)(2,1)S(1)} %get-tuple-element.45.after.v2, bf16[4,2,64,128]{3,2,1,0:T(8,128)(2,1)S(1)} %collective-permute-done.9.rin, ...), custom_call_target="tpu_custom_call" | custom-call | flops 905969664 | bytes 3473408 | tf_op jit(solution)/shard_map/grad23_kernel/pallas_call | solution.py:337
  49.8 3.8 %collective-permute-start.13 = (bf16[2,64,128]{2,1,0:T(8,128)(2,1)S(1)}, bf16[2,64,128]{2,1,0:T(8,128)(2,1)S(1)}, u32[]{:S(2)}, u32[]{:S(2)}) collective-permute-start(bf16[2,64,128]{2,1,0:T(8,128)(2,1)S(1)} %get-tuple-element.51), channel_id=1, source_target_pairs={{0,1},{1,0},{2,3},{3,2},{4,5},{5,4},{6,7},{7,6},{8,9},{9,8},{10,11... | collective-permute-start | bytes 98312 | tf_op jit(solution)/shard_map/ppermute | solution.py:364
  53.6 0.0 collective-permute-start.14
  53.6 2.1 %inner_last_kernel.1.base = f32[4,8,64,128]{3,2,1,0:T(8,128)S(1)} custom-call(bf16[2,10,64,128]{3,2,1,0:T(8,128)(2,1)S(1)} %grad01_kernel.1.v3x, bf16[2,8,64,128]{3,2,1,0:T(8,128)(2,1)S(1)} %get-tuple-element.50.v3, bf16[2,10,64,128]{3,2,1,0:T(8,128)(2,1)S(1)} %up01_kernel.1.v2x, bf16[2,8,64,128]{3,2,1,0:T(8,128)(2,1)S(1)} %get-tuple-element.45.after.v2, ...), custom_call_target="tpu_custom_call" | custom-call | flops 1358954496 | bytes 2949120 | tf_op jit(solution)/shard_map/inner_last_kernel/pallas_call | solution.py:337
  55.7 0.0 collective-permute-done.13.rin
  55.8 1.2 %collective-permute-done.14.rout = bf16[2,64,128]{2,1,0:T(8,128)(2,1)S(1)} collective-permute-done((bf16[2,64,128]{2,1,0:T(8,128)(2,1)S(1)}, bf16[2,64,128]{2,1,0:T(8,128)(2,1)S(1)}, u32[]{:S(2)}, u32[]{:S(2)}) %collective-permute-start.14) | collective-permute-done | bytes 32800 | tf_op jit(solution)/shard_map/ppermute | solution.py:367
  56.9 0.0 collective-permute-done.15.vxr
  56.9 1.4 %last_kernel.1 = bf16[32,4,1024]{2,1,0:T(4,128)(2,1)S(1)} custom-call(f32[4,8,64,128]{3,2,1,0:T(8,128)S(1)} %inner_last_kernel.1.base, bf16[2,64,128]{2,1,0:T(8,128)(2,1)S(1)} %collective-permute-done.13.rin, bf16[2,64,128]{2,1,0:T(8,128)(2,1)S(1)} %collective-permute-done.14.rout, bf16[2,10,64,128]{3,2,1,0:T(8,128)(2,1)S(1)} %collective-permute-done.15.vxr, ...), custom_call_target="tpu_custom_call" | custom-call | flops 452984832 | bytes 3211520 | tf_op jit(solution)/shard_map/last_kernel/pallas_call | solution.py:337
  58.3 16.4 %all_to_all.5 = bf16[32,4,1024]{2,1,0:T(4,128)(2,1)S(1)} all-to-all(bf16[32,4,1024]{2,1,0:T(4,128)(2,1)S(1)} %last_kernel.1), channel_id=1, replica_groups=mesh['tm'=4,'space'=32] {'space'}, dimensions={0} | all-to-all | bytes 524288 | tf_op jit(solution)/shard_map/all_to_all | solution.py:465
  74.7 0.7 copy.9
  (8 shorter events, 0.1 us)
Async XLA Ops:
  1.5 12.4 %collective-permute-start.3 = (bf16[3,4,2,64,128]{4,3,2,1,0:T(8,128)(2,1)S(1)}, bf16[3,4,2,64,128]{4,3,2,1,0:T(8,128)(2,1)S(1)}, u32[]{:S(2)}, u32[]{:S(2)}) collective-permute-start(bf16[3,4,2,64,128]{4,3,2,1,0:T(8,128)(2,1)S(1)} %get-tuple-element.34), channel_id=1, source_target_pairs={{0,1},{1,0},{2,3},{3,2},{4,5},{5,4},{6,7},{7,6},{8,9},{9,8},{10,11... | collective-permute-start | bytes 1179656 | tf_op jit(solution)/shard_map/ppermute | solution.py:364
  3.0 10.9 %collective-permute-start.4 = (bf16[3,4,2,64,128]{4,3,2,1,0:T(8,128)(2,1)S(1)}, bf16[3,4,2,64,128]{4,3,2,1,0:T(8,128)(2,1)S(1)}, u32[]{:S(2)}, u32[]{:S(2)}) collective-permute-start(bf16[3,4,2,64,128]{4,3,2,1,0:T(8,128)(2,1)S(1)} %get-tuple-element.35), channel_id=1, source_target_pairs={{0,31},{1,2},{2,1},{3,4},{4,3},{5,6},{6,5},{7,8},{8,7},{9,10},{10,... | collective-permute-start | bytes 1179656 | tf_op jit(solution)/shard_map/ppermute | solution.py:367
  4.7 15.4 %collective-permute-start = (bf16[2,8,64,128]{3,2,1,0:T(8,128)(2,1)S(1)}, bf16[2,8,64,128]{3,2,1,0:T(8,128)(2,1)S(1)}, u32[]{:S(2)}, u32[]{:S(2)}) collective-permute-start(bf16[2,8,64,128]{3,2,1,0:T(8,128)(2,1)S(1)} %get-tuple-element.29), channel_id=1, source_target_pairs={{0,32},{32,64},{64,96},{96,0},{1,33},{33,65},{65,97},{97,1},{2,34}... | collective-permute-start | bytes 786440 | tf_op jit(solution)/shard_map/ppermute | solution.py:377
  5.9 14.2 %collective-permute-start.1 = (bf16[2,2,64,128]{3,2,1,0:T(8,128)(2,1)S(1)}, bf16[2,2,64,128]{3,2,1,0:T(8,128)(2,1)S(1)}, u32[]{:S(2)}, u32[]{:S(2)}) collective-permute-start(bf16[2,2,64,128]{3,2,1,0:T(8,128)(2,1)S(1)} %get-tuple-element.30), channel_id=1, source_target_pairs={{0,33},{1,32},{2,35},{3,34},{4,37},{5,36},{6,39},{7,38},{8,41},{9,... | collective-permute-start | bytes 196616 | tf_op jit(solution)/shard_map/ppermute | solution.py:374
  12.3 7.9 %collective-permute-start.2 = (bf16[2,2,64,128]{3,2,1,0:T(8,128)(2,1)S(1)}, bf16[2,2,64,128]{3,2,1,0:T(8,128)(2,1)S(1)}, u32[]{:S(2)}, u32[]{:S(2)}) collective-permute-start(bf16[2,2,64,128]{3,2,1,0:T(8,128)(2,1)S(1)} %get-tuple-element.31), channel_id=1, source_target_pairs={{0,63},{1,34},{2,33},{3,36},{4,35},{5,38},{6,37},{7,40},{8,39},{9,... | collective-permute-start | bytes 196616 | tf_op jit(solution)/shard_map/ppermute | solution.py:374
  14.0 8.0 %collective-permute-start.5 = (bf16[2,10,64,128]{3,2,1,0:T(8,128)(2,1)S(1)}, bf16[2,10,64,128]{3,2,1,0:T(8,128)(2,1)S(1)}, u32[]{:S(2)}, u32[]{:S(2)}) collective-permute-start(bf16[2,10,64,128]{3,2,1,0:T(8,128)(2,1)S(1)} %extend_kernel.1), channel_id=1, source_target_pairs={{32,0},{64,32},{96,64},{0,96},{33,1},{65,33},{97,65},{1,97},{34,2}... | collective-permute-start | bytes 983048 | tf_op jit(solution)/shard_map/ppermute | solution.py:370
  15.5 4.7 %copy-start = (bf16[2,3,3,3,128,128]{5,4,3,2,1,0:T(8,128)(2,1)S(1)}, bf16[2,3,3,3,128,128]{5,4,3,2,1,0:T(8,128)(2,1)}, u32[]{:S(2)}) copy-start(bf16[2,3,3,3,128,128]{5,4,3,2,1,0:T(8,128)(2,1)} %w1.13) | copy-start | bytes 5308420
  20.2 1.8 %copy-start.1 = (bf16[2,3,3,3,128,128]{5,4,3,2,1,0:T(8,128)(2,1)S(1)}, bf16[2,3,3,3,128,128]{5,4,3,2,1,0:T(8,128)(2,1)}, u32[]{:S(2)}) copy-start(bf16[2,3,3,3,128,128]{5,4,3,2,1,0:T(8,128)(2,1)} %w2.7) | copy-start | bytes 5308420
  21.3 1.6 %copy-start.2 = (bf16[2,4,8,64,128]{4,3,2,1,0:T(8,128)(2,1)S(1)}, bf16[2,4,8,64,128]{4,3,2,1,0:T(8,128)(2,1)}, u32[]{:S(2)}) copy-start(bf16[2,4,8,64,128]{4,3,2,1,0:T(8,128)(2,1)} %bi.7) | copy-start | bytes 3145732
  21.3 14.0 %collective-permute-start.8 = (bf16[2,10,64,128]{3,2,1,0:T(8,128)(2,1)S(1)}, bf16[2,10,64,128]{3,2,1,0:T(8,128)(2,1)S(1)}, u32[]{:S(2)}, u32[]{:S(2)}) collective-permute-start(bf16[2,10,64,128]{3,2,1,0:T(8,128)(2,1)S(1)} %pre01_kernel.1.v1x), channel_id=1, source_target_pairs={{32,0},{64,32},{96,64},{0,96},{33,1},{65,33},{97,65},{1,97},{34,2}... | collective-permute-start | bytes 983048 | tf_op jit(solution)/shard_map/ppermute | solution.py:370
  22.9 17.6 %collective-permute-start.11 = (bf16[2,12,64,128]{3,2,1,0:T(8,128)(2,1)S(1)}, bf16[2,12,64,128]{3,2,1,0:T(8,128)(2,1)S(1)}, u32[]{:S(2)}, u32[]{:S(2)}) collective-permute-start(bf16[2,12,64,128]{3,2,1,0:T(8,128)(2,1)S(1)} %extend0_kernel.1), channel_id=1, source_target_pairs={{0,32},{32,64},{64,96},{96,0},{1,33},{33,65},{65,97},{97,1},{2,34}... | collective-permute-start | bytes 1179656 | tf_op jit(solution)/shard_map/ppermute | solution.py:377
  23.8 4.1 %collective-permute-start.6 = (bf16[4,2,64,128]{3,2,1,0:T(8,128)(2,1)S(1)}, bf16[4,2,64,128]{3,2,1,0:T(8,128)(2,1)S(1)}, u32[]{:S(2)}, u32[]{:S(2)}) collective-permute-start(bf16[4,2,64,128]{3,2,1,0:T(8,128)(2,1)S(1)} %get-tuple-element.43), channel_id=1, source_target_pairs={{0,1},{1,0},{2,3},{3,2},{4,5},{5,4},{6,7},{7,6},{8,9},{9,8},{10,11... | collective-permute-start | bytes 393224 | tf_op jit(solution)/shard_map/ppermute | solution.py:364
  26.9 4.7 %collective-permute-start.7 = (bf16[4,2,64,128]{3,2,1,0:T(8,128)(2,1)S(1)}, bf16[4,2,64,128]{3,2,1,0:T(8,128)(2,1)S(1)}, u32[]{:S(2)}, u32[]{:S(2)}) collective-permute-start(bf16[4,2,64,128]{3,2,1,0:T(8,128)(2,1)S(1)} %get-tuple-element.44), channel_id=1, source_target_pairs={{0,31},{1,2},{2,1},{3,4},{4,3},{5,6},{6,5},{7,8},{8,7},{9,10},{10,... | collective-permute-start | bytes 393224 | tf_op jit(solution)/shard_map/ppermute | solution.py:367
  33.4 14.9 %collective-permute-start.12 = (bf16[2,10,64,128]{3,2,1,0:T(8,128)(2,1)S(1)}, bf16[2,10,64,128]{3,2,1,0:T(8,128)(2,1)S(1)}, u32[]{:S(2)}, u32[]{:S(2)}) collective-permute-start(bf16[2,10,64,128]{3,2,1,0:T(8,128)(2,1)S(1)} %up01_kernel.1.v2x), channel_id=1, source_target_pairs={{32,0},{64,32},{96,64},{0,96},{33,1},{65,33},{97,65},{1,97},{34,2}... | collective-permute-start | bytes 983048 | tf_op jit(solution)/shard_map/ppermute | solution.py:370
  36.8 6.8 %collective-permute-start.9 = (bf16[4,2,64,128]{3,2,1,0:T(8,128)(2,1)S(1)}, bf16[4,2,64,128]{3,2,1,0:T(8,128)(2,1)S(1)}, u32[]{:S(2)}, u32[]{:S(2)}) collective-permute-start(bf16[4,2,64,128]{3,2,1,0:T(8,128)(2,1)S(1)} %get-tuple-element.46), channel_id=1, source_target_pairs={{0,1},{1,0},{2,3},{3,2},{4,5},{5,4},{6,7},{7,6},{8,9},{9,8},{10,11... | collective-permute-start | bytes 393224 | tf_op jit(solution)/shard_map/ppermute | solution.py:364
  40.5 4.4 %collective-permute-start.10 = (bf16[4,2,64,128]{3,2,1,0:T(8,128)(2,1)S(1)}, bf16[4,2,64,128]{3,2,1,0:T(8,128)(2,1)S(1)}, u32[]{:S(2)}, u32[]{:S(2)}) collective-permute-start(bf16[4,2,64,128]{3,2,1,0:T(8,128)(2,1)S(1)} %get-tuple-element.47), channel_id=1, source_target_pairs={{0,31},{1,2},{2,1},{3,4},{4,3},{5,6},{6,5},{7,8},{8,7},{9,10},{10,... | collective-permute-start | bytes 393224 | tf_op jit(solution)/shard_map/ppermute | solution.py:367
  46.7 10.2 %collective-permute-start.15 = (bf16[2,10,64,128]{3,2,1,0:T(8,128)(2,1)S(1)}, bf16[2,10,64,128]{3,2,1,0:T(8,128)(2,1)S(1)}, u32[]{:S(2)}, u32[]{:S(2)}) collective-permute-start(bf16[2,10,64,128]{3,2,1,0:T(8,128)(2,1)S(1)} %grad01_kernel.1.v3x), channel_id=1, source_target_pairs={{32,0},{64,32},{96,64},{0,96},{33,1},{65,33},{97,65},{1,97},{34,2}... | collective-permute-start | bytes 983048 | tf_op jit(solution)/shard_map/ppermute | solution.py:370
  49.8 5.9 %collective-permute-start.13 = (bf16[2,64,128]{2,1,0:T(8,128)(2,1)S(1)}, bf16[2,64,128]{2,1,0:T(8,128)(2,1)S(1)}, u32[]{:S(2)}, u32[]{:S(2)}) collective-permute-start(bf16[2,64,128]{2,1,0:T(8,128)(2,1)S(1)} %get-tuple-element.51), channel_id=1, source_target_pairs={{0,1},{1,0},{2,3},{3,2},{4,5},{5,4},{6,7},{7,6},{8,9},{9,8},{10,11... | collective-permute-start | bytes 98312 | tf_op jit(solution)/shard_map/ppermute | solution.py:364
  53.6 3.3 %collective-permute-start.14 = (bf16[2,64,128]{2,1,0:T(8,128)(2,1)S(1)}, bf16[2,64,128]{2,1,0:T(8,128)(2,1)S(1)}, u32[]{:S(2)}, u32[]{:S(2)}) collective-permute-start(bf16[2,64,128]{2,1,0:T(8,128)(2,1)S(1)} %get-tuple-element.52), channel_id=1, source_target_pairs={{0,31},{1,2},{2,1},{3,4},{4,3},{5,6},{6,5},{7,8},{8,7},{9,10},{10,... | collective-permute-start | bytes 98312 | tf_op jit(solution)/shard_map/ppermute | solution.py:367
  53.6 3.3 %copy-start.3 = (s32[1,1,64,1]{2,3,1,0:T(1,128)S(1)}, s32[1,1,64,1]{2,3,1,0:T(1,128)}, u32[]{:S(2)}) copy-start(s32[1,1,64,1]{2,3,1,0:T(1,128)} %param.13) | copy-start | bytes 772

commit v4 on v3

--- a/solution.py
+++ b/solution.py
@@ -34,12 +34,12 @@
     )
 
 
-def back_taps(lhs, w, layer, steps=(0, 1, 2)):
+def back_taps(lhs, w, layer, steps=(0, 1, 2), rows=(0, 1, 2)):
     rhs = jnp.concatenate(
         [
             jnp.concatenate([w[layer, 2 - dt, 2 - dr, 2 - j] for j in range(3)], axis=0)
             for dt in steps
-            for dr in range(3)
+            for dr in rows
         ],
         axis=1,
     )
@@ -100,12 +100,13 @@
     out[t, 9:10] = jnp.where(s == lax.axis_size("space") - 1, zero, value[9:10])
 
 
-def send_edges(first, late, rin, rout):
+def send_edges(first, late, ein, eout):
     p = side()
-    rin[0:2] = first[:, pl.ds(1 + 6 * (1 - p), 2)]
-    rout[0:2] = first[:, pl.ds(1 + 6 * p, 2)]
-    rin[2:4] = late[:, pl.ds(6 * (1 - p), 2)]
-    rout[2:4] = late[:, pl.ds(6 * p, 2)]
+    for t in range(2):
+        ein[t], eout[t] = first[t, 7 - 5 * p], first[t, 2 + 5 * p]
+        for k in range(2):
+            ein[2 + 2 * t + k] = late[t, 6 * (1 - p) + k]
+            eout[2 + 2 * t + k] = late[t, 6 * p + k]
 
 
 def start_kernel(
@@ -189,14 +190,19 @@
         store_ten(v1x, t, ga[t] * factor(whole))
 
 
-def factor_kernel(bi, rin, rout, bx, after, w1, da, d, ext):
+def factor01_kernel(bi, rin, rout, bx, after, w1, d, ext):
     ext[0:2] = with_sooner(bx[...])
-    ext[2:6, 2:10] = bi[0]
-    put_edges(ext, slice(2, 6), rin[2], rout[2])
-    for t in range(2):
-        da[t] = factor(conv_fore(ext, w1, 0, t, 0, 10))
-    for t in range(2):
-        d[t] = factor(conv_fore(ext, w1, 0, 2 + t, 1, 8))
+    ext[2:4, 2:10] = bi[0, 0:2]
+    put_edges(ext, slice(2, 4), rin[2, 0:2], rout[2, 0:2])
+    for t in range(2):
+        d[t] = factor(conv_fore(ext, w1, 0, t, 0, 10))
+
+
+def factor23_kernel(bi, rin, rout, after, w1, d, ext):
+    ext[:, 2:10] = bi[0]
+    put_edges(ext, slice(0, 4), rin[2], rout[2])
+    for t in range(2):
+        d[t] = factor(conv_fore(ext, w1, 0, t, 1, 8))
 
 
 def later_part(ext, w, layer):
@@ -212,44 +218,36 @@
     send_edges(v1x, v1, ein, eout)
 
 
-def local01(ext, vx, v, rin, rout):
-    ext[0:2, 1:11] = vx[...]
-    ext[2:4, 2:10] = v[...]
-    put_edges(ext, slice(0, 4), rin[...], rout[...])
-
-
-def local23(ext, v, rin, rout, vxr):
-    ext[0:2, 2:10] = v[...]
-    put_edges(ext, slice(0, 2), rin[2:4], rout[2:4])
+def up01_kernel(base01, rin, rout, w1, v2x):
+    top, bottom = rim_rows(*halos(rin, rout), w1, 1)
+    for t in range(2):
+        store_ten(v2x, t, ten_rows(base01, t, top, bottom))
+
+
+def grad01_kernel(base01, rin, rout, d, after, w2, v3x):
+    top, bottom = rim_rows(*halos(rin, rout), w2, 0)
+    for t in range(2):
+        store_ten(v3x, t, ten_rows(base01, t, top, bottom) * d[t])
+
+
+def whole23(base23, rin, rout, vxr, w, layer, ext):
     ext[2:4, 1:11] = with_later(vxr[...])
-
-
-def up01_kernel(v1x, v1, rin, rout, v0, r0in, r0out, w1, v2x, ext, old):
-    p = side()
-    local01(ext, v1x, v1, rin, rout)
-    old[:, 2:10] = v0[0:2]
-    put_edges(old, slice(0, 2), r0in[0, 0:2], r0out[0, 0:2])
-    for t in range(2):
-        store_ten(v2x, t, old[t, 1:11].astype(F32) + conv_back(ext, w1, 1, t, 0, 10))
-
-
-def grad01_kernel(v2x, v2, rin, rout, d, w2, v3x, ext):
-    local01(ext, v2x, v2, rin, rout)
-    for t in range(2):
-        store_ten(v3x, t, conv_back(ext, w2, 0, t, 0, 10) * d[t])
-
-
-def up23_kernel(v1, rin, rout, vxr, v0, v2x, w1, v2, ein, eout, ext):
-    local23(ext, v1, rin, rout, vxr)
-    for t in range(2):
-        v2[t] = (v0[2 + t].astype(F32) + conv_back(ext, w1, 1, t, 1, 8)).astype(BF)
+    above, below = halos(rin, rout)
+    top = edge_rows([above[3], above[5]], w, layer, 0, 2)
+    bottom = edge_rows([below[2], below[4]], w, layer, 2, 2)
+    more = later_part(ext, w, layer)
+    return [eight_rows(base23, t, top, bottom) + more[t] for t in range(2)]
+
+
+def up23_kernel(base23, rin, rout, vxr, v2x, w1, v2, ein, eout, ext):
+    for t, whole in enumerate(whole23(base23, rin, rout, vxr, w1, 1, ext)):
+        v2[t] = whole.astype(BF)
     send_edges(v2x, v2, ein, eout)
 
 
-def grad23_kernel(v2, rin, rout, vxr, d, v3x, w2, v3, ein, eout, ext):
-    local23(ext, v2, rin, rout, vxr)
-    for t in range(2):
-        v3[t] = (conv_back(ext, w2, 0, t, 1, 8) * d[t]).astype(BF)
+def grad23_kernel(base23, rin, rout, vxr, d, w2, v3, ein, eout, ext):
+    for t, whole in enumerate(whole23(base23, rin, rout, vxr, w2, 0, ext)):
+        v3[t] = (whole * d[t]).astype(BF)
     p = side()
     for t in range(2):
         ein[t], eout[t] = v3[t, 7 * (1 - p)], v3[t, 7 * p]
@@ -271,35 +269,88 @@
         base[2 + t] = v2[t].astype(F32) + conv_back(ext, w1, 0, 2 + t, 1, 8, steps)
 
 
-def edge_rows(halo, w, layer, dr):
+def edge_rows(halo, w, layer, dr, first=0):
     zero = jnp.zeros((COLS, C), BF)
     frames = [zero, zero, halo[0], halo[1], zero, zero]
-    lhs = [jnp.concatenate(frames[t : t + 3], axis=1) for t in range(4)]
-    rhs = [
-        jnp.concatenate([w[layer, 2 - dt, 2 - dr, 2 - j] for j in range(3)], axis=0)
-        for dt in range(3)
+    lhs = [jnp.concatenate(frames[t : t + 3], axis=1) for t in range(first, 4)]
+    out = back_taps(jnp.concatenate(lhs, axis=0), w, layer, rows=(dr,))
+    return out.reshape(4 - first, 1, COLS, C)
+
+
+def halos(rin, rout):
+    low, near, far = side() == 1, rin[...], inside(rout[...])
+    return jnp.where(low, near, far), jnp.where(low, far, near)
+
+
+def rim_rows(above, below, w, layer):
+    zero = jnp.zeros((COLS, C), BF)
+    up = [(above[0], zero), (above[1], zero), (above[2], above[3]), (above[4], above[5])]
+    down = [(zero, below[0]), (zero, below[1]), (below[2], below[3]), (below[4], below[5])]
+    tops, bottoms = [], []
+    for t in range(2):
+        three = range(t, t + 3)
+        tops += [
+            [x for f in three for x in up[f]],
+            [x for f in three for x in (up[f][1], zero)],
+        ]
+        bottoms += [
+            [x for f in three for x in (zero, down[f][0])],
+            [x for f in three for x in down[f]],
+        ]
+    out = []
+    for lines, rows in ((tops, (0, 1)), (bottoms, (1, 2))):
+        lhs = jnp.concatenate([jnp.concatenate(line, axis=1) for line in lines], axis=0)
+        out.append(back_taps(lhs, w, layer, rows=rows).reshape(2, 2, COLS, C))
+    return out
+
+
+def local_part(ext, vx, v, w, layer):
+    ext[0:2, 1:11] = vx[...]
+    ext[2:4, 2:10] = v[...]
+    for frames, edge in ((slice(0, 2), 1), (slice(2, 4), 2)):
+        ext[frames, 0:edge] = jnp.zeros((2, edge, COLS, C), BF)
+        ext[frames, 12 - edge : 12] = jnp.zeros((2, edge, COLS, C), BF)
+    first = [conv_back(ext, w, layer, t, 0, 10) for t in range(2)]
+    late = [
+        conv_back(ext, w, layer, 2 + t, 1, 8, steps) for t, steps in ((0, (0, 1)), (1, (0,)))
     ]
-    out = lax.dot_general(
-        jnp.concatenate(lhs, axis=0),
-        jnp.concatenate(rhs, axis=1),
-        (((1,), (1,)), ((), ())),
-        preferred_element_type=F32,
-    )
-    return shift_add(out).reshape(4, 1, COLS, C)
+    return first, late
+
+
+def inner_up_kernel(v1x, v1, v0, r0in, r0out, w1, base01, base23, ext, old):
+    old[:, 2:10] = v0[0:2]
+    put_edges(old, slice(0, 2), r0in[0, 0:2], r0out[0, 0:2])
+    first, late = local_part(ext, v1x, v1, w1, 1)
+    for t in range(2):
+        base01[t] = old[t, 1:11].astype(F32) + first[t]
+        base23[t] = v0[2 + t].astype(F32) + late[t]
+
+
+def inner_grad_kernel(v2x, v2, after, w2, base01, base23, ext):
+    first, late = local_part(ext, v2x, v2, w2, 0)
+    for t in range(2):
+        base01[t], base23[t] = first[t], late[t]
+
+
+def ten_rows(base, t, top, bottom):
+    return jnp.concatenate(
+        [base[t, 0:2] + top[t], base[t, 2:8], base[t, 8:10] + bottom[t]], axis=0
+    )
+
+
+def eight_rows(base, t, top, bottom):
+    return jnp.concatenate(
+        [base[t, 0:1] + top[t], base[t, 1:7], base[t, 7:8] + bottom[t]], axis=0
+    )
 
 
 def last_kernel(base, rin, rout, vxr, owner, w1, out, ext, rows):
     ext[2:4, 1:11] = with_later(vxr[...])
-    low, near = side() == 1, rin[...]
-    far = inside(rout[...])
-    top = edge_rows(jnp.where(low, near, far), w1, 0, 0)
-    bottom = edge_rows(jnp.where(low, far, near), w1, 0, 2)
+    above, below = halos(rin, rout)
+    top, bottom = edge_rows(above, w1, 0, 0), edge_rows(below, w1, 0, 2)
     more = [0.0, 0.0, *later_part(ext, w1, 0)]
     for t in range(4):
-        whole = jnp.concatenate(
-            [base[t, 0:1] + top[t], base[t, 1:7], base[t, 7:8] + bottom[t]], axis=0
-        )
-        pair = row_pairs(whole + more[t])
+        pair = row_pairs(eight_rows(base, t, top, bottom) + more[t])
         rows[t * 4 * COLS : (t + 1) * 4 * COLS] = pair.reshape(4 * COLS, C)
     units = owner.shape[1]
     strips, capacity = out.shape[0], out.shape[1]
@@ -381,7 +432,7 @@
     ext = pltpu.VMEM((4, 12, COLS, C), BF)
 
     ten, eight = field(2, 10, dtype=F32), field(2, 8, dtype=F32)
-    edges = [field(2, 8), field(4, 2), field(4, 2)]
+    edges = [field(2, 8), field(6), field(6)]
 
     v0, rin, rout, b1x, dpi, dpo = run(
         start_kernel,
@@ -430,26 +481,28 @@
     r1out, r1in = swap_out(eout), swap_in(ein)
     b0x = run(extend0_kernel, field(2, 12), (bi, rin, rout, v1), 1, scratch=[])
     b0x = from_sooner(b0x)
-    v2x = run(
-        up01_kernel,
-        field(2, 10),
-        (v1x, v1, r1in, r1out, v0, rin, rout, w1),
-        20,
+    base01, base23 = run(
+        inner_up_kernel,
+        [ten, eight],
+        (v1x, v1, v0, rin, rout, w1),
+        28,
         scratch=[ext, pltpu.VMEM((2, 12, COLS, C), BF)],
     )
+    v2x = run(up01_kernel, field(2, 10), (base01, r1in, r1out, w1), 8, scratch=[])
     v2xr = from_later(v2x)
-    v2, ein, eout = run(up23_kernel, edges, (v1, r1in, r1out, v1xr, v0, v2x, w1), 16)
+    v2, ein, eout = run(up23_kernel, edges, (base23, r1in, r1out, v1xr, v2x, w1), 10)
     r2out, r2in = swap_out(eout), swap_in(ein)
-    d0a, d0 = run(
-        factor_kernel,
-        [ten, eight],
-        (bi, rin, rout, b0x, v2, w1),
-        36,
-        scratch=[pltpu.VMEM((6, 12, COLS, C), BF)],
-    )
-    v3x = run(grad01_kernel, field(2, 10), (v2x, v2, r2in, r2out, d0a, w2), 20)
+    d0a = run(factor01_kernel, ten, (bi, rin, rout, b0x, v2, w1), 20)
+    base01, base23 = run(inner_grad_kernel, [ten, eight], (v2x, v2, d0a, w2), 28)
+    d0 = run(factor23_kernel, eight, (bi, rin, rout, base23, w1), 16)
+    v3x = run(grad01_kernel, field(2, 10), (base01, r2in, r2out, d0a, d0, w2), 8, scratch=[])
     v3xr = from_later(v3x)
-    v3, ein, eout = run(grad23_kernel, [field(2, 8), field(2), field(2)], (v2, r2in, r2out, v2xr, d0, v3x, w2), 16)
+    v3, ein, eout = run(
+        grad23_kernel,
+        [field(2, 8), field(2), field(2)],
+        (base23, r2in, r2out, v2xr, d0, w2),
+        10,
+    )
     r3out, r3in = swap_out(eout), swap_in(ein)
     base = run(inner_last_kernel, field(4, 8, dtype=F32), (v3x, v3, v2x, v2, w1), 24)
     owner = owner_map.reshape(1, -1)

time: 75.6 us -> 72 us (0.952)
  waiting for transfers between devices: 7.07 us -> 3.62 us
  Pallas kernels: 23 us -> 24.8 us
  starting transfers between devices: 28 us -> 26.9 us
  blocking collectives: 16.4 us -> 15.5 us
    ppermute x4, waiting for transfers between devices: 6.11 us -> 2.9 us  [swap_out(): return lax.ppermute(x, 'space', outer_pairs)]
    pallas_call x14 -> x17, Pallas kernels: 23 us -> 24.8 us  [run(): pl.pallas_call(kernel, out_shape=outs, in_specs=in_specs or [VM] * len(ar...]
    all_to_all x1, blocking collectives: 16.4 us -> 15.5 us  [on_device(): lax.all_to_all(outgoing, 'space', split_axis=0, concat_axis=0, tiled=True)]
    ppermute x4, starting transfers between devices: 12 us -> 11.2 us  [swap_in(): return lax.ppermute(x, 'space', inner_pairs)]
  transfers between devices with their start and end apart: 16 -> 16, of which waited for: 5 -> 3; matrix products, arithmetic and copies ran while one was open for 0% -> 0% of each run, Pallas kernels for 27% -> 29%
where the time goes in v4:
time: 72 us; the launch traced here: 71.7 us
  starting transfers between devices  26.9 us (37%)
  Pallas kernels  24.8 us (34%)
  blocking collectives  15.5 us (22%)
  waiting for transfers between devices  3.62 us (5%)
  local copies, waits for them, and re-layouts  0.72 us (1%)
    pallas_call x17, Pallas kernels, run(): pl.pallas_call(kernel, out_shape=outs, in_specs=in_specs or [VM] * len(ar...  24.8 us
    all_to_all x1, blocking collectives, on_device(): lax.all_to_all(outgoing, 'space', split_axis=0, concat_axis=0, tiled=True)  15.5 us
    ppermute x4, starting transfers between devices, swap_in(): return lax.ppermute(x, 'space', inner_pairs)  11.2 us
    ppermute x2, starting transfers between devices, corner(): return lax.ppermute(x, ('tm', 'space'), route)  6.37 us
    ppermute x4, starting transfers between devices, from_later(): return lax.ppermute(x, 'tm', later)  5.27 us
    ppermute x4, waiting for transfers between devices, swap_out(): return lax.ppermute(x, 'space', outer_pairs)  2.9 us
    ppermute x4, starting transfers between devices, swap_out(): return lax.ppermute(x, 'space', outer_pairs)  2.13 us
    ppermute x2, starting transfers between devices, from_sooner(): return lax.ppermute(x, 'tm', sooner)  1.9 us
  transfers between devices with their start and end apart: 16, of which 3 were waited for; matrix products, arithmetic and copies ran while one was open for 0% of the time, Pallas kernels for 29%

profile of v4, /device:TPU:1, one launch (start us, length us, event | category | flops | bytes accessed | tf_op | source)
XLA Modules:
  0.0 71.7 jit_solution(18220730599940954377)
XLA Ops:
  0.0 1.5 %start_kernel.1 = (bf16[4,8,64,128]{3,2,1,0:T(8,128)(2,1)S(1)}, bf16[3,4,2,64,128]{4,3,2,1,0:T(8,128)(2,1)S(1)}, bf16[3,4,2,64,128]{4,3,2,1,0:T(8,128)(2,1)S(1)}...) custom-call(bf16[4,8,64,128]{3,2,1,0:T(8,128)(2,1)} %cot.1, ...), custom_call_target="tpu_custom_call" | custom-call | flops 56623104 | bytes 1572896 | tf_op jit(solution)/shard_map/start_kernel/pallas_call | solution.py:388
  1.5 1.5 %collective-permute-start.3 = (bf16[3,4,2,64,128]{4,3,2,1,0:T(8,128)(2,1)S(1)}, bf16[3,4,2,64,128]{4,3,2,1,0:T(8,128)(2,1)S(1)}, u32[]{:S(2)}, u32[]{:S(2)}) collective-permute-start(bf16[3,4,2,64,128]{4,3,2,1,0:T(8,128)(2,1)S(1)} %get-tuple-element.36), channel_id=1, source_target_pairs={{0,1},{1,0},{2,3},{3,2},{4,5},{5,4},{6,7},{7,6},{8,9},{9,8},{10,11... | collective-permute-start | bytes 1179656 | tf_op jit(solution)/shard_map/ppermute | solution.py:415
  3.0 1.7 %collective-permute-start.4 = (bf16[3,4,2,64,128]{4,3,2,1,0:T(8,128)(2,1)S(1)}, bf16[3,4,2,64,128]{4,3,2,1,0:T(8,128)(2,1)S(1)}, u32[]{:S(2)}, u32[]{:S(2)}) collective-permute-start(bf16[3,4,2,64,128]{4,3,2,1,0:T(8,128)(2,1)S(1)} %get-tuple-element.37), channel_id=1, source_target_pairs={{0,31},{1,2},{2,1},{3,4},{4,3},{5,6},{6,5},{7,8},{8,7},{9,10},{10,... | collective-permute-start | bytes 1179656 | tf_op jit(solution)/shard_map/ppermute | solution.py:418
  4.7 1.2 %collective-permute-start = (bf16[2,8,64,128]{3,2,1,0:T(8,128)(2,1)S(1)}, bf16[2,8,64,128]{3,2,1,0:T(8,128)(2,1)S(1)}, u32[]{:S(2)}, u32[]{:S(2)}) collective-permute-start(bf16[2,8,64,128]{3,2,1,0:T(8,128)(2,1)S(1)} %get-tuple-element.31), channel_id=1, source_target_pairs={{0,32},{32,64},{64,96},{96,0},{1,33},{33,65},{65,97},{97,1},{2,34}... | collective-permute-start | bytes 786440 | tf_op jit(solution)/shard_map/ppermute | solution.py:428
  5.9 6.4 %collective-permute-start.1 = (bf16[2,2,64,128]{3,2,1,0:T(8,128)(2,1)S(1)}, bf16[2,2,64,128]{3,2,1,0:T(8,128)(2,1)S(1)}, u32[]{:S(2)}, u32[]{:S(2)}) collective-permute-start(bf16[2,2,64,128]{3,2,1,0:T(8,128)(2,1)S(1)} %get-tuple-element.32), channel_id=1, source_target_pairs={{0,33},{1,32},{2,35},{3,34},{4,37},{5,36},{6,39},{7,38},{8,41},{9,... | collective-permute-start | bytes 196616 | tf_op jit(solution)/shard_map/ppermute | solution.py:425
  12.3 0.0 collective-permute-start.2
  12.3 1.6 %fetch_kernel.1 = (bf16[4,8,64,128]{3,2,1,0:T(8,128)(2,1)S(1)}, bf16[1,3,3,3,128,128]{5,4,3,2,1,0:T(8,128)(2,1)S(1)}, bf16[1,3,3,3,128,128]{5,4,3,2,1,0:T(8,128)(2,1)S(1)}) custom-call(bf16[4,8,64,128]{3,2,1,0:T(8,128)(2,1)S(1)} %get-tuple-element.34.after.v0, bf16[2,4,8,64,128]{4,3,2,1,0:T(8,128)(2,1)} %bi.9, bf16[2,3,3,3,128,128]{5,4,3,2,1,0:T(8,128)(2,1)} %w2.9, ...), custom_call_target="tpu_custom_call" | custom-call | flops 56623104 | bytes 5111808 | tf_op jit(solution)/shard_map/fetch_kernel/pallas_call | solution.py:388
  13.9 0.0 collective-permute-done.3.rin.r0in
  13.9 0.0 collective-permute-done.4.rout.r0out
  14.0 1.5 %collective-permute-start.5 = (bf16[2,10,64,128]{3,2,1,0:T(8,128)(2,1)S(1)}, bf16[2,10,64,128]{3,2,1,0:T(8,128)(2,1)S(1)}, u32[]{:S(2)}, u32[]{:S(2)}) collective-permute-start(bf16[2,10,64,128]{3,2,1,0:T(8,128)(2,1)S(1)} %extend_kernel.1), channel_id=1, source_target_pairs={{32,0},{64,32},{96,64},{0,96},{33,1},{65,33},{97,65},{1,97},{34,2}... | collective-permute-start | bytes 983048 | tf_op jit(solution)/shard_map/ppermute | solution.py:421
  15.5 4.6 %early_kernel.1 = (f32[2,10,64,128]{3,2,1,0:T(8,128)S(1)}, f32[2,8,64,128]{3,2,1,0:T(8,128)S(1)}, f32[2,8,64,128]{3,2,1,0:T(8,128)S(1)}, f32[2,10,64,128]{3,2,1,0:T(8,128)S(1)}) custom-call(bf16[4,8,64,128]{3,2,1,0:T(8,128)(2,1)S(1)} %get-tuple-element.34.after.v0, bf16[4,8,64,128]{3,2,1,0:T(8,128)(2,1)S(1)} %get-tuple-element.35.bi1, ...), custom_call_target="tpu_custom_call" | custom-call | flops 3057647616 | bytes 3604480 | tf_op jit(solution)/shard_map/early_kernel/pallas_call | solution.py:388
  20.1 0.0 collective-permute-done.1.dpi
  20.2 0.0 collective-permute-done.2.dpo
  20.2 0.0 collective-permute-done.bx
  20.2 0.0 copy-start.1
  20.2 1.1 %pre01_kernel.1.v1x = bf16[2,10,64,128]{3,2,1,0:T(8,128)(2,1)S(1)} custom-call(bf16[2,8,64,128]{3,2,1,0:T(8,128)(2,1)S(1)} %collective-permute-done.bx, bf16[2,2,64,128]{3,2,1,0:T(8,128)(2,1)S(1)} %collective-permute-done.1.dpi, bf16[2,2,64,128]{3,2,1,0:T(8,128)(2,1)S(1)} %collective-permute-done.2.dpo, f32[2,10,64,128]{3,2,1,0:T(8,128)S(1)} %get-tuple-element.40.ga, ...), custom_call_target="tpu_custom_call" | custom-call | flops 566231040 | bytes 3473408 | tf_op jit(solution)/shard_map/pre01_kernel/pallas_call | solution.py:388
  21.3 0.0 copy-start.2
  21.3 0.7 collective-permute-done.5.vx
  22.0 0.9 %pre23_kernel.1 = (bf16[2,8,64,128]{3,2,1,0:T(8,128)(2,1)S(1)}, bf16[6,64,128]{2,1,0:T(8,128)(2,1)S(1)}, bf16[6,64,128]{2,1,0:T(8,128)(2,1)S(1)}) custom-call(f32[2,8,64,128]{3,2,1,0:T(8,128)S(1)} %get-tuple-element.42.ga23, bf16[2,10,64,128]{3,2,1,0:T(8,128)(2,1)S(1)} %collective-permute-done.5.vx, f32[2,8,64,128]{3,2,1,0:T(8,128)S(1)} %get-tuple-element.43.d, ...), custom_call_target="tpu_custom_call" | custom-call | flops 452984832 | bytes 3473408 | tf_op jit(solution)/shard_map/pre23_kernel/pallas_call | solution.py:388
  22.9 0.7 collective-permute-start.9
  23.6 2.1 %collective-permute-start.8 = (bf16[2,10,64,128]{3,2,1,0:T(8,128)(2,1)S(1)}, bf16[2,10,64,128]{3,2,1,0:T(8,128)(2,1)S(1)}, u32[]{:S(2)}, u32[]{:S(2)}) collective-permute-start(bf16[2,10,64,128]{3,2,1,0:T(8,128)(2,1)S(1)} %pre01_kernel.1.v1x), channel_id=1, source_target_pairs={{32,0},{64,32},{96,64},{0,96},{33,1},{65,33},{97,65},{1,97},{34,2}... | collective-permute-start | bytes 983048 | tf_op jit(solution)/shard_map/ppermute | solution.py:421
  25.7 2.8 %collective-permute-start.6 = (bf16[6,64,128]{2,1,0:T(8,128)(2,1)S(1)}, bf16[6,64,128]{2,1,0:T(8,128)(2,1)S(1)}, u32[]{:S(2)}, u32[]{:S(2)}) collective-permute-start(bf16[6,64,128]{2,1,0:T(8,128)(2,1)S(1)} %get-tuple-element.46), channel_id=1, source_target_pairs={{0,1},{1,0},{2,3},{3,2},{4,5},{5,4},{6,7},{7,6},{8,9},{9,8},{10,11... | collective-permute-start | bytes 294920 | tf_op jit(solution)/shard_map/ppermute | solution.py:415
  28.5 0.4 collective-permute-start.7
  28.9 2.5 %inner_up_kernel.1 = (f32[2,10,64,128]{3,2,1,0:T(8,128)S(1)}, f32[2,8,64,128]{3,2,1,0:T(8,128)S(1)}) custom-call(bf16[2,10,64,128]{3,2,1,0:T(8,128)(2,1)S(1)} %pre01_kernel.1.v1x, bf16[2,8,64,128]{3,2,1,0:T(8,128)(2,1)S(1)} %get-tuple-element.44.v1.after, bf16[4,8,64,128]{3,2,1,0:T(8,128)(2,1)S(1)} %get-tuple-element.34.after.v0, ...), custom_call_target="tpu_custom_call" | custom-call | flops 1585446912 | bytes 3670016 | tf_op jit(solution)/shard_map/inner_up_kernel/pallas_call | solution.py:388
  31.4 0.0 collective-permute-done.6.rin
  31.4 1.4 %collective-permute-done.7.rout = bf16[6,64,128]{2,1,0:T(8,128)(2,1)S(1)} collective-permute-done((bf16[6,64,128]{2,1,0:T(8,128)(2,1)S(1)}, bf16[6,64,128]{2,1,0:T(8,128)(2,1)S(1)}, u32[]{:S(2)}, u32[]{:S(2)}) %collective-permute-start.7) | collective-permute-done | bytes 98336 | tf_op jit(solution)/shard_map/ppermute | solution.py:418
  32.8 0.6 up01_kernel.1.v2x
  33.4 1.6 %collective-permute-start.12 = (bf16[2,10,64,128]{3,2,1,0:T(8,128)(2,1)S(1)}, bf16[2,10,64,128]{3,2,1,0:T(8,128)(2,1)S(1)}, u32[]{:S(2)}, u32[]{:S(2)}) collective-permute-start(bf16[2,10,64,128]{3,2,1,0:T(8,128)(2,1)S(1)} %up01_kernel.1.v2x), channel_id=1, source_target_pairs={{32,0},{64,32},{96,64},{0,96},{33,1},{65,33},{97,65},{1,97},{34,2}... | collective-permute-start | bytes 983048 | tf_op jit(solution)/shard_map/ppermute | solution.py:421
  35.0 0.0 collective-permute-done.8.vxr
  35.0 1.0 %up23_kernel.1 = (bf16[2,8,64,128]{3,2,1,0:T(8,128)(2,1)S(1)}, bf16[6,64,128]{2,1,0:T(8,128)(2,1)S(1)}, bf16[6,64,128]{2,1,0:T(8,128)(2,1)S(1)}) custom-call(f32[2,8,64,128]{3,2,1,0:T(8,128)S(1)} %get-tuple-element.48.base23, bf16[6,64,128]{2,1,0:T(8,128)(2,1)S(1)} %collective-permute-done.6.rin, bf16[6,64,128]{2,1,0:T(8,128)(2,1)S(1)} %collective-permute-done.7.rout, ...), custom_call_target="tpu_custom_call" | custom-call | flops 566231040 | bytes 3145728 | tf_op jit(solution)/shard_map/up23_kernel/pallas_call | solution.py:388
  36.0 3.4 %collective-permute-start.10 = (bf16[6,64,128]{2,1,0:T(8,128)(2,1)S(1)}, bf16[6,64,128]{2,1,0:T(8,128)(2,1)S(1)}, u32[]{:S(2)}, u32[]{:S(2)}) collective-permute-start(bf16[6,64,128]{2,1,0:T(8,128)(2,1)S(1)} %get-tuple-element.51), channel_id=1, source_target_pairs={{0,1},{1,0},{2,3},{3,2},{4,5},{5,4},{6,7},{7,6},{8,9},{9,8},{10,11... | collective-permute-start | bytes 294920 | tf_op jit(solution)/shard_map/ppermute | solution.py:415
  39.4 1.8 %factor01_kernel.1.after.d = f32[2,10,64,128]{3,2,1,0:T(8,128)S(1)} custom-call(bf16[2,4,8,64,128]{4,3,2,1,0:T(8,128)(2,1)S(1)} %copy-done.2, bf16[3,4,2,64,128]{4,3,2,1,0:T(8,128)(2,1)S(1)} %collective-permute-done.3.rin.r0in, bf16[3,4,2,64,128]{4,3,2,1,0:T(8,128)(2,1)S(1)} %collective-permute-done.4.rout.r0out, ...), custom_call_target="tpu_custom_call" | custom-call | flops 1132462080 | bytes 4259840 | tf_op jit(solution)/shard_map/factor01_kernel/pallas_call | solution.py:388
  41.3 2.5 %inner_grad_kernel.1 = (f32[2,10,64,128]{3,2,1,0:T(8,128)S(1)}, f32[2,8,64,128]{3,2,1,0:T(8,128)S(1)}) custom-call(bf16[2,10,64,128]{3,2,1,0:T(8,128)(2,1)S(1)} %up01_kernel.1.v2x, bf16[2,8,64,128]{3,2,1,0:T(8,128)(2,1)S(1)} %get-tuple-element.49.after.v2, f32[2,10,64,128]{3,2,1,0:T(8,128)S(1)} %factor01_kernel.1.after.d, ...), custom_call_target="tpu_custom_call" | custom-call | flops 1585446912 | bytes 3014656 | tf_op jit(solution)/shard_map/inner_grad_kernel/pallas_call | solution.py:388
  43.8 1.5 %factor23_kernel.1.after.d = f32[2,8,64,128]{3,2,1,0:T(8,128)S(1)} custom-call(bf16[2,4,8,64,128]{4,3,2,1,0:T(8,128)(2,1)S(1)} %copy-done.2, bf16[3,4,2,64,128]{4,3,2,1,0:T(8,128)(2,1)S(1)} %collective-permute-done.3.rin.r0in, bf16[3,4,2,64,128]{4,3,2,1,0:T(8,128)(2,1)S(1)} %collective-permute-done.4.rout.r0out, ...), custom_call_target="tpu_custom_call" | custom-call | flops 905969664 | bytes 4128768 | tf_op jit(solution)/shard_map/factor23_kernel/pallas_call | solution.py:388
  45.3 0.0 collective-permute-done.11.rout
  45.3 0.6 grad01_kernel.1.v3x
  45.9 0.1 collective-permute-start.15
  46.0 0.0 collective-permute-done.12.vxr
  46.0 1.0 %grad23_kernel.1 = (bf16[2,8,64,128]{3,2,1,0:T(8,128)(2,1)S(1)}, bf16[2,64,128]{2,1,0:T(8,128)(2,1)S(1)}, bf16[2,64,128]{2,1,0:T(8,128)(2,1)S(1)}) custom-call(f32[2,8,64,128]{3,2,1,0:T(8,128)S(1)} %get-tuple-element.53.after.base23, bf16[6,64,128]{2,1,0:T(8,128)(2,1)S(1)} %collective-permute-done.10.rin, ...), custom_call_target="tpu_custom_call" | custom-call | flops 566231040 | bytes 3342336 | tf_op jit(solution)/shard_map/grad23_kernel/pallas_call | solution.py:388
  47.0 3.5 %collective-permute-start.13 = (bf16[2,64,128]{2,1,0:T(8,128)(2,1)S(1)}, bf16[2,64,128]{2,1,0:T(8,128)(2,1)S(1)}, u32[]{:S(2)}, u32[]{:S(2)}) collective-permute-start(bf16[2,64,128]{2,1,0:T(8,128)(2,1)S(1)} %get-tuple-element.55), channel_id=1, source_target_pairs={{0,1},{1,0},{2,3},{3,2},{4,5},{5,4},{6,7},{7,6},{8,9},{9,8},{10,11... | collective-permute-start | bytes 98312 | tf_op jit(solution)/shard_map/ppermute | solution.py:415
  50.5 0.0 collective-permute-start.14
  50.5 2.1 %inner_last_kernel.1.base = f32[4,8,64,128]{3,2,1,0:T(8,128)S(1)} custom-call(bf16[2,10,64,128]{3,2,1,0:T(8,128)(2,1)S(1)} %grad01_kernel.1.v3x, bf16[2,8,64,128]{3,2,1,0:T(8,128)(2,1)S(1)} %get-tuple-element.54.v3, bf16[2,10,64,128]{3,2,1,0:T(8,128)(2,1)S(1)} %up01_kernel.1.v2x, bf16[2,8,64,128]{3,2,1,0:T(8,128)(2,1)S(1)} %get-tuple-element.49.after.v2, ...), custom_call_target="tpu_custom_call" | custom-call | flops 1358954496 | bytes 2949120 | tf_op jit(solution)/shard_map/inner_last_kernel/pallas_call | solution.py:388
  52.7 0.0 collective-permute-done.13.rin
  52.7 1.5 %collective-permute-done.14.rout = bf16[2,64,128]{2,1,0:T(8,128)(2,1)S(1)} collective-permute-done((bf16[2,64,128]{2,1,0:T(8,128)(2,1)S(1)}, bf16[2,64,128]{2,1,0:T(8,128)(2,1)S(1)}, u32[]{:S(2)}, u32[]{:S(2)}) %collective-permute-start.14) | collective-permute-done | bytes 32800 | tf_op jit(solution)/shard_map/ppermute | solution.py:418
  54.1 0.0 collective-permute-done.15.vxr
  54.1 1.4 %last_kernel.1 = bf16[32,4,1024]{2,1,0:T(4,128)(2,1)S(1)} custom-call(f32[4,8,64,128]{3,2,1,0:T(8,128)S(1)} %inner_last_kernel.1.base, bf16[2,64,128]{2,1,0:T(8,128)(2,1)S(1)} %collective-permute-done.13.rin, bf16[2,64,128]{2,1,0:T(8,128)(2,1)S(1)} %collective-permute-done.14.rout, bf16[2,10,64,128]{3,2,1,0:T(8,128)(2,1)S(1)} %collective-permute-done.15.vxr, ...), custom_call_target="tpu_custom_call" | custom-call | flops 452984832 | bytes 3211520 | tf_op jit(solution)/shard_map/last_kernel/pallas_call | solution.py:388
  55.5 15.5 %all_to_all.5 = bf16[32,4,1024]{2,1,0:T(4,128)(2,1)S(1)} all-to-all(bf16[32,4,1024]{2,1,0:T(4,128)(2,1)S(1)} %last_kernel.1), channel_id=1, replica_groups=mesh['tm'=4,'space'=32] {'space'}, dimensions={0} | all-to-all | bytes 524288 | tf_op jit(solution)/shard_map/all_to_all | solution.py:518
  71.0 0.7 copy.9
  (11 shorter events, 0.1 us)
Async XLA Ops:
  1.5 12.4 %collective-permute-start.3 = (bf16[3,4,2,64,128]{4,3,2,1,0:T(8,128)(2,1)S(1)}, bf16[3,4,2,64,128]{4,3,2,1,0:T(8,128)(2,1)S(1)}, u32[]{:S(2)}, u32[]{:S(2)}) collective-permute-start(bf16[3,4,2,64,128]{4,3,2,1,0:T(8,128)(2,1)S(1)} %get-tuple-element.36), channel_id=1, source_target_pairs={{0,1},{1,0},{2,3},{3,2},{4,5},{5,4},{6,7},{7,6},{8,9},{9,8},{10,11... | collective-permute-start | bytes 1179656 | tf_op jit(solution)/shard_map/ppermute | solution.py:415
  3.0 10.9 %collective-permute-start.4 = (bf16[3,4,2,64,128]{4,3,2,1,0:T(8,128)(2,1)S(1)}, bf16[3,4,2,64,128]{4,3,2,1,0:T(8,128)(2,1)S(1)}, u32[]{:S(2)}, u32[]{:S(2)}) collective-permute-start(bf16[3,4,2,64,128]{4,3,2,1,0:T(8,128)(2,1)S(1)} %get-tuple-element.37), channel_id=1, source_target_pairs={{0,31},{1,2},{2,1},{3,4},{4,3},{5,6},{6,5},{7,8},{8,7},{9,10},{10,... | collective-permute-start | bytes 1179656 | tf_op jit(solution)/shard_map/ppermute | solution.py:418
  4.7 15.4 %collective-permute-start = (bf16[2,8,64,128]{3,2,1,0:T(8,128)(2,1)S(1)}, bf16[2,8,64,128]{3,2,1,0:T(8,128)(2,1)S(1)}, u32[]{:S(2)}, u32[]{:S(2)}) collective-permute-start(bf16[2,8,64,128]{3,2,1,0:T(8,128)(2,1)S(1)} %get-tuple-element.31), channel_id=1, source_target_pairs={{0,32},{32,64},{64,96},{96,0},{1,33},{33,65},{65,97},{97,1},{2,34}... | collective-permute-start | bytes 786440 | tf_op jit(solution)/shard_map/ppermute | solution.py:428
  5.9 14.2 %collective-permute-start.1 = (bf16[2,2,64,128]{3,2,1,0:T(8,128)(2,1)S(1)}, bf16[2,2,64,128]{3,2,1,0:T(8,128)(2,1)S(1)}, u32[]{:S(2)}, u32[]{:S(2)}) collective-permute-start(bf16[2,2,64,128]{3,2,1,0:T(8,128)(2,1)S(1)} %get-tuple-element.32), channel_id=1, source_target_pairs={{0,33},{1,32},{2,35},{3,34},{4,37},{5,36},{6,39},{7,38},{8,41},{9,... | collective-permute-start | bytes 196616 | tf_op jit(solution)/shard_map/ppermute | solution.py:425
  12.3 7.9 %collective-permute-start.2 = (bf16[2,2,64,128]{3,2,1,0:T(8,128)(2,1)S(1)}, bf16[2,2,64,128]{3,2,1,0:T(8,128)(2,1)S(1)}, u32[]{:S(2)}, u32[]{:S(2)}) collective-permute-start(bf16[2,2,64,128]{3,2,1,0:T(8,128)(2,1)S(1)} %get-tuple-element.33), channel_id=1, source_target_pairs={{0,63},{1,34},{2,33},{3,36},{4,35},{5,38},{6,37},{7,40},{8,39},{9,... | collective-permute-start | bytes 196616 | tf_op jit(solution)/shard_map/ppermute | solution.py:425
  14.0 8.0 %collective-permute-start.5 = (bf16[2,10,64,128]{3,2,1,0:T(8,128)(2,1)S(1)}, bf16[2,10,64,128]{3,2,1,0:T(8,128)(2,1)S(1)}, u32[]{:S(2)}, u32[]{:S(2)}) collective-permute-start(bf16[2,10,64,128]{3,2,1,0:T(8,128)(2,1)S(1)} %extend_kernel.1), channel_id=1, source_target_pairs={{32,0},{64,32},{96,64},{0,96},{33,1},{65,33},{97,65},{1,97},{34,2}... | collective-permute-start | bytes 983048 | tf_op jit(solution)/shard_map/ppermute | solution.py:421
  15.5 4.7 %copy-start = (bf16[2,3,3,3,128,128]{5,4,3,2,1,0:T(8,128)(2,1)S(1)}, bf16[2,3,3,3,128,128]{5,4,3,2,1,0:T(8,128)(2,1)}, u32[]{:S(2)}) copy-start(bf16[2,3,3,3,128,128]{5,4,3,2,1,0:T(8,128)(2,1)} %w1.17) | copy-start | bytes 5308420
  20.2 1.8 %copy-start.1 = (bf16[2,3,3,3,128,128]{5,4,3,2,1,0:T(8,128)(2,1)S(1)}, bf16[2,3,3,3,128,128]{5,4,3,2,1,0:T(8,128)(2,1)}, u32[]{:S(2)}) copy-start(bf16[2,3,3,3,128,128]{5,4,3,2,1,0:T(8,128)(2,1)} %w2.9) | copy-start | bytes 5308420
  21.3 1.6 %copy-start.2 = (bf16[2,4,8,64,128]{4,3,2,1,0:T(8,128)(2,1)S(1)}, bf16[2,4,8,64,128]{4,3,2,1,0:T(8,128)(2,1)}, u32[]{:S(2)}) copy-start(bf16[2,4,8,64,128]{4,3,2,1,0:T(8,128)(2,1)} %bi.9) | copy-start | bytes 3145732
  22.9 16.5 %collective-permute-start.9 = (bf16[2,12,64,128]{3,2,1,0:T(8,128)(2,1)S(1)}, bf16[2,12,64,128]{3,2,1,0:T(8,128)(2,1)S(1)}, u32[]{:S(2)}, u32[]{:S(2)}) collective-permute-start(bf16[2,12,64,128]{3,2,1,0:T(8,128)(2,1)S(1)} %extend0_kernel.1), channel_id=1, source_target_pairs={{0,32},{32,64},{64,96},{96,0},{1,33},{33,65},{65,97},{97,1},{2,34}... | collective-permute-start | bytes 1179656 | tf_op jit(solution)/shard_map/ppermute | solution.py:428
  23.6 11.4 %collective-permute-start.8 = (bf16[2,10,64,128]{3,2,1,0:T(8,128)(2,1)S(1)}, bf16[2,10,64,128]{3,2,1,0:T(8,128)(2,1)S(1)}, u32[]{:S(2)}, u32[]{:S(2)}) collective-permute-start(bf16[2,10,64,128]{3,2,1,0:T(8,128)(2,1)S(1)} %pre01_kernel.1.v1x), channel_id=1, source_target_pairs={{32,0},{64,32},{96,64},{0,96},{33,1},{65,33},{97,65},{1,97},{34,2}... | collective-permute-start | bytes 983048 | tf_op jit(solution)/shard_map/ppermute | solution.py:421
  25.7 5.7 %collective-permute-start.6 = (bf16[6,64,128]{2,1,0:T(8,128)(2,1)S(1)}, bf16[6,64,128]{2,1,0:T(8,128)(2,1)S(1)}, u32[]{:S(2)}, u32[]{:S(2)}) collective-permute-start(bf16[6,64,128]{2,1,0:T(8,128)(2,1)S(1)} %get-tuple-element.46), channel_id=1, source_target_pairs={{0,1},{1,0},{2,3},{3,2},{4,5},{5,4},{6,7},{7,6},{8,9},{9,8},{10,11... | collective-permute-start | bytes 294920 | tf_op jit(solution)/shard_map/ppermute | solution.py:415
  28.5 4.3 %collective-permute-start.7 = (bf16[6,64,128]{2,1,0:T(8,128)(2,1)S(1)}, bf16[6,64,128]{2,1,0:T(8,128)(2,1)S(1)}, u32[]{:S(2)}, u32[]{:S(2)}) collective-permute-start(bf16[6,64,128]{2,1,0:T(8,128)(2,1)S(1)} %get-tuple-element.47), channel_id=1, source_target_pairs={{0,31},{1,2},{2,1},{3,4},{4,3},{5,6},{6,5},{7,8},{8,7},{9,10},{10,... | collective-permute-start | bytes 294920 | tf_op jit(solution)/shard_map/ppermute | solution.py:418
  33.4 12.6 %collective-permute-start.12 = (bf16[2,10,64,128]{3,2,1,0:T(8,128)(2,1)S(1)}, bf16[2,10,64,128]{3,2,1,0:T(8,128)(2,1)S(1)}, u32[]{:S(2)}, u32[]{:S(2)}) collective-permute-start(bf16[2,10,64,128]{3,2,1,0:T(8,128)(2,1)S(1)} %up01_kernel.1.v2x), channel_id=1, source_target_pairs={{32,0},{64,32},{96,64},{0,96},{33,1},{65,33},{97,65},{1,97},{34,2}... | collective-permute-start | bytes 983048 | tf_op jit(solution)/shard_map/ppermute | solution.py:421
  36.0 9.3 %collective-permute-start.10 = (bf16[6,64,128]{2,1,0:T(8,128)(2,1)S(1)}, bf16[6,64,128]{2,1,0:T(8,128)(2,1)S(1)}, u32[]{:S(2)}, u32[]{:S(2)}) collective-permute-start(bf16[6,64,128]{2,1,0:T(8,128)(2,1)S(1)} %get-tuple-element.51), channel_id=1, source_target_pairs={{0,1},{1,0},{2,3},{3,2},{4,5},{5,4},{6,7},{7,6},{8,9},{9,8},{10,11... | collective-permute-start | bytes 294920 | tf_op jit(solution)/shard_map/ppermute | solution.py:415
  39.4 5.9 %collective-permute-start.11 = (bf16[6,64,128]{2,1,0:T(8,128)(2,1)S(1)}, bf16[6,64,128]{2,1,0:T(8,128)(2,1)S(1)}, u32[]{:S(2)}, u32[]{:S(2)}) collective-permute-start(bf16[6,64,128]{2,1,0:T(8,128)(2,1)S(1)} %get-tuple-element.52), channel_id=1, source_target_pairs={{0,31},{1,2},{2,1},{3,4},{4,3},{5,6},{6,5},{7,8},{8,7},{9,10},{10,... | collective-permute-start | bytes 294920 | tf_op jit(solution)/shard_map/ppermute | solution.py:418
  45.9 8.2 %collective-permute-start.15 = (bf16[2,10,64,128]{3,2,1,0:T(8,128)(2,1)S(1)}, bf16[2,10,64,128]{3,2,1,0:T(8,128)(2,1)S(1)}, u32[]{:S(2)}, u32[]{:S(2)}) collective-permute-start(bf16[2,10,64,128]{3,2,1,0:T(8,128)(2,1)S(1)} %grad01_kernel.1.v3x), channel_id=1, source_target_pairs={{32,0},{64,32},{96,64},{0,96},{33,1},{65,33},{97,65},{1,97},{34,2}... | collective-permute-start | bytes 983048 | tf_op jit(solution)/shard_map/ppermute | solution.py:421
  47.0 5.6 %collective-permute-start.13 = (bf16[2,64,128]{2,1,0:T(8,128)(2,1)S(1)}, bf16[2,64,128]{2,1,0:T(8,128)(2,1)S(1)}, u32[]{:S(2)}, u32[]{:S(2)}) collective-permute-start(bf16[2,64,128]{2,1,0:T(8,128)(2,1)S(1)} %get-tuple-element.55), channel_id=1, source_target_pairs={{0,1},{1,0},{2,3},{3,2},{4,5},{5,4},{6,7},{7,6},{8,9},{9,8},{10,11... | collective-permute-start | bytes 98312 | tf_op jit(solution)/shard_map/ppermute | solution.py:415
  50.5 3.6 %collective-permute-start.14 = (bf16[2,64,128]{2,1,0:T(8,128)(2,1)S(1)}, bf16[2,64,128]{2,1,0:T(8,128)(2,1)S(1)}, u32[]{:S(2)}, u32[]{:S(2)}) collective-permute-start(bf16[2,64,128]{2,1,0:T(8,128)(2,1)S(1)} %get-tuple-element.56), channel_id=1, source_target_pairs={{0,31},{1,2},{2,1},{3,4},{4,3},{5,6},{6,5},{7,8},{8,7},{9,10},{10,... | collective-permute-start | bytes 98312 | tf_op jit(solution)/shard_map/ppermute | solution.py:418
  50.5 3.6 %copy-start.3 = (s32[1,1,64,1]{2,3,1,0:T(1,128)S(1)}, s32[1,1,64,1]{2,3,1,0:T(1,128)}, u32[]{:S(2)}) copy-start(s32[1,1,64,1]{2,3,1,0:T(1,128)} %param.13) | copy-start | bytes 772

commit v5 on v4

--- a/solution.py
+++ b/solution.py
@@ -218,13 +218,13 @@
     send_edges(v1x, v1, ein, eout)
 
 
-def up01_kernel(base01, rin, rout, w1, v2x):
+def up01_kernel(base01, rin, rout, after, w1, v2x):
     top, bottom = rim_rows(*halos(rin, rout), w1, 1)
     for t in range(2):
         store_ten(v2x, t, ten_rows(base01, t, top, bottom))
 
 
-def grad01_kernel(base01, rin, rout, d, after, w2, v3x):
+def grad01_kernel(base01, rin, rout, d, w2, v3x):
     top, bottom = rim_rows(*halos(rin, rout), w2, 0)
     for t in range(2):
         store_ten(v3x, t, ten_rows(base01, t, top, bottom) * d[t])
@@ -488,14 +488,14 @@
         28,
         scratch=[ext, pltpu.VMEM((2, 12, COLS, C), BF)],
     )
-    v2x = run(up01_kernel, field(2, 10), (base01, r1in, r1out, w1), 8, scratch=[])
+    d0 = run(factor23_kernel, eight, (bi, rin, rout, base23, w1), 16)
+    v2x = run(up01_kernel, field(2, 10), (base01, r1in, r1out, d0, w1), 8, scratch=[])
     v2xr = from_later(v2x)
     v2, ein, eout = run(up23_kernel, edges, (base23, r1in, r1out, v1xr, v2x, w1), 10)
     r2out, r2in = swap_out(eout), swap_in(ein)
     d0a = run(factor01_kernel, ten, (bi, rin, rout, b0x, v2, w1), 20)
     base01, base23 = run(inner_grad_kernel, [ten, eight], (v2x, v2, d0a, w2), 28)
-    d0 = run(factor23_kernel, eight, (bi, rin, rout, base23, w1), 16)
-    v3x = run(grad01_kernel, field(2, 10), (base01, r2in, r2out, d0a, d0, w2), 8, scratch=[])
+    v3x = run(grad01_kernel, field(2, 10), (base01, r2in, r2out, d0a, w2), 8, scratch=[])
     v3xr = from_later(v3x)
     v3, ein, eout = run(
         grad23_kernel,

time: 72 us -> 71 us (0.986)
  waiting for transfers between devices: 3.62 us -> 2.2 us
  blocking collectives: 15.5 us -> 16.3 us
    ppermute x4, waiting for transfers between devices: 2.9 us -> 1.47 us  [swap_out(): return lax.ppermute(x, 'space', outer_pairs)]
    all_to_all x1, blocking collectives: 15.5 us -> 16.3 us  [on_device(): lax.all_to_all(outgoing, 'space', split_axis=0, concat_axis=0, tiled=True)]
  transfers between devices with their start and end apart: 16 -> 16, of which waited for: 3 -> 2; matrix products, arithmetic and copies ran while one was open for 0% -> 0% of each run, Pallas kernels for 29% -> 30%
where the time goes in v5:
time: 71 us; the launch traced here: 70.8 us
  starting transfers between devices  26.6 us (37%)
  Pallas kernels  24.8 us (35%)
  blocking collectives  16.3 us (23%)
  waiting for transfers between devices  2.2 us (3%)
  local copies, waits for them, and re-layouts  0.72 us (1%)
    pallas_call x17, Pallas kernels, run(): pl.pallas_call(kernel, out_shape=outs, in_specs=in_specs or [VM] * len(ar...  24.8 us
    all_to_all x1, blocking collectives, on_device(): lax.all_to_all(outgoing, 'space', split_axis=0, concat_axis=0, tiled=True)  16.3 us
    ppermute x4, starting transfers between devices, swap_in(): return lax.ppermute(x, 'space', inner_pairs)  11.2 us
    ppermute x2, starting transfers between devices, corner(): return lax.ppermute(x, ('tm', 'space'), route)  6.37 us
    ppermute x4, starting transfers between devices, from_later(): return lax.ppermute(x, 'tm', later)  4.98 us
    ppermute x4, starting transfers between devices, swap_out(): return lax.ppermute(x, 'space', outer_pairs)  2.13 us
    ppermute x2, starting transfers between devices, from_sooner(): return lax.ppermute(x, 'tm', sooner)  1.9 us
    ppermute x4, waiting for transfers between devices, swap_out(): return lax.ppermute(x, 'space', outer_pairs)  1.47 us
  transfers between devices with their start and end apart: 16, of which 2 were waited for; matrix products, arithmetic and copies ran while one was open for 0% of the time, Pallas kernels for 30%

profile of v5, /device:TPU:1, one launch (start us, length us, event | category | flops | bytes accessed | tf_op | source)
XLA Modules:
  0.0 70.8 jit_solution(5779823722165080284)
XLA Ops:
  0.0 1.5 %start_kernel.1 = (bf16[4,8,64,128]{3,2,1,0:T(8,128)(2,1)S(1)}, bf16[3,4,2,64,128]{4,3,2,1,0:T(8,128)(2,1)S(1)}, bf16[3,4,2,64,128]{4,3,2,1,0:T(8,128)(2,1)S(1)}...) custom-call(bf16[4,8,64,128]{3,2,1,0:T(8,128)(2,1)} %cot.1, ...), custom_call_target="tpu_custom_call" | custom-call | flops 56623104 | bytes 1572896 | tf_op jit(solution)/shard_map/start_kernel/pallas_call | solution.py:388
  1.5 1.5 %collective-permute-start.3 = (bf16[3,4,2,64,128]{4,3,2,1,0:T(8,128)(2,1)S(1)}, bf16[3,4,2,64,128]{4,3,2,1,0:T(8,128)(2,1)S(1)}, u32[]{:S(2)}, u32[]{:S(2)}) collective-permute-start(bf16[3,4,2,64,128]{4,3,2,1,0:T(8,128)(2,1)S(1)} %get-tuple-element.36), channel_id=1, source_target_pairs={{0,1},{1,0},{2,3},{3,2},{4,5},{5,4},{6,7},{7,6},{8,9},{9,8},{10,11... | collective-permute-start | bytes 1179656 | tf_op jit(solution)/shard_map/ppermute | solution.py:415
  3.0 1.7 %collective-permute-start.4 = (bf16[3,4,2,64,128]{4,3,2,1,0:T(8,128)(2,1)S(1)}, bf16[3,4,2,64,128]{4,3,2,1,0:T(8,128)(2,1)S(1)}, u32[]{:S(2)}, u32[]{:S(2)}) collective-permute-start(bf16[3,4,2,64,128]{4,3,2,1,0:T(8,128)(2,1)S(1)} %get-tuple-element.37), channel_id=1, source_target_pairs={{0,31},{1,2},{2,1},{3,4},{4,3},{5,6},{6,5},{7,8},{8,7},{9,10},{10,... | collective-permute-start | bytes 1179656 | tf_op jit(solution)/shard_map/ppermute | solution.py:418
  4.7 1.2 %collective-permute-start = (bf16[2,8,64,128]{3,2,1,0:T(8,128)(2,1)S(1)}, bf16[2,8,64,128]{3,2,1,0:T(8,128)(2,1)S(1)}, u32[]{:S(2)}, u32[]{:S(2)}) collective-permute-start(bf16[2,8,64,128]{3,2,1,0:T(8,128)(2,1)S(1)} %get-tuple-element.31), channel_id=1, source_target_pairs={{0,32},{32,64},{64,96},{96,0},{1,33},{33,65},{65,97},{97,1},{2,34}... | collective-permute-start | bytes 786440 | tf_op jit(solution)/shard_map/ppermute | solution.py:428
  5.9 6.4 %collective-permute-start.1 = (bf16[2,2,64,128]{3,2,1,0:T(8,128)(2,1)S(1)}, bf16[2,2,64,128]{3,2,1,0:T(8,128)(2,1)S(1)}, u32[]{:S(2)}, u32[]{:S(2)}) collective-permute-start(bf16[2,2,64,128]{3,2,1,0:T(8,128)(2,1)S(1)} %get-tuple-element.32), channel_id=1, source_target_pairs={{0,33},{1,32},{2,35},{3,34},{4,37},{5,36},{6,39},{7,38},{8,41},{9,... | collective-permute-start | bytes 196616 | tf_op jit(solution)/shard_map/ppermute | solution.py:425
  12.3 0.0 collective-permute-start.2
  12.3 1.6 %fetch_kernel.1 = (bf16[4,8,64,128]{3,2,1,0:T(8,128)(2,1)S(1)}, bf16[1,3,3,3,128,128]{5,4,3,2,1,0:T(8,128)(2,1)S(1)}, bf16[1,3,3,3,128,128]{5,4,3,2,1,0:T(8,128)(2,1)S(1)}) custom-call(bf16[4,8,64,128]{3,2,1,0:T(8,128)(2,1)S(1)} %get-tuple-element.34.after.v0, bf16[2,4,8,64,128]{4,3,2,1,0:T(8,128)(2,1)} %bi.9, bf16[2,3,3,3,128,128]{5,4,3,2,1,0:T(8,128)(2,1)} %w2.9, ...), custom_call_target="tpu_custom_call" | custom-call | flops 56623104 | bytes 5111808 | tf_op jit(solution)/shard_map/fetch_kernel/pallas_call | solution.py:388
  13.9 0.0 collective-permute-done.3.rin.r0in
  13.9 0.0 collective-permute-done.4.rout.r0out
  14.0 1.5 %collective-permute-start.5 = (bf16[2,10,64,128]{3,2,1,0:T(8,128)(2,1)S(1)}, bf16[2,10,64,128]{3,2,1,0:T(8,128)(2,1)S(1)}, u32[]{:S(2)}, u32[]{:S(2)}) collective-permute-start(bf16[2,10,64,128]{3,2,1,0:T(8,128)(2,1)S(1)} %extend_kernel.1), channel_id=1, source_target_pairs={{32,0},{64,32},{96,64},{0,96},{33,1},{65,33},{97,65},{1,97},{34,2}... | collective-permute-start | bytes 983048 | tf_op jit(solution)/shard_map/ppermute | solution.py:421
  15.5 4.6 %early_kernel.1 = (f32[2,10,64,128]{3,2,1,0:T(8,128)S(1)}, f32[2,8,64,128]{3,2,1,0:T(8,128)S(1)}, f32[2,8,64,128]{3,2,1,0:T(8,128)S(1)}, f32[2,10,64,128]{3,2,1,0:T(8,128)S(1)}) custom-call(bf16[4,8,64,128]{3,2,1,0:T(8,128)(2,1)S(1)} %get-tuple-element.34.after.v0, bf16[4,8,64,128]{3,2,1,0:T(8,128)(2,1)S(1)} %get-tuple-element.35.bi1, ...), custom_call_target="tpu_custom_call" | custom-call | flops 3057647616 | bytes 3604480 | tf_op jit(solution)/shard_map/early_kernel/pallas_call | solution.py:388
  20.1 0.0 collective-permute-done.1.dpi
  20.2 0.0 collective-permute-done.2.dpo
  20.2 0.0 collective-permute-done.bx
  20.2 0.0 copy-start.1
  20.2 1.1 %pre01_kernel.1.v1x = bf16[2,10,64,128]{3,2,1,0:T(8,128)(2,1)S(1)} custom-call(bf16[2,8,64,128]{3,2,1,0:T(8,128)(2,1)S(1)} %collective-permute-done.bx, bf16[2,2,64,128]{3,2,1,0:T(8,128)(2,1)S(1)} %collective-permute-done.1.dpi, bf16[2,2,64,128]{3,2,1,0:T(8,128)(2,1)S(1)} %collective-permute-done.2.dpo, f32[2,10,64,128]{3,2,1,0:T(8,128)S(1)} %get-tuple-element.40.ga, ...), custom_call_target="tpu_custom_call" | custom-call | flops 566231040 | bytes 3473408 | tf_op jit(solution)/shard_map/pre01_kernel/pallas_call | solution.py:388
  21.3 0.0 copy-start.2
  21.3 0.7 collective-permute-done.5.vx
  22.0 0.9 %pre23_kernel.1 = (bf16[2,8,64,128]{3,2,1,0:T(8,128)(2,1)S(1)}, bf16[6,64,128]{2,1,0:T(8,128)(2,1)S(1)}, bf16[6,64,128]{2,1,0:T(8,128)(2,1)S(1)}) custom-call(f32[2,8,64,128]{3,2,1,0:T(8,128)S(1)} %get-tuple-element.42.ga23, bf16[2,10,64,128]{3,2,1,0:T(8,128)(2,1)S(1)} %collective-permute-done.5.vx, f32[2,8,64,128]{3,2,1,0:T(8,128)S(1)} %get-tuple-element.43.d, ...), custom_call_target="tpu_custom_call" | custom-call | flops 452984832 | bytes 3473408 | tf_op jit(solution)/shard_map/pre23_kernel/pallas_call | solution.py:388
  22.9 0.7 collective-permute-start.9
  23.6 2.1 %collective-permute-start.8 = (bf16[2,10,64,128]{3,2,1,0:T(8,128)(2,1)S(1)}, bf16[2,10,64,128]{3,2,1,0:T(8,128)(2,1)S(1)}, u32[]{:S(2)}, u32[]{:S(2)}) collective-permute-start(bf16[2,10,64,128]{3,2,1,0:T(8,128)(2,1)S(1)} %pre01_kernel.1.v1x), channel_id=1, source_target_pairs={{32,0},{64,32},{96,64},{0,96},{33,1},{65,33},{97,65},{1,97},{34,2}... | collective-permute-start | bytes 983048 | tf_op jit(solution)/shard_map/ppermute | solution.py:421
  25.7 2.8 %collective-permute-start.6 = (bf16[6,64,128]{2,1,0:T(8,128)(2,1)S(1)}, bf16[6,64,128]{2,1,0:T(8,128)(2,1)S(1)}, u32[]{:S(2)}, u32[]{:S(2)}) collective-permute-start(bf16[6,64,128]{2,1,0:T(8,128)(2,1)S(1)} %get-tuple-element.46), channel_id=1, source_target_pairs={{0,1},{1,0},{2,3},{3,2},{4,5},{5,4},{6,7},{7,6},{8,9},{9,8},{10,11... | collective-permute-start | bytes 294920 | tf_op jit(solution)/shard_map/ppermute | solution.py:415
  28.5 0.4 collective-permute-start.7
  28.9 2.5 %inner_up_kernel.1 = (f32[2,10,64,128]{3,2,1,0:T(8,128)S(1)}, f32[2,8,64,128]{3,2,1,0:T(8,128)S(1)}) custom-call(bf16[2,10,64,128]{3,2,1,0:T(8,128)(2,1)S(1)} %pre01_kernel.1.v1x, bf16[2,8,64,128]{3,2,1,0:T(8,128)(2,1)S(1)} %get-tuple-element.44.v1.after, bf16[4,8,64,128]{3,2,1,0:T(8,128)(2,1)S(1)} %get-tuple-element.34.after.v0, ...), custom_call_target="tpu_custom_call" | custom-call | flops 1585446912 | bytes 3670016 | tf_op jit(solution)/shard_map/inner_up_kernel/pallas_call | solution.py:388
  31.4 1.5 %factor23_kernel.1.after.d = f32[2,8,64,128]{3,2,1,0:T(8,128)S(1)} custom-call(bf16[2,4,8,64,128]{4,3,2,1,0:T(8,128)(2,1)S(1)} %copy-done.2, bf16[3,4,2,64,128]{4,3,2,1,0:T(8,128)(2,1)S(1)} %collective-permute-done.3.rin.r0in, bf16[3,4,2,64,128]{4,3,2,1,0:T(8,128)(2,1)S(1)} %collective-permute-done.4.rout.r0out, ...), custom_call_target="tpu_custom_call" | custom-call | flops 905969664 | bytes 4128768 | tf_op jit(solution)/shard_map/factor23_kernel/pallas_call | solution.py:388
  32.9 0.0 collective-permute-done.6.rin
  32.9 0.0 collective-permute-done.7.rout
  32.9 0.6 up01_kernel.1.v2x
  33.5 1.3 %collective-permute-start.12 = (bf16[2,10,64,128]{3,2,1,0:T(8,128)(2,1)S(1)}, bf16[2,10,64,128]{3,2,1,0:T(8,128)(2,1)S(1)}, u32[]{:S(2)}, u32[]{:S(2)}) collective-permute-start(bf16[2,10,64,128]{3,2,1,0:T(8,128)(2,1)S(1)} %up01_kernel.1.v2x), channel_id=1, source_target_pairs={{32,0},{64,32},{96,64},{0,96},{33,1},{65,33},{97,65},{1,97},{34,2}... | collective-permute-start | bytes 983048 | tf_op jit(solution)/shard_map/ppermute | solution.py:421
  34.8 0.0 collective-permute-done.8.vxr
  34.8 1.0 %up23_kernel.1 = (bf16[2,8,64,128]{3,2,1,0:T(8,128)(2,1)S(1)}, bf16[6,64,128]{2,1,0:T(8,128)(2,1)S(1)}, bf16[6,64,128]{2,1,0:T(8,128)(2,1)S(1)}) custom-call(f32[2,8,64,128]{3,2,1,0:T(8,128)S(1)} %get-tuple-element.48.after.base23, bf16[6,64,128]{2,1,0:T(8,128)(2,1)S(1)} %collective-permute-done.6.rin, bf16[6,64,128]{2,1,0:T(8,128)(2,1)S(1)} %collective-permute-done.7.rout, ...), custom_call_target="tpu_custom_call" | custom-call | flops 566231040 | bytes 3145728 | tf_op jit(solution)/shard_map/up23_kernel/pallas_call | solution.py:388
  35.9 3.4 %collective-permute-start.10 = (bf16[6,64,128]{2,1,0:T(8,128)(2,1)S(1)}, bf16[6,64,128]{2,1,0:T(8,128)(2,1)S(1)}, u32[]{:S(2)}, u32[]{:S(2)}) collective-permute-start(bf16[6,64,128]{2,1,0:T(8,128)(2,1)S(1)} %get-tuple-element.51), channel_id=1, source_target_pairs={{0,1},{1,0},{2,3},{3,2},{4,5},{5,4},{6,7},{7,6},{8,9},{9,8},{10,11... | collective-permute-start | bytes 294920 | tf_op jit(solution)/shard_map/ppermute | solution.py:415
  39.3 0.0 collective-permute-start.11
  39.3 0.0 collective-permute-done.9.bx
  39.3 1.8 %factor01_kernel.1.after.d = f32[2,10,64,128]{3,2,1,0:T(8,128)S(1)} custom-call(bf16[2,4,8,64,128]{4,3,2,1,0:T(8,128)(2,1)S(1)} %copy-done.2, bf16[3,4,2,64,128]{4,3,2,1,0:T(8,128)(2,1)S(1)} %collective-permute-done.3.rin.r0in, bf16[3,4,2,64,128]{4,3,2,1,0:T(8,128)(2,1)S(1)} %collective-permute-done.4.rout.r0out, ...), custom_call_target="tpu_custom_call" | custom-call | flops 1132462080 | bytes 4259840 | tf_op jit(solution)/shard_map/factor01_kernel/pallas_call | solution.py:388
  41.1 2.5 %inner_grad_kernel.1 = (f32[2,10,64,128]{3,2,1,0:T(8,128)S(1)}, f32[2,8,64,128]{3,2,1,0:T(8,128)S(1)}) custom-call(bf16[2,10,64,128]{3,2,1,0:T(8,128)(2,1)S(1)} %up01_kernel.1.v2x, bf16[2,8,64,128]{3,2,1,0:T(8,128)(2,1)S(1)} %get-tuple-element.49.after.v2, f32[2,10,64,128]{3,2,1,0:T(8,128)S(1)} %factor01_kernel.1.after.d, ...), custom_call_target="tpu_custom_call" | custom-call | flops 1585446912 | bytes 3014656 | tf_op jit(solution)/shard_map/inner_grad_kernel/pallas_call | solution.py:388
  43.6 0.0 collective-permute-done.10.rin
  43.6 0.0 collective-permute-done.11.rout
  43.6 0.6 grad01_kernel.1.v3x
  44.2 0.1 collective-permute-start.15
  44.3 1.0 %grad23_kernel.1 = (bf16[2,8,64,128]{3,2,1,0:T(8,128)(2,1)S(1)}, bf16[2,64,128]{2,1,0:T(8,128)(2,1)S(1)}, bf16[2,64,128]{2,1,0:T(8,128)(2,1)S(1)}) custom-call(f32[2,8,64,128]{3,2,1,0:T(8,128)S(1)} %get-tuple-element.53.base23, bf16[6,64,128]{2,1,0:T(8,128)(2,1)S(1)} %collective-permute-done.10.rin, bf16[6,64,128]{2,1,0:T(8,128)(2,1)S(1)} %collective-permute-done.11.rout, ...), custom_call_target="tpu_custom_call" | custom-call | flops 566231040 | bytes 3342336 | tf_op jit(solution)/shard_map/grad23_kernel/pallas_call | solution.py:388
  45.3 3.5 %collective-permute-start.13 = (bf16[2,64,128]{2,1,0:T(8,128)(2,1)S(1)}, bf16[2,64,128]{2,1,0:T(8,128)(2,1)S(1)}, u32[]{:S(2)}, u32[]{:S(2)}) collective-permute-start(bf16[2,64,128]{2,1,0:T(8,128)(2,1)S(1)} %get-tuple-element.55), channel_id=1, source_target_pairs={{0,1},{1,0},{2,3},{3,2},{4,5},{5,4},{6,7},{7,6},{8,9},{9,8},{10,11... | collective-permute-start | bytes 98312 | tf_op jit(solution)/shard_map/ppermute | solution.py:415
  48.8 0.0 collective-permute-start.14
  48.8 2.1 %inner_last_kernel.1.base = f32[4,8,64,128]{3,2,1,0:T(8,128)S(1)} custom-call(bf16[2,10,64,128]{3,2,1,0:T(8,128)(2,1)S(1)} %grad01_kernel.1.v3x, bf16[2,8,64,128]{3,2,1,0:T(8,128)(2,1)S(1)} %get-tuple-element.54.v3, bf16[2,10,64,128]{3,2,1,0:T(8,128)(2,1)S(1)} %up01_kernel.1.v2x, bf16[2,8,64,128]{3,2,1,0:T(8,128)(2,1)S(1)} %get-tuple-element.49.after.v2, ...), custom_call_target="tpu_custom_call" | custom-call | flops 1358954496 | bytes 2949120 | tf_op jit(solution)/shard_map/inner_last_kernel/pallas_call | solution.py:388
  51.0 1.5 %collective-permute-done.14.rout = bf16[2,64,128]{2,1,0:T(8,128)(2,1)S(1)} collective-permute-done((bf16[2,64,128]{2,1,0:T(8,128)(2,1)S(1)}, bf16[2,64,128]{2,1,0:T(8,128)(2,1)S(1)}, u32[]{:S(2)}, u32[]{:S(2)}) %collective-permute-start.14) | collective-permute-done | bytes 32800 | tf_op jit(solution)/shard_map/ppermute | solution.py:418
  52.4 1.4 %last_kernel.1 = bf16[32,4,1024]{2,1,0:T(4,128)(2,1)S(1)} custom-call(f32[4,8,64,128]{3,2,1,0:T(8,128)S(1)} %inner_last_kernel.1.base, bf16[2,64,128]{2,1,0:T(8,128)(2,1)S(1)} %collective-permute-done.13.rin, bf16[2,64,128]{2,1,0:T(8,128)(2,1)S(1)} %collective-permute-done.14.rout, bf16[2,10,64,128]{3,2,1,0:T(8,128)(2,1)S(1)} %collective-permute-done.15.vxr, ...), custom_call_target="tpu_custom_call" | custom-call | flops 452984832 | bytes 3211520 | tf_op jit(solution)/shard_map/last_kernel/pallas_call | solution.py:388
  53.8 16.3 %all_to_all.5 = bf16[32,4,1024]{2,1,0:T(4,128)(2,1)S(1)} all-to-all(bf16[32,4,1024]{2,1,0:T(4,128)(2,1)S(1)} %last_kernel.1), channel_id=1, replica_groups=mesh['tm'=4,'space'=32] {'space'}, dimensions={0} | all-to-all | bytes 524288 | tf_op jit(solution)/shard_map/all_to_all | solution.py:518
  70.1 0.7 copy.9
  (11 shorter events, 0.1 us)
Async XLA Ops:
  1.5 12.4 %collective-permute-start.3 = (bf16[3,4,2,64,128]{4,3,2,1,0:T(8,128)(2,1)S(1)}, bf16[3,4,2,64,128]{4,3,2,1,0:T(8,128)(2,1)S(1)}, u32[]{:S(2)}, u32[]{:S(2)}) collective-permute-start(bf16[3,4,2,64,128]{4,3,2,1,0:T(8,128)(2,1)S(1)} %get-tuple-element.36), channel_id=1, source_target_pairs={{0,1},{1,0},{2,3},{3,2},{4,5},{5,4},{6,7},{7,6},{8,9},{9,8},{10,11... | collective-permute-start | bytes 1179656 | tf_op jit(solution)/shard_map/ppermute | solution.py:415
  3.0 10.9 %collective-permute-start.4 = (bf16[3,4,2,64,128]{4,3,2,1,0:T(8,128)(2,1)S(1)}, bf16[3,4,2,64,128]{4,3,2,1,0:T(8,128)(2,1)S(1)}, u32[]{:S(2)}, u32[]{:S(2)}) collective-permute-start(bf16[3,4,2,64,128]{4,3,2,1,0:T(8,128)(2,1)S(1)} %get-tuple-element.37), channel_id=1, source_target_pairs={{0,31},{1,2},{2,1},{3,4},{4,3},{5,6},{6,5},{7,8},{8,7},{9,10},{10,... | collective-permute-start | bytes 1179656 | tf_op jit(solution)/shard_map/ppermute | solution.py:418
  4.7 15.4 %collective-permute-start = (bf16[2,8,64,128]{3,2,1,0:T(8,128)(2,1)S(1)}, bf16[2,8,64,128]{3,2,1,0:T(8,128)(2,1)S(1)}, u32[]{:S(2)}, u32[]{:S(2)}) collective-permute-start(bf16[2,8,64,128]{3,2,1,0:T(8,128)(2,1)S(1)} %get-tuple-element.31), channel_id=1, source_target_pairs={{0,32},{32,64},{64,96},{96,0},{1,33},{33,65},{65,97},{97,1},{2,34}... | collective-permute-start | bytes 786440 | tf_op jit(solution)/shard_map/ppermute | solution.py:428
  5.9 14.2 %collective-permute-start.1 = (bf16[2,2,64,128]{3,2,1,0:T(8,128)(2,1)S(1)}, bf16[2,2,64,128]{3,2,1,0:T(8,128)(2,1)S(1)}, u32[]{:S(2)}, u32[]{:S(2)}) collective-permute-start(bf16[2,2,64,128]{3,2,1,0:T(8,128)(2,1)S(1)} %get-tuple-element.32), channel_id=1, source_target_pairs={{0,33},{1,32},{2,35},{3,34},{4,37},{5,36},{6,39},{7,38},{8,41},{9,... | collective-permute-start | bytes 196616 | tf_op jit(solution)/shard_map/ppermute | solution.py:425
  12.3 7.9 %collective-permute-start.2 = (bf16[2,2,64,128]{3,2,1,0:T(8,128)(2,1)S(1)}, bf16[2,2,64,128]{3,2,1,0:T(8,128)(2,1)S(1)}, u32[]{:S(2)}, u32[]{:S(2)}) collective-permute-start(bf16[2,2,64,128]{3,2,1,0:T(8,128)(2,1)S(1)} %get-tuple-element.33), channel_id=1, source_target_pairs={{0,63},{1,34},{2,33},{3,36},{4,35},{5,38},{6,37},{7,40},{8,39},{9,... | collective-permute-start | bytes 196616 | tf_op jit(solution)/shard_map/ppermute | solution.py:425
  14.0 8.0 %collective-permute-start.5 = (bf16[2,10,64,128]{3,2,1,0:T(8,128)(2,1)S(1)}, bf16[2,10,64,128]{3,2,1,0:T(8,128)(2,1)S(1)}, u32[]{:S(2)}, u32[]{:S(2)}) collective-permute-start(bf16[2,10,64,128]{3,2,1,0:T(8,128)(2,1)S(1)} %extend_kernel.1), channel_id=1, source_target_pairs={{32,0},{64,32},{96,64},{0,96},{33,1},{65,33},{97,65},{1,97},{34,2}... | collective-permute-start | bytes 983048 | tf_op jit(solution)/shard_map/ppermute | solution.py:421
  15.5 4.7 %copy-start = (bf16[2,3,3,3,128,128]{5,4,3,2,1,0:T(8,128)(2,1)S(1)}, bf16[2,3,3,3,128,128]{5,4,3,2,1,0:T(8,128)(2,1)}, u32[]{:S(2)}) copy-start(bf16[2,3,3,3,128,128]{5,4,3,2,1,0:T(8,128)(2,1)} %w1.17) | copy-start | bytes 5308420
  20.2 1.8 %copy-start.1 = (bf16[2,3,3,3,128,128]{5,4,3,2,1,0:T(8,128)(2,1)S(1)}, bf16[2,3,3,3,128,128]{5,4,3,2,1,0:T(8,128)(2,1)}, u32[]{:S(2)}) copy-start(bf16[2,3,3,3,128,128]{5,4,3,2,1,0:T(8,128)(2,1)} %w2.9) | copy-start | bytes 5308420
  21.3 1.6 %copy-start.2 = (bf16[2,4,8,64,128]{4,3,2,1,0:T(8,128)(2,1)S(1)}, bf16[2,4,8,64,128]{4,3,2,1,0:T(8,128)(2,1)}, u32[]{:S(2)}) copy-start(bf16[2,4,8,64,128]{4,3,2,1,0:T(8,128)(2,1)} %bi.9) | copy-start | bytes 3145732
  22.9 16.3 %collective-permute-start.9 = (bf16[2,12,64,128]{3,2,1,0:T(8,128)(2,1)S(1)}, bf16[2,12,64,128]{3,2,1,0:T(8,128)(2,1)S(1)}, u32[]{:S(2)}, u32[]{:S(2)}) collective-permute-start(bf16[2,12,64,128]{3,2,1,0:T(8,128)(2,1)S(1)} %extend0_kernel.1), channel_id=1, source_target_pairs={{0,32},{32,64},{64,96},{96,0},{1,33},{33,65},{65,97},{97,1},{2,34}... | collective-permute-start | bytes 1179656 | tf_op jit(solution)/shard_map/ppermute | solution.py:428
  23.6 11.2 %collective-permute-start.8 = (bf16[2,10,64,128]{3,2,1,0:T(8,128)(2,1)S(1)}, bf16[2,10,64,128]{3,2,1,0:T(8,128)(2,1)S(1)}, u32[]{:S(2)}, u32[]{:S(2)}) collective-permute-start(bf16[2,10,64,128]{3,2,1,0:T(8,128)(2,1)S(1)} %pre01_kernel.1.v1x), channel_id=1, source_target_pairs={{32,0},{64,32},{96,64},{0,96},{33,1},{65,33},{97,65},{1,97},{34,2}... | collective-permute-start | bytes 983048 | tf_op jit(solution)/shard_map/ppermute | solution.py:421
  25.7 7.2 %collective-permute-start.6 = (bf16[6,64,128]{2,1,0:T(8,128)(2,1)S(1)}, bf16[6,64,128]{2,1,0:T(8,128)(2,1)S(1)}, u32[]{:S(2)}, u32[]{:S(2)}) collective-permute-start(bf16[6,64,128]{2,1,0:T(8,128)(2,1)S(1)} %get-tuple-element.46), channel_id=1, source_target_pairs={{0,1},{1,0},{2,3},{3,2},{4,5},{5,4},{6,7},{7,6},{8,9},{9,8},{10,11... | collective-permute-start | bytes 294920 | tf_op jit(solution)/shard_map/ppermute | solution.py:415
  28.5 4.4 %collective-permute-start.7 = (bf16[6,64,128]{2,1,0:T(8,128)(2,1)S(1)}, bf16[6,64,128]{2,1,0:T(8,128)(2,1)S(1)}, u32[]{:S(2)}, u32[]{:S(2)}) collective-permute-start(bf16[6,64,128]{2,1,0:T(8,128)(2,1)S(1)} %get-tuple-element.47), channel_id=1, source_target_pairs={{0,31},{1,2},{2,1},{3,4},{4,3},{5,6},{6,5},{7,8},{8,7},{9,10},{10,... | collective-permute-start | bytes 294920 | tf_op jit(solution)/shard_map/ppermute | solution.py:418
  33.5 10.8 %collective-permute-start.12 = (bf16[2,10,64,128]{3,2,1,0:T(8,128)(2,1)S(1)}, bf16[2,10,64,128]{3,2,1,0:T(8,128)(2,1)S(1)}, u32[]{:S(2)}, u32[]{:S(2)}) collective-permute-start(bf16[2,10,64,128]{3,2,1,0:T(8,128)(2,1)S(1)} %up01_kernel.1.v2x), channel_id=1, source_target_pairs={{32,0},{64,32},{96,64},{0,96},{33,1},{65,33},{97,65},{1,97},{34,2}... | collective-permute-start | bytes 983048 | tf_op jit(solution)/shard_map/ppermute | solution.py:421
  35.9 7.7 %collective-permute-start.10 = (bf16[6,64,128]{2,1,0:T(8,128)(2,1)S(1)}, bf16[6,64,128]{2,1,0:T(8,128)(2,1)S(1)}, u32[]{:S(2)}, u32[]{:S(2)}) collective-permute-start(bf16[6,64,128]{2,1,0:T(8,128)(2,1)S(1)} %get-tuple-element.51), channel_id=1, source_target_pairs={{0,1},{1,0},{2,3},{3,2},{4,5},{5,4},{6,7},{7,6},{8,9},{9,8},{10,11... | collective-permute-start | bytes 294920 | tf_op jit(solution)/shard_map/ppermute | solution.py:415
  39.3 4.3 %collective-permute-start.11 = (bf16[6,64,128]{2,1,0:T(8,128)(2,1)S(1)}, bf16[6,64,128]{2,1,0:T(8,128)(2,1)S(1)}, u32[]{:S(2)}, u32[]{:S(2)}) collective-permute-start(bf16[6,64,128]{2,1,0:T(8,128)(2,1)S(1)} %get-tuple-element.52), channel_id=1, source_target_pairs={{0,31},{1,2},{2,1},{3,4},{4,3},{5,6},{6,5},{7,8},{8,7},{9,10},{10,... | collective-permute-start | bytes 294920 | tf_op jit(solution)/shard_map/ppermute | solution.py:418
  44.2 8.2 %collective-permute-start.15 = (bf16[2,10,64,128]{3,2,1,0:T(8,128)(2,1)S(1)}, bf16[2,10,64,128]{3,2,1,0:T(8,128)(2,1)S(1)}, u32[]{:S(2)}, u32[]{:S(2)}) collective-permute-start(bf16[2,10,64,128]{3,2,1,0:T(8,128)(2,1)S(1)} %grad01_kernel.1.v3x), channel_id=1, source_target_pairs={{32,0},{64,32},{96,64},{0,96},{33,1},{65,33},{97,65},{1,97},{34,2}... | collective-permute-start | bytes 983048 | tf_op jit(solution)/shard_map/ppermute | solution.py:421
  45.3 5.6 %collective-permute-start.13 = (bf16[2,64,128]{2,1,0:T(8,128)(2,1)S(1)}, bf16[2,64,128]{2,1,0:T(8,128)(2,1)S(1)}, u32[]{:S(2)}, u32[]{:S(2)}) collective-permute-start(bf16[2,64,128]{2,1,0:T(8,128)(2,1)S(1)} %get-tuple-element.55), channel_id=1, source_target_pairs={{0,1},{1,0},{2,3},{3,2},{4,5},{5,4},{6,7},{7,6},{8,9},{9,8},{10,11... | collective-permute-start | bytes 98312 | tf_op jit(solution)/shard_map/ppermute | solution.py:415
  48.8 3.6 %collective-permute-start.14 = (bf16[2,64,128]{2,1,0:T(8,128)(2,1)S(1)}, bf16[2,64,128]{2,1,0:T(8,128)(2,1)S(1)}, u32[]{:S(2)}, u32[]{:S(2)}) collective-permute-start(bf16[2,64,128]{2,1,0:T(8,128)(2,1)S(1)} %get-tuple-element.56), channel_id=1, source_target_pairs={{0,31},{1,2},{2,1},{3,4},{4,3},{5,6},{6,5},{7,8},{8,7},{9,10},{10,... | collective-permute-start | bytes 98312 | tf_op jit(solution)/shard_map/ppermute | solution.py:418
  48.8 3.6 %copy-start.3 = (s32[1,1,64,1]{2,3,1,0:T(1,128)S(1)}, s32[1,1,64,1]{2,3,1,0:T(1,128)}, u32[]{:S(2)}) copy-start(s32[1,1,64,1]{2,3,1,0:T(1,128)} %param.13) | copy-start | bytes 772

commit v6 on v5

--- a/solution.py
+++ b/solution.py
@@ -393,7 +393,7 @@
         scratch_shapes=scratch,
         compiler_params=pltpu.CompilerParams(vmem_limit_bytes=40 << 20),
         cost_estimate=pl.CostEstimate(
-            flops=units * COLS * 27 * C * C * 2, bytes_accessed=moved, transcendentals=0
+            flops=units * COLS * 27 * C * C * 1, bytes_accessed=moved, transcendentals=0
         ),
         name=kernel.__name__,
     )(*args)

time: 71 us -> 78.4 us (1.10)
  waiting for transfers between devices: 2.2 us -> 9.16 us
    ppermute x4, waiting for transfers between devices: 1.47 us -> 7.3 us  [swap_out(): return lax.ppermute(x, 'space', outer_pairs)]
    ppermute x4, starting transfers between devices: 11.2 us -> 14.4 us  [swap_in(): return lax.ppermute(x, 'space', inner_pairs)]
    ppermute x2, waiting for transfers between devices: 0.01 us -> 1.84 us  [corner(): return lax.ppermute(x, ('tm', 'space'), route)]
    ppermute x2, starting transfers between devices: 1.9 us -> 0.08 us  [from_sooner(): return lax.ppermute(x, 'tm', sooner)]
    ppermute x2, starting transfers between devices: 6.37 us -> 5.21 us  [corner(): return lax.ppermute(x, ('tm', 'space'), route)]
  transfers between devices with their start and end apart: 16 -> 16, of which waited for: 2 -> 4; matrix products, arithmetic and copies ran while one was open for 0% -> 0% of each run, Pallas kernels for 30% -> 27%
where the time goes in v6:
time: 78.4 us; the launch traced here: 78.2 us
  starting transfers between devices  27.2 us (35%)
  Pallas kernels  24.8 us (32%)
  blocking collectives  15.7 us (20%)
  waiting for transfers between devices  9.16 us (12%)
  local copies, waits for them, and re-layouts  1.16 us (1%)
    pallas_call x17, Pallas kernels, run(): pl.pallas_call(kernel, out_shape=outs, in_specs=in_specs or [VM] * len(ar...  24.8 us
    all_to_all x1, blocking collectives, on_device(): lax.all_to_all(outgoing, 'space', split_axis=0, concat_axis=0, tiled=True)  15.7 us
    ppermute x4, starting transfers between devices, swap_in(): return lax.ppermute(x, 'space', inner_pairs)  14.4 us
    ppermute x4, waiting for transfers between devices, swap_out(): return lax.ppermute(x, 'space', outer_pairs)  7.3 us
    ppermute x4, starting transfers between devices, from_later(): return lax.ppermute(x, 'tm', later)  5.74 us
    ppermute x2, starting transfers between devices, corner(): return lax.ppermute(x, ('tm', 'space'), route)  5.21 us
    ppermute x2, waiting for transfers between devices, corner(): return lax.ppermute(x, ('tm', 'space'), route)  1.84 us
    ppermute x4, starting transfers between devices, swap_out(): return lax.ppermute(x, 'space', outer_pairs)  1.71 us
  transfers between devices with their start and end apart: 16, of which 4 were waited for; matrix products, arithmetic and copies ran while one was open for 0% of the time, Pallas kernels for 27%

profile of v6, /device:TPU:1, one launch (start us, length us, event | category | flops | bytes accessed | tf_op | source)
XLA Modules:
  0.0 78.2 jit_solution(706065147591833890)
XLA Ops:
  0.0 1.5 %start_kernel.1 = (bf16[4,8,64,128]{3,2,1,0:T(8,128)(2,1)S(1)}, bf16[3,4,2,64,128]{4,3,2,1,0:T(8,128)(2,1)S(1)}, bf16[3,4,2,64,128]{4,3,2,1,0:T(8,128)(2,1)S(1)}...) custom-call(bf16[4,8,64,128]{3,2,1,0:T(8,128)(2,1)} %cot.1, ...), custom_call_target="tpu_custom_call" | custom-call | flops 28311552 | bytes 1572896 | tf_op jit(solution)/shard_map/start_kernel/pallas_call | solution.py:388
  1.5 1.5 %collective-permute-start.3 = (bf16[3,4,2,64,128]{4,3,2,1,0:T(8,128)(2,1)S(1)}, bf16[3,4,2,64,128]{4,3,2,1,0:T(8,128)(2,1)S(1)}, u32[]{:S(2)}, u32[]{:S(2)}) collective-permute-start(bf16[3,4,2,64,128]{4,3,2,1,0:T(8,128)(2,1)S(1)} %get-tuple-element.36), channel_id=1, source_target_pairs={{0,1},{1,0},{2,3},{3,2},{4,5},{5,4},{6,7},{7,6},{8,9},{9,8},{10,11... | collective-permute-start | bytes 1179656 | tf_op jit(solution)/shard_map/ppermute | solution.py:415
  3.0 1.7 %collective-permute-start.4 = (bf16[3,4,2,64,128]{4,3,2,1,0:T(8,128)(2,1)S(1)}, bf16[3,4,2,64,128]{4,3,2,1,0:T(8,128)(2,1)S(1)}, u32[]{:S(2)}, u32[]{:S(2)}) collective-permute-start(bf16[3,4,2,64,128]{4,3,2,1,0:T(8,128)(2,1)S(1)} %get-tuple-element.37), channel_id=1, source_target_pairs={{0,31},{1,2},{2,1},{3,4},{4,3},{5,6},{6,5},{7,8},{8,7},{9,10},{10,... | collective-permute-start | bytes 1179656 | tf_op jit(solution)/shard_map/ppermute | solution.py:418
  4.7 0.0 collective-permute-done.3.rin.r0in
  4.7 5.5 %collective-permute-done.4.rout.r0out = bf16[3,4,2,64,128]{4,3,2,1,0:T(8,128)(2,1)S(1)} collective-permute-done((bf16[3,4,2,64,128]{4,3,2,1,0:T(8,128)(2,1)S(1)}, bf16[3,4,2,64,128]{4,3,2,1,0:T(8,128)(2,1)S(1)}, u32[]{:S(2)}, u32[]{:S(2)}) %collective-permute-start.4) | collective-permute-done | bytes 393248 | tf_op jit(solution)/shard_map/ppermute | solution.py:418
  10.3 2.9 %collective-permute-start.5 = (bf16[2,10,64,128]{3,2,1,0:T(8,128)(2,1)S(1)}, bf16[2,10,64,128]{3,2,1,0:T(8,128)(2,1)S(1)}, u32[]{:S(2)}, u32[]{:S(2)}) collective-permute-start(bf16[2,10,64,128]{3,2,1,0:T(8,128)(2,1)S(1)} %extend_kernel.1), channel_id=1, source_target_pairs={{32,0},{64,32},{96,64},{0,96},{33,1},{65,33},{97,65},{1,97},{34,2}... | collective-permute-start | bytes 983048 | tf_op jit(solution)/shard_map/ppermute | solution.py:421
  13.2 0.0 collective-permute-start
  13.2 5.2 %collective-permute-start.1 = (bf16[2,2,64,128]{3,2,1,0:T(8,128)(2,1)S(1)}, bf16[2,2,64,128]{3,2,1,0:T(8,128)(2,1)S(1)}, u32[]{:S(2)}, u32[]{:S(2)}) collective-permute-start(bf16[2,2,64,128]{3,2,1,0:T(8,128)(2,1)S(1)} %get-tuple-element.32), channel_id=1, source_target_pairs={{0,33},{1,32},{2,35},{3,34},{4,37},{5,36},{6,39},{7,38},{8,41},{9,... | collective-permute-start | bytes 196616 | tf_op jit(solution)/shard_map/ppermute | solution.py:425
  18.4 0.0 collective-permute-start.2
  18.4 1.6 %fetch_kernel.1 = (bf16[4,8,64,128]{3,2,1,0:T(8,128)(2,1)S(1)}, bf16[1,3,3,3,128,128]{5,4,3,2,1,0:T(8,128)(2,1)S(1)}, bf16[1,3,3,3,128,128]{5,4,3,2,1,0:T(8,128)(2,1)S(1)}) custom-call(bf16[4,8,64,128]{3,2,1,0:T(8,128)(2,1)S(1)} %get-tuple-element.34.after.v0, bf16[2,4,8,64,128]{4,3,2,1,0:T(8,128)(2,1)} %bi.9, bf16[2,3,3,3,128,128]{5,4,3,2,1,0:T(8,128)(2,1)} %w2.9, ...), custom_call_target="tpu_custom_call" | custom-call | flops 28311552 | bytes 5111808 | tf_op jit(solution)/shard_map/fetch_kernel/pallas_call | solution.py:388
  20.0 0.0 copy-start
  20.0 4.6 %early_kernel.1 = (f32[2,10,64,128]{3,2,1,0:T(8,128)S(1)}, f32[2,8,64,128]{3,2,1,0:T(8,128)S(1)}, f32[2,8,64,128]{3,2,1,0:T(8,128)S(1)}, f32[2,10,64,128]{3,2,1,0:T(8,128)S(1)}) custom-call(bf16[4,8,64,128]{3,2,1,0:T(8,128)(2,1)S(1)} %get-tuple-element.34.after.v0, bf16[4,8,64,128]{3,2,1,0:T(8,128)(2,1)S(1)} %get-tuple-element.35.bi1, ...), custom_call_target="tpu_custom_call" | custom-call | flops 1528823808 | bytes 3604480 | tf_op jit(solution)/shard_map/early_kernel/pallas_call | solution.py:388
  24.7 1.8 %collective-permute-done.1.dpi = bf16[2,2,64,128]{3,2,1,0:T(8,128)(2,1)S(1)} collective-permute-done((bf16[2,2,64,128]{3,2,1,0:T(8,128)(2,1)S(1)}, bf16[2,2,64,128]{3,2,1,0:T(8,128)(2,1)S(1)}, u32[]{:S(2)}, u32[]{:S(2)}) %collective-permute-start.1) | collective-permute-done | bytes 65568 | tf_op jit(solution)/shard_map/ppermute | solution.py:425
  26.5 0.0 copy-start.1
  26.5 1.1 %pre01_kernel.1.v1x = bf16[2,10,64,128]{3,2,1,0:T(8,128)(2,1)S(1)} custom-call(bf16[2,8,64,128]{3,2,1,0:T(8,128)(2,1)S(1)} %collective-permute-done.bx, bf16[2,2,64,128]{3,2,1,0:T(8,128)(2,1)S(1)} %collective-permute-done.1.dpi, bf16[2,2,64,128]{3,2,1,0:T(8,128)(2,1)S(1)} %collective-permute-done.2.dpo, f32[2,10,64,128]{3,2,1,0:T(8,128)S(1)} %get-tuple-element.40.ga, ...), custom_call_target="tpu_custom_call" | custom-call | flops 283115520 | bytes 3473408 | tf_op jit(solution)/shard_map/pre01_kernel/pallas_call | solution.py:388
  27.6 0.0 copy-start.2
  27.6 0.0 collective-permute-done.5.vx
  27.6 0.3 copy-done.1
  28.0 0.9 %pre23_kernel.1 = (bf16[2,8,64,128]{3,2,1,0:T(8,128)(2,1)S(1)}, bf16[6,64,128]{2,1,0:T(8,128)(2,1)S(1)}, bf16[6,64,128]{2,1,0:T(8,128)(2,1)S(1)}) custom-call(f32[2,8,64,128]{3,2,1,0:T(8,128)S(1)} %get-tuple-element.42.ga23, bf16[2,10,64,128]{3,2,1,0:T(8,128)(2,1)S(1)} %collective-permute-done.5.vx, f32[2,8,64,128]{3,2,1,0:T(8,128)S(1)} %get-tuple-element.43.d, ...), custom_call_target="tpu_custom_call" | custom-call | flops 226492416 | bytes 3473408 | tf_op jit(solution)/shard_map/pre23_kernel/pallas_call | solution.py:388
  28.8 0.1 copy-done.2
  29.0 0.1 collective-permute-start.9
  29.1 2.7 %collective-permute-start.8 = (bf16[2,10,64,128]{3,2,1,0:T(8,128)(2,1)S(1)}, bf16[2,10,64,128]{3,2,1,0:T(8,128)(2,1)S(1)}, u32[]{:S(2)}, u32[]{:S(2)}) collective-permute-start(bf16[2,10,64,128]{3,2,1,0:T(8,128)(2,1)S(1)} %pre01_kernel.1.v1x), channel_id=1, source_target_pairs={{32,0},{64,32},{96,64},{0,96},{33,1},{65,33},{97,65},{1,97},{34,2}... | collective-permute-start | bytes 983048 | tf_op jit(solution)/shard_map/ppermute | solution.py:421
  31.7 6.4 %collective-permute-start.6 = (bf16[6,64,128]{2,1,0:T(8,128)(2,1)S(1)}, bf16[6,64,128]{2,1,0:T(8,128)(2,1)S(1)}, u32[]{:S(2)}, u32[]{:S(2)}) collective-permute-start(bf16[6,64,128]{2,1,0:T(8,128)(2,1)S(1)} %get-tuple-element.46), channel_id=1, source_target_pairs={{0,1},{1,0},{2,3},{3,2},{4,5},{5,4},{6,7},{7,6},{8,9},{9,8},{10,11... | collective-permute-start | bytes 294920 | tf_op jit(solution)/shard_map/ppermute | solution.py:415
  38.2 0.0 collective-permute-start.7
  38.2 2.5 %inner_up_kernel.1 = (f32[2,10,64,128]{3,2,1,0:T(8,128)S(1)}, f32[2,8,64,128]{3,2,1,0:T(8,128)S(1)}) custom-call(bf16[2,10,64,128]{3,2,1,0:T(8,128)(2,1)S(1)} %pre01_kernel.1.v1x, bf16[2,8,64,128]{3,2,1,0:T(8,128)(2,1)S(1)} %get-tuple-element.44.v1.after, bf16[4,8,64,128]{3,2,1,0:T(8,128)(2,1)S(1)} %get-tuple-element.34.after.v0, ...), custom_call_target="tpu_custom_call" | custom-call | flops 792723456 | bytes 3670016 | tf_op jit(solution)/shard_map/inner_up_kernel/pallas_call | solution.py:388
  40.6 1.5 %factor23_kernel.1.after.d = f32[2,8,64,128]{3,2,1,0:T(8,128)S(1)} custom-call(bf16[2,4,8,64,128]{4,3,2,1,0:T(8,128)(2,1)S(1)} %copy-done.2, bf16[3,4,2,64,128]{4,3,2,1,0:T(8,128)(2,1)S(1)} %collective-permute-done.3.rin.r0in, bf16[3,4,2,64,128]{4,3,2,1,0:T(8,128)(2,1)S(1)} %collective-permute-done.4.rout.r0out, ...), custom_call_target="tpu_custom_call" | custom-call | flops 452984832 | bytes 4128768 | tf_op jit(solution)/shard_map/factor23_kernel/pallas_call | solution.py:388
  42.2 0.0 collective-permute-done.6.rin
  42.2 0.3 collective-permute-done.7.rout
  42.5 0.6 up01_kernel.1.v2x
  43.1 0.1 collective-permute-start.12
  43.2 0.0 collective-permute-done.8.vxr
  43.2 1.0 %up23_kernel.1 = (bf16[2,8,64,128]{3,2,1,0:T(8,128)(2,1)S(1)}, bf16[6,64,128]{2,1,0:T(8,128)(2,1)S(1)}, bf16[6,64,128]{2,1,0:T(8,128)(2,1)S(1)}) custom-call(f32[2,8,64,128]{3,2,1,0:T(8,128)S(1)} %get-tuple-element.48.after.base23, bf16[6,64,128]{2,1,0:T(8,128)(2,1)S(1)} %collective-permute-done.6.rin, bf16[6,64,128]{2,1,0:T(8,128)(2,1)S(1)} %collective-permute-done.7.rout, ...), custom_call_target="tpu_custom_call" | custom-call | flops 283115520 | bytes 3145728 | tf_op jit(solution)/shard_map/up23_kernel/pallas_call | solution.py:388
  44.2 3.1 %collective-permute-start.10 = (bf16[6,64,128]{2,1,0:T(8,128)(2,1)S(1)}, bf16[6,64,128]{2,1,0:T(8,128)(2,1)S(1)}, u32[]{:S(2)}, u32[]{:S(2)}) collective-permute-start(bf16[6,64,128]{2,1,0:T(8,128)(2,1)S(1)} %get-tuple-element.51), channel_id=1, source_target_pairs={{0,1},{1,0},{2,3},{3,2},{4,5},{5,4},{6,7},{7,6},{8,9},{9,8},{10,11... | collective-permute-start | bytes 294920 | tf_op jit(solution)/shard_map/ppermute | solution.py:415
  47.3 0.0 collective-permute-start.11
  47.3 0.0 collective-permute-done.9.bx
  47.3 1.8 %factor01_kernel.1.after.d = f32[2,10,64,128]{3,2,1,0:T(8,128)S(1)} custom-call(bf16[2,4,8,64,128]{4,3,2,1,0:T(8,128)(2,1)S(1)} %copy-done.2, bf16[3,4,2,64,128]{4,3,2,1,0:T(8,128)(2,1)S(1)} %collective-permute-done.3.rin.r0in, bf16[3,4,2,64,128]{4,3,2,1,0:T(8,128)(2,1)S(1)} %collective-permute-done.4.rout.r0out, ...), custom_call_target="tpu_custom_call" | custom-call | flops 566231040 | bytes 4259840 | tf_op jit(solution)/shard_map/factor01_kernel/pallas_call | solution.py:388
  49.2 2.5 %inner_grad_kernel.1 = (f32[2,10,64,128]{3,2,1,0:T(8,128)S(1)}, f32[2,8,64,128]{3,2,1,0:T(8,128)S(1)}) custom-call(bf16[2,10,64,128]{3,2,1,0:T(8,128)(2,1)S(1)} %up01_kernel.1.v2x, bf16[2,8,64,128]{3,2,1,0:T(8,128)(2,1)S(1)} %get-tuple-element.49.after.v2, f32[2,10,64,128]{3,2,1,0:T(8,128)S(1)} %factor01_kernel.1.after.d, ...), custom_call_target="tpu_custom_call" | custom-call | flops 792723456 | bytes 3014656 | tf_op jit(solution)/shard_map/inner_grad_kernel/pallas_call | solution.py:388
  51.7 0.0 collective-permute-done.11.rout
  51.7 0.6 grad01_kernel.1.v3x
  52.3 0.1 collective-permute-start.15
  52.4 1.0 %grad23_kernel.1 = (bf16[2,8,64,128]{3,2,1,0:T(8,128)(2,1)S(1)}, bf16[2,64,128]{2,1,0:T(8,128)(2,1)S(1)}, bf16[2,64,128]{2,1,0:T(8,128)(2,1)S(1)}) custom-call(f32[2,8,64,128]{3,2,1,0:T(8,128)S(1)} %get-tuple-element.53.base23, bf16[6,64,128]{2,1,0:T(8,128)(2,1)S(1)} %collective-permute-done.10.rin, bf16[6,64,128]{2,1,0:T(8,128)(2,1)S(1)} %collective-permute-done.11.rout, ...), custom_call_target="tpu_custom_call" | custom-call | flops 283115520 | bytes 3342336 | tf_op jit(solution)/shard_map/grad23_kernel/pallas_call | solution.py:388
  53.4 3.4 %collective-permute-start.13 = (bf16[2,64,128]{2,1,0:T(8,128)(2,1)S(1)}, bf16[2,64,128]{2,1,0:T(8,128)(2,1)S(1)}, u32[]{:S(2)}, u32[]{:S(2)}) collective-permute-start(bf16[2,64,128]{2,1,0:T(8,128)(2,1)S(1)} %get-tuple-element.55), channel_id=1, source_target_pairs={{0,1},{1,0},{2,3},{3,2},{4,5},{5,4},{6,7},{7,6},{8,9},{9,8},{10,11... | collective-permute-start | bytes 98312 | tf_op jit(solution)/shard_map/ppermute | solution.py:415
  56.8 0.0 collective-permute-start.14
  56.8 2.1 %inner_last_kernel.1.base = f32[4,8,64,128]{3,2,1,0:T(8,128)S(1)} custom-call(bf16[2,10,64,128]{3,2,1,0:T(8,128)(2,1)S(1)} %grad01_kernel.1.v3x, bf16[2,8,64,128]{3,2,1,0:T(8,128)(2,1)S(1)} %get-tuple-element.54.v3, bf16[2,10,64,128]{3,2,1,0:T(8,128)(2,1)S(1)} %up01_kernel.1.v2x, bf16[2,8,64,128]{3,2,1,0:T(8,128)(2,1)S(1)} %get-tuple-element.49.after.v2, ...), custom_call_target="tpu_custom_call" | custom-call | flops 679477248 | bytes 2949120 | tf_op jit(solution)/shard_map/inner_last_kernel/pallas_call | solution.py:388
  58.9 1.5 %collective-permute-done.14.rout = bf16[2,64,128]{2,1,0:T(8,128)(2,1)S(1)} collective-permute-done((bf16[2,64,128]{2,1,0:T(8,128)(2,1)S(1)}, bf16[2,64,128]{2,1,0:T(8,128)(2,1)S(1)}, u32[]{:S(2)}, u32[]{:S(2)}) %collective-permute-start.14) | collective-permute-done | bytes 32800 | tf_op jit(solution)/shard_map/ppermute | solution.py:418
  60.4 1.4 %last_kernel.1 = bf16[32,4,1024]{2,1,0:T(4,128)(2,1)S(1)} custom-call(f32[4,8,64,128]{3,2,1,0:T(8,128)S(1)} %inner_last_kernel.1.base, bf16[2,64,128]{2,1,0:T(8,128)(2,1)S(1)} %collective-permute-done.13.rin, bf16[2,64,128]{2,1,0:T(8,128)(2,1)S(1)} %collective-permute-done.14.rout, bf16[2,10,64,128]{3,2,1,0:T(8,128)(2,1)S(1)} %collective-permute-done.15.vxr, ...), custom_call_target="tpu_custom_call" | custom-call | flops 226492416 | bytes 3211520 | tf_op jit(solution)/shard_map/last_kernel/pallas_call | solution.py:388
  61.8 15.7 %all_to_all.5 = bf16[32,4,1024]{2,1,0:T(4,128)(2,1)S(1)} all-to-all(bf16[32,4,1024]{2,1,0:T(4,128)(2,1)S(1)} %last_kernel.1), channel_id=1, replica_groups=mesh['tm'=4,'space'=32] {'space'}, dimensions={0} | all-to-all | bytes 524288 | tf_op jit(solution)/shard_map/all_to_all | solution.py:518
  77.4 0.7 copy.9
  (11 shorter events, 0.1 us)
Async XLA Ops:
  1.5 3.2 %collective-permute-start.3 = (bf16[3,4,2,64,128]{4,3,2,1,0:T(8,128)(2,1)S(1)}, bf16[3,4,2,64,128]{4,3,2,1,0:T(8,128)(2,1)S(1)}, u32[]{:S(2)}, u32[]{:S(2)}) collective-permute-start(bf16[3,4,2,64,128]{4,3,2,1,0:T(8,128)(2,1)S(1)} %get-tuple-element.36), channel_id=1, source_target_pairs={{0,1},{1,0},{2,3},{3,2},{4,5},{5,4},{6,7},{7,6},{8,9},{9,8},{10,11... | collective-permute-start | bytes 1179656 | tf_op jit(solution)/shard_map/ppermute | solution.py:415
  3.0 7.2 %collective-permute-start.4 = (bf16[3,4,2,64,128]{4,3,2,1,0:T(8,128)(2,1)S(1)}, bf16[3,4,2,64,128]{4,3,2,1,0:T(8,128)(2,1)S(1)}, u32[]{:S(2)}, u32[]{:S(2)}) collective-permute-start(bf16[3,4,2,64,128]{4,3,2,1,0:T(8,128)(2,1)S(1)} %get-tuple-element.37), channel_id=1, source_target_pairs={{0,31},{1,2},{2,1},{3,4},{4,3},{5,6},{6,5},{7,8},{8,7},{9,10},{10,... | collective-permute-start | bytes 1179656 | tf_op jit(solution)/shard_map/ppermute | solution.py:418
  10.3 17.4 %collective-permute-start.5 = (bf16[2,10,64,128]{3,2,1,0:T(8,128)(2,1)S(1)}, bf16[2,10,64,128]{3,2,1,0:T(8,128)(2,1)S(1)}, u32[]{:S(2)}, u32[]{:S(2)}) collective-permute-start(bf16[2,10,64,128]{3,2,1,0:T(8,128)(2,1)S(1)} %extend_kernel.1), channel_id=1, source_target_pairs={{32,0},{64,32},{96,64},{0,96},{33,1},{65,33},{97,65},{1,97},{34,2}... | collective-permute-start | bytes 983048 | tf_op jit(solution)/shard_map/ppermute | solution.py:421
  13.2 13.3 %collective-permute-start = (bf16[2,8,64,128]{3,2,1,0:T(8,128)(2,1)S(1)}, bf16[2,8,64,128]{3,2,1,0:T(8,128)(2,1)S(1)}, u32[]{:S(2)}, u32[]{:S(2)}) collective-permute-start(bf16[2,8,64,128]{3,2,1,0:T(8,128)(2,1)S(1)} %get-tuple-element.31), channel_id=1, source_target_pairs={{0,32},{32,64},{64,96},{96,0},{1,33},{33,65},{65,97},{97,1},{2,34}... | collective-permute-start | bytes 786440 | tf_op jit(solution)/shard_map/ppermute | solution.py:428
  13.2 13.3 %collective-permute-start.1 = (bf16[2,2,64,128]{3,2,1,0:T(8,128)(2,1)S(1)}, bf16[2,2,64,128]{3,2,1,0:T(8,128)(2,1)S(1)}, u32[]{:S(2)}, u32[]{:S(2)}) collective-permute-start(bf16[2,2,64,128]{3,2,1,0:T(8,128)(2,1)S(1)} %get-tuple-element.32), channel_id=1, source_target_pairs={{0,33},{1,32},{2,35},{3,34},{4,37},{5,36},{6,39},{7,38},{8,41},{9,... | collective-permute-start | bytes 196616 | tf_op jit(solution)/shard_map/ppermute | solution.py:425
  18.4 8.1 %collective-permute-start.2 = (bf16[2,2,64,128]{3,2,1,0:T(8,128)(2,1)S(1)}, bf16[2,2,64,128]{3,2,1,0:T(8,128)(2,1)S(1)}, u32[]{:S(2)}, u32[]{:S(2)}) collective-permute-start(bf16[2,2,64,128]{3,2,1,0:T(8,128)(2,1)S(1)} %get-tuple-element.33), channel_id=1, source_target_pairs={{0,63},{1,34},{2,33},{3,36},{4,35},{5,38},{6,37},{7,40},{8,39},{9,... | collective-permute-start | bytes 196616 | tf_op jit(solution)/shard_map/ppermute | solution.py:425
  20.0 6.5 %copy-start = (bf16[2,3,3,3,128,128]{5,4,3,2,1,0:T(8,128)(2,1)S(1)}, bf16[2,3,3,3,128,128]{5,4,3,2,1,0:T(8,128)(2,1)}, u32[]{:S(2)}) copy-start(bf16[2,3,3,3,128,128]{5,4,3,2,1,0:T(8,128)(2,1)} %w1.17) | copy-start | bytes 5308420
  26.5 1.5 %copy-start.1 = (bf16[2,3,3,3,128,128]{5,4,3,2,1,0:T(8,128)(2,1)S(1)}, bf16[2,3,3,3,128,128]{5,4,3,2,1,0:T(8,128)(2,1)}, u32[]{:S(2)}) copy-start(bf16[2,3,3,3,128,128]{5,4,3,2,1,0:T(8,128)(2,1)} %w2.9) | copy-start | bytes 5308420
  27.6 1.3 %copy-start.2 = (bf16[2,4,8,64,128]{4,3,2,1,0:T(8,128)(2,1)S(1)}, bf16[2,4,8,64,128]{4,3,2,1,0:T(8,128)(2,1)}, u32[]{:S(2)}) copy-start(bf16[2,4,8,64,128]{4,3,2,1,0:T(8,128)(2,1)} %bi.9) | copy-start | bytes 3145732
  29.0 18.4 %collective-permute-start.9 = (bf16[2,12,64,128]{3,2,1,0:T(8,128)(2,1)S(1)}, bf16[2,12,64,128]{3,2,1,0:T(8,128)(2,1)S(1)}, u32[]{:S(2)}, u32[]{:S(2)}) collective-permute-start(bf16[2,12,64,128]{3,2,1,0:T(8,128)(2,1)S(1)} %extend0_kernel.1), channel_id=1, source_target_pairs={{0,32},{32,64},{64,96},{96,0},{1,33},{33,65},{65,97},{97,1},{2,34}... | collective-permute-start | bytes 1179656 | tf_op jit(solution)/shard_map/ppermute | solution.py:428
  29.1 14.1 %collective-permute-start.8 = (bf16[2,10,64,128]{3,2,1,0:T(8,128)(2,1)S(1)}, bf16[2,10,64,128]{3,2,1,0:T(8,128)(2,1)S(1)}, u32[]{:S(2)}, u32[]{:S(2)}) collective-permute-start(bf16[2,10,64,128]{3,2,1,0:T(8,128)(2,1)S(1)} %pre01_kernel.1.v1x), channel_id=1, source_target_pairs={{32,0},{64,32},{96,64},{0,96},{33,1},{65,33},{97,65},{1,97},{34,2}... | collective-permute-start | bytes 983048 | tf_op jit(solution)/shard_map/ppermute | solution.py:421
  31.7 10.4 %collective-permute-start.6 = (bf16[6,64,128]{2,1,0:T(8,128)(2,1)S(1)}, bf16[6,64,128]{2,1,0:T(8,128)(2,1)S(1)}, u32[]{:S(2)}, u32[]{:S(2)}) collective-permute-start(bf16[6,64,128]{2,1,0:T(8,128)(2,1)S(1)} %get-tuple-element.46), channel_id=1, source_target_pairs={{0,1},{1,0},{2,3},{3,2},{4,5},{5,4},{6,7},{7,6},{8,9},{9,8},{10,11... | collective-permute-start | bytes 294920 | tf_op jit(solution)/shard_map/ppermute | solution.py:415
  38.2 4.3 %collective-permute-start.7 = (bf16[6,64,128]{2,1,0:T(8,128)(2,1)S(1)}, bf16[6,64,128]{2,1,0:T(8,128)(2,1)S(1)}, u32[]{:S(2)}, u32[]{:S(2)}) collective-permute-start(bf16[6,64,128]{2,1,0:T(8,128)(2,1)S(1)} %get-tuple-element.47), channel_id=1, source_target_pairs={{0,31},{1,2},{2,1},{3,4},{4,3},{5,6},{6,5},{7,8},{8,7},{9,10},{10,... | collective-permute-start | bytes 294920 | tf_op jit(solution)/shard_map/ppermute | solution.py:418
  43.1 9.3 %collective-permute-start.12 = (bf16[2,10,64,128]{3,2,1,0:T(8,128)(2,1)S(1)}, bf16[2,10,64,128]{3,2,1,0:T(8,128)(2,1)S(1)}, u32[]{:S(2)}, u32[]{:S(2)}) collective-permute-start(bf16[2,10,64,128]{3,2,1,0:T(8,128)(2,1)S(1)} %up01_kernel.1.v2x), channel_id=1, source_target_pairs={{32,0},{64,32},{96,64},{0,96},{33,1},{65,33},{97,65},{1,97},{34,2}... | collective-permute-start | bytes 983048 | tf_op jit(solution)/shard_map/ppermute | solution.py:421
  44.2 7.4 %collective-permute-start.10 = (bf16[6,64,128]{2,1,0:T(8,128)(2,1)S(1)}, bf16[6,64,128]{2,1,0:T(8,128)(2,1)S(1)}, u32[]{:S(2)}, u32[]{:S(2)}) collective-permute-start(bf16[6,64,128]{2,1,0:T(8,128)(2,1)S(1)} %get-tuple-element.51), channel_id=1, source_target_pairs={{0,1},{1,0},{2,3},{3,2},{4,5},{5,4},{6,7},{7,6},{8,9},{9,8},{10,11... | collective-permute-start | bytes 294920 | tf_op jit(solution)/shard_map/ppermute | solution.py:415
  47.3 4.3 %collective-permute-start.11 = (bf16[6,64,128]{2,1,0:T(8,128)(2,1)S(1)}, bf16[6,64,128]{2,1,0:T(8,128)(2,1)S(1)}, u32[]{:S(2)}, u32[]{:S(2)}) collective-permute-start(bf16[6,64,128]{2,1,0:T(8,128)(2,1)S(1)} %get-tuple-element.52), channel_id=1, source_target_pairs={{0,31},{1,2},{2,1},{3,4},{4,3},{5,6},{6,5},{7,8},{8,7},{9,10},{10,... | collective-permute-start | bytes 294920 | tf_op jit(solution)/shard_map/ppermute | solution.py:418
  52.3 8.1 %collective-permute-start.15 = (bf16[2,10,64,128]{3,2,1,0:T(8,128)(2,1)S(1)}, bf16[2,10,64,128]{3,2,1,0:T(8,128)(2,1)S(1)}, u32[]{:S(2)}, u32[]{:S(2)}) collective-permute-start(bf16[2,10,64,128]{3,2,1,0:T(8,128)(2,1)S(1)} %grad01_kernel.1.v3x), channel_id=1, source_target_pairs={{32,0},{64,32},{96,64},{0,96},{33,1},{65,33},{97,65},{1,97},{34,2}... | collective-permute-start | bytes 983048 | tf_op jit(solution)/shard_map/ppermute | solution.py:421
  53.4 5.5 %collective-permute-start.13 = (bf16[2,64,128]{2,1,0:T(8,128)(2,1)S(1)}, bf16[2,64,128]{2,1,0:T(8,128)(2,1)S(1)}, u32[]{:S(2)}, u32[]{:S(2)}) collective-permute-start(bf16[2,64,128]{2,1,0:T(8,128)(2,1)S(1)} %get-tuple-element.55), channel_id=1, source_target_pairs={{0,1},{1,0},{2,3},{3,2},{4,5},{5,4},{6,7},{7,6},{8,9},{9,8},{10,11... | collective-permute-start | bytes 98312 | tf_op jit(solution)/shard_map/ppermute | solution.py:415
  56.8 3.6 %collective-permute-start.14 = (bf16[2,64,128]{2,1,0:T(8,128)(2,1)S(1)}, bf16[2,64,128]{2,1,0:T(8,128)(2,1)S(1)}, u32[]{:S(2)}, u32[]{:S(2)}) collective-permute-start(bf16[2,64,128]{2,1,0:T(8,128)(2,1)S(1)} %get-tuple-element.56), channel_id=1, source_target_pairs={{0,31},{1,2},{2,1},{3,4},{4,3},{5,6},{6,5},{7,8},{8,7},{9,10},{10,... | collective-permute-start | bytes 98312 | tf_op jit(solution)/shard_map/ppermute | solution.py:418
  56.8 3.6 %copy-start.3 = (s32[1,1,64,1]{2,3,1,0:T(1,128)S(1)}, s32[1,1,64,1]{2,3,1,0:T(1,128)}, u32[]{:S(2)}) copy-start(s32[1,1,64,1]{2,3,1,0:T(1,128)} %param.13) | copy-start | bytes 772
